TPU v7x, 32 devices: a whole 2x2x4 slice. The times are simulated.
32 devices in a mesh: ep: 4 (over y, x), dp: 4 (over z), fs: 2 (over core).
Axes of the slice: x: 2, y: 2, z: 4, core: 2. Of those that a mesh axis runs over, the one named last changes fastest.
Arguments:
- tokens: bfloat16 [16, 1024, 768], P(('dp', 'fs'), 'ep'), may hold values from -6 to 6
- prev_logits: float32 [16, 1024, 6], P(('dp', 'fs'), 'ep'), may hold values from -3 to 3
- segments: int32 [16, 1024], P(('dp', 'fs')), may hold values from 0 to 3, never falling along the last dimension, each value on 1 to 512 neighbouring positions
- routes: int32 [16, 1024, 2], P(('dp', 'fs'), 'ep'), may hold values from 0 to 5, all different within a row; in each aligned block of 256 rows (0 to 255, 256 to 511, ..., all dimensions but the last counted through in order) at most 128 rows name the same one
- cotangent: bfloat16 [16, 1024, 768], P(('dp', 'fs'), 'ep'), may hold values from -6 to 6
- gain_attn: bfloat16 [768], P('fs'), may hold values from 0.5 to 1.5
- w_qkv: bfloat16 [768, 2304], P('fs'), may hold values from -0.21875 to 0.21875
- w_out: bfloat16 [768, 768], P('fs'), may hold values from -0.625 to 0.625
- gain_moe: bfloat16 [768], P('fs'), may hold values from 0.5 to 1.5
- w_router: bfloat16 [768, 6], P('fs'), may hold values from -0.15625 to 0.15625
- const_proj: bfloat16 [768, 4], P('fs'), may hold values from -0.21875 to 0.21875
- const_vec: bfloat16 [768, 2], P('fs'), may hold values from -24 to 24
- w_gate: bfloat16 [4, 768, 1024], P('ep', 'fs'), may hold values from -0.21875 to 0.21875
- w_up: bfloat16 [4, 768, 1024], P('ep', 'fs'), may hold values from -0.21875 to 0.21875
- w_down: bfloat16 [4, 1024, 768], P('ep', 'fs'), may hold values from -0.75 to 0.75
Outputs:
- block_out: bfloat16 [16, 1024, 768], P(('dp', 'fs'), 'ep')
- grad_tokens: float32 [16, 1024, 768], P(('dp', 'fs'), 'ep')
- grad_prev: float32 [16, 1024, 6], P(('dp', 'fs'), 'ep')
- grad_gain_attn: float32 [768], P(('ep', 'dp', 'fs'))
- grad_w_qkv: float32 [768, 2304], P(('ep', 'dp', 'fs'))
- grad_w_out: float32 [768, 768], P(('ep', 'dp', 'fs'))
- grad_gain_moe: float32 [768], P(('ep', 'dp', 'fs'))
- grad_w_router: float32 [768, 6], P(('ep', 'dp', 'fs'))
- grad_const_proj: float32 [768, 4], P(('ep', 'dp', 'fs'))
- grad_const_vec: float32 [768, 2], P(('ep', 'dp', 'fs'))
- grad_w_gate: float32 [4, 768, 1024], P('ep', ('dp', 'fs'))
- grad_w_up: float32 [4, 768, 1024], P('ep', ('dp', 'fs'))
- grad_w_down: float32 [4, 1024, 768], P('ep', ('dp', 'fs'))
Inputs may be any that keep to these rules, and one draw needn't show every extreme that they name: `routes`: each token names two different route numbers. In each aligned block of 256 tokens of a sequence, no route number is named more than 128 times, a bound that some block reaches. `segments`: along a sequence segment numbers never fall; each of the 4 numbers occurs, no segment is longer than half of 1024 tokens, and one is exactly that long.
All inputs are finite; a program needn't handle non-finite values.
Results may differ from a plain program's by a relative error of at most 0.015.
Values may be sent and summed in bfloat16 or wider, within the bound.
A program may use at most 256 MiB of HBM per device.

v0:
```python
import functools

import jax
import jax.numpy as jnp
from jax import lax
from jax.experimental import pallas as pl
from jax.experimental.pallas import tpu as pltpu
from jax.sharding import PartitionSpec as P

HEAD = 64
SEGS = 4


NORM_EPS = 1e-06
MASK_FILL = -1e30
HIGHEST = lax.Precision.HIGHEST


def rms_scale(values, gains):
    inverse = lax.rsqrt(jnp.mean(values * values, axis=-1, keepdims=True) + NORM_EPS)
    return values * inverse * gains


def small_softmax(logit_rows):
    largest = jnp.max(logit_rows, axis=-1, keepdims=True)
    powers = jnp.exp(logit_rows - largest)
    return powers / jnp.sum(powers, axis=-1, keepdims=True)


def add_tuple(first_tuple, second_tuple):
    if first_tuple is None:
        return second_tuple
    return tuple(
        (first_term + second_term for first_term, second_term in zip(first_tuple, second_tuple))
    )


def shards(
    tokens,
    prev_logits,
    segments,
    routes,
    cotangent,
    gain_attn,
    w_qkv,
    w_out,
    gain_moe,
    w_router,
    const_proj,
    const_vec,
    w_gate,
    w_up,
    w_down,
):
    micro_count, row_count, model_width = tokens.shape
    head_count = model_width // HEAD
    peer_count = lax.axis_size("ep")
    my_index = lax.axis_index("ep")
    route_count = w_router.shape[1]
    expert_count = route_count - 4
    half_count = peer_count // expert_count
    capacity = (3 * row_count // route_count + 7) // 8 * 8
    seq_length = row_count * peer_count
    slot_count = expert_count * capacity
    pos_all = jnp.arange(seq_length, dtype=jnp.int32)
    pos_mine = my_index * row_count + jnp.arange(row_count, dtype=jnp.int32)
    expert_ids = jnp.arange(expert_count, dtype=jnp.int32)
    slot_ids = jnp.arange(slot_count, dtype=jnp.int32)
    route_ids = jnp.arange(route_count, dtype=jnp.int32)
    layer_outputs = []
    input_grads = []
    prev_grads = []
    dense_acc = None
    expert_acc = None
    for step_index in range(micro_count):
        gathered = (
            lax.all_gather(w_qkv, "fs", axis=0, tiled=True),
            lax.all_gather(w_out, "fs", axis=0, tiled=True),
            lax.all_gather(w_router, "fs", axis=0, tiled=True),
            lax.all_gather(const_proj, "fs", axis=0, tiled=True),
            lax.all_gather(const_vec, "fs", axis=0, tiled=True),
            lax.all_gather(gain_attn, "fs", axis=0, tiled=True),
            lax.all_gather(gain_moe, "fs", axis=0, tiled=True),
            lax.all_gather(w_gate, "fs", axis=1, tiled=True),
            lax.all_gather(w_up, "fs", axis=1, tiled=True),
            lax.all_gather(w_down, "fs", axis=1, tiled=True),
        )
        (
            qkv_weight,
            out_weight,
            router_weight,
            cproj_weight,
            cvec_weight,
            attn_gain,
            moe_gain,
            gate_weight,
            up_weight,
            down_weight,
        ) = gathered
        gate_weight = gate_weight[0]
        up_weight = up_weight[0]
        down_weight = down_weight[0]
        attn_gain = attn_gain.astype(jnp.float32)
        moe_gain = moe_gain.astype(jnp.float32)
        router_float = router_weight.astype(jnp.float32)
        cproj_float = cproj_weight.astype(jnp.float32)
        cvec_float = cvec_weight.astype(jnp.float32)
        token_rows = tokens[step_index].astype(jnp.float32)
        seg_all = segments[step_index]
        seg_mine = lax.dynamic_slice_in_dim(seg_all, my_index * row_count, row_count)
        allowed = (seg_mine[:, None] == seg_all[None, :]) & (pos_all[None, :] <= pos_mine[:, None])
        valid_rows = (seg_mine != SEGS - 1).astype(jnp.float32)[:, None]
        normed = rms_scale(token_rows, attn_gain).astype(jnp.bfloat16)
        qkv_rows = jnp.dot(normed, qkv_weight, preferred_element_type=jnp.float32).astype(
            jnp.bfloat16
        )
        queries = qkv_rows[:, :model_width].reshape(row_count, head_count, HEAD)
        keys_local = qkv_rows[:, model_width : 2 * model_width]
        values_local = qkv_rows[:, 2 * model_width :]
        keys_all, values_all = (
            lax.all_gather(keys_local, "ep", axis=0, tiled=True),
            lax.all_gather(values_local, "ep", axis=0, tiled=True),
        )
        key_heads = keys_all.reshape(seq_length, head_count, HEAD)
        value_heads = values_all.reshape(seq_length, head_count, HEAD)
        scores = (
            jnp.einsum("qhd,khd->hqk", queries, key_heads, preferred_element_type=jnp.float32)
            * 0.125
        )
        scores = jnp.where(allowed[None], scores, MASK_FILL)
        largest = jnp.max(scores, axis=-1, keepdims=True)
        powers = jnp.exp(scores - largest)
        row_total = jnp.sum(powers, axis=-1, keepdims=True)
        log_total = largest + jnp.log(row_total)
        attn_probs = powers / row_total
        attended = jnp.einsum(
            "hqk,khd->qhd",
            attn_probs.astype(jnp.bfloat16),
            value_heads,
            preferred_element_type=jnp.float32,
        ).reshape(row_count, model_width)
        attended = (attended * valid_rows).astype(jnp.bfloat16)
        residual = token_rows + jnp.dot(attended, out_weight, preferred_element_type=jnp.float32)
        mixed = rms_scale(residual, moe_gain).astype(jnp.bfloat16)
        mixed_float = mixed.astype(jnp.float32)
        logits = (
            jnp.dot(mixed, router_weight, preferred_element_type=jnp.float32)
            + prev_logits[step_index]
        )
        router_probs = small_softmax(logits)
        route_rows = routes[step_index]
        choose = (route_rows[:, :, None] == route_ids[None, None, :]).astype(jnp.float32)
        gate_values = jnp.sum(choose * router_probs[:, None, :], axis=-1)
        const_logits = jnp.dot(mixed, cproj_weight, preferred_element_type=jnp.float32)
        mixings = []
        const_outs = []
        for const_index in range(2):
            mixing = small_softmax(const_logits[:, 2 * const_index : 2 * const_index + 2])
            mixings.append(mixing)
            const_outs.append(
                mixing[:, :1] * mixed_float + mixing[:, 1:] * cvec_float[:, const_index][None, :]
            )
        pair_route = route_rows.reshape(-1)
        expert_hit = (pair_route[:, None] == expert_ids[None, :]).astype(jnp.int32)
        slot_index = jnp.sum((jnp.cumsum(expert_hit, axis=0) - expert_hit) * expert_hit, axis=1)
        slot_cell = jnp.sum(expert_hit * expert_ids[None, :], axis=1) * capacity + slot_index
        slot_place = jnp.where(jnp.sum(expert_hit, axis=1) > 0, slot_cell, -1)
        slot_table = (slot_ids[:, None] == slot_place[None, :]).astype(jnp.bfloat16)
        pair_rows = jnp.repeat(mixed, 2, axis=0)
        packed = jnp.einsum(
            "sp,pd->sd", slot_table, pair_rows, preferred_element_type=jnp.float32
        ).astype(jnp.bfloat16)
        outgoing = jnp.broadcast_to(
            packed.reshape(expert_count, 1, capacity, model_width),
            (expert_count, half_count, capacity, model_width),
        ).reshape(peer_count, capacity, model_width)
        received = lax.all_to_all(outgoing, "ep", split_axis=0, concat_axis=0, tiled=True)
        flat_rows = received.reshape(-1, model_width)
        gate_part = jnp.dot(flat_rows, gate_weight, preferred_element_type=jnp.float32)
        up_part = jnp.dot(flat_rows, up_weight, preferred_element_type=jnp.float32)
        hidden = (jax.nn.silu(gate_part) * up_part).astype(jnp.bfloat16)
        part_out = (
            jnp.dot(hidden, down_weight, preferred_element_type=jnp.float32)
            .astype(jnp.bfloat16)
            .reshape(received.shape)
        )
        returned_rows = lax.all_to_all(part_out, "ep", split_axis=0, concat_axis=0, tiled=True)
        returned_rows, kept_rows = (returned_rows, received)
        halves = returned_rows.reshape(expert_count, half_count, capacity, model_width)
        pair_ffn = jnp.zeros((2 * row_count, model_width), jnp.float32)
        for half_index in range(half_count):
            pair_ffn = pair_ffn + jnp.einsum(
                "sp,sd->pd",
                slot_table,
                halves[:, half_index].reshape(slot_count, model_width),
                preferred_element_type=jnp.float32,
            )
        expert_out = pair_ffn.reshape(row_count, 2, model_width)
        expert_out = (
            expert_out + choose[:, :, expert_count + 1 : expert_count + 2] * mixed_float[:, None, :]
        )
        for const_index in range(2):
            column = expert_count + 2 + const_index
            expert_out = (
                expert_out + choose[:, :, column : column + 1] * const_outs[const_index][:, None, :]
            )
        result_rows = residual + jnp.sum(gate_values[:, :, None] * expert_out, axis=1)
        layer_outputs.append(result_rows.astype(jnp.bfloat16))
        grad_rows = cotangent[step_index].astype(jnp.float32)
        d_gates = jnp.sum(expert_out * grad_rows[:, None, :], axis=-1)
        d_probs = jnp.sum(choose * d_gates[:, :, None], axis=1)
        d_logits = router_probs * (
            d_probs - jnp.sum(router_probs * d_probs, axis=-1, keepdims=True)
        )
        prev_grads.append(d_logits)
        grad_router = jnp.dot(mixed_float.T, d_logits, precision=HIGHEST)
        d_mixed = jnp.dot(d_logits, router_float.T, precision=HIGHEST)
        weighted = gate_values[:, :, None] * grad_rows[:, None, :]
        d_mixed = d_mixed + jnp.sum(
            choose[:, :, expert_count + 1 : expert_count + 2] * weighted, axis=1
        )
        cproj_grads = []
        cvec_grads = []
        for const_index in range(2):
            column = expert_count + 2 + const_index
            mixing = mixings[const_index]
            d_const = jnp.sum(choose[:, :, column : column + 1] * weighted, axis=1)
            d_mix = jnp.stack(
                [
                    jnp.sum(d_const * mixed_float, axis=-1),
                    jnp.sum(d_const * cvec_float[:, const_index][None, :], axis=-1),
                ],
                axis=-1,
            )
            d_mixlog = mixing * (d_mix - jnp.sum(mixing * d_mix, axis=-1, keepdims=True))
            cproj_grads.append(jnp.dot(mixed_float.T, d_mixlog, precision=HIGHEST))
            cvec_grads.append(jnp.sum(mixing[:, 1:] * d_const, axis=0))
            d_mixed = (
                d_mixed
                + mixing[:, :1] * d_const
                + jnp.dot(
                    d_mixlog,
                    cproj_float[:, 2 * const_index : 2 * const_index + 2].T,
                    precision=HIGHEST,
                )
            )
        grad_cproj = jnp.concatenate(cproj_grads, axis=1)
        grad_cvec = jnp.stack(cvec_grads, axis=1)
        d_pairs = weighted.reshape(2 * row_count, model_width).astype(jnp.bfloat16)
        d_packed = jnp.einsum(
            "sp,pd->sd", slot_table, d_pairs, preferred_element_type=jnp.float32
        ).astype(jnp.bfloat16)
        d_outgoing = jnp.broadcast_to(
            d_packed.reshape(expert_count, 1, capacity, model_width),
            (expert_count, half_count, capacity, model_width),
        ).reshape(peer_count, capacity, model_width)
        d_received = lax.all_to_all(d_outgoing, "ep", split_axis=0, concat_axis=0, tiled=True)
        flat_rows = kept_rows.reshape(-1, model_width)
        flat_grads = d_received.reshape(-1, model_width)
        gate_part = jnp.dot(flat_rows, gate_weight, preferred_element_type=jnp.float32)
        up_part = jnp.dot(flat_rows, up_weight, preferred_element_type=jnp.float32)
        activated = jax.nn.silu(gate_part)
        hidden = (activated * up_part).astype(jnp.bfloat16)
        grad_down = jnp.einsum("rf,rd->fd", hidden, flat_grads, preferred_element_type=jnp.float32)
        d_hidden = jnp.einsum(
            "rd,fd->rf", flat_grads, down_weight, preferred_element_type=jnp.float32
        )
        sigmoid_gate = jax.nn.sigmoid(gate_part)
        d_gate_part = (
            d_hidden * up_part * sigmoid_gate * (1.0 + gate_part * (1.0 - sigmoid_gate))
        ).astype(jnp.bfloat16)
        d_up_part = (d_hidden * activated).astype(jnp.bfloat16)
        grad_gate = jnp.einsum(
            "rd,rf->df", flat_rows, d_gate_part, preferred_element_type=jnp.float32
        )
        grad_up = jnp.einsum("rd,rf->df", flat_rows, d_up_part, preferred_element_type=jnp.float32)
        d_inputs = jnp.einsum(
            "rf,df->rd", d_gate_part, gate_weight, preferred_element_type=jnp.float32
        )
        d_inputs = d_inputs + jnp.einsum(
            "rf,df->rd", d_up_part, up_weight, preferred_element_type=jnp.float32
        )
        d_inputs = d_inputs.astype(jnp.bfloat16).reshape(peer_count, capacity, model_width)
        d_returned = lax.all_to_all(d_inputs, "ep", split_axis=0, concat_axis=0, tiled=True)
        d_halves = d_returned.reshape(expert_count, half_count, capacity, model_width)
        for half_index in range(half_count):
            d_pair_in = jnp.einsum(
                "sp,sd->pd",
                slot_table,
                d_halves[:, half_index].reshape(slot_count, model_width),
                preferred_element_type=jnp.float32,
            )
            d_mixed = d_mixed + jnp.sum(d_pair_in.reshape(row_count, 2, model_width), axis=1)
        expert_acc = add_tuple(expert_acc, (grad_gate, grad_up, grad_down))
        moe_vjp = jax.vjp(rms_scale, residual, moe_gain)[1]
        d_residual_norm, grad_moe_gain = moe_vjp(d_mixed)
        d_residual = grad_rows + d_residual_norm
        d_branch = d_residual.astype(jnp.bfloat16)
        grad_out = jnp.einsum("rd,re->de", attended, d_branch, preferred_element_type=jnp.float32)
        d_attended = (
            jnp.einsum("re,de->rd", d_branch, out_weight, preferred_element_type=jnp.float32)
            * valid_rows
        ).astype(jnp.bfloat16)
        d_heads = d_attended.reshape(row_count, head_count, HEAD)
        scores = (
            jnp.einsum("qhd,khd->hqk", queries, key_heads, preferred_element_type=jnp.float32)
            * 0.125
        )
        scores = jnp.where(allowed[None], scores, MASK_FILL)
        attn_probs = jnp.exp(scores - log_total)
        d_weights = jnp.einsum(
            "qhd,khd->hqk", d_heads, value_heads, preferred_element_type=jnp.float32
        )
        delta_rows = jnp.sum(attn_probs * d_weights, axis=-1, keepdims=True)
        d_scores = (attn_probs * (d_weights - delta_rows)).astype(jnp.bfloat16)
        d_queries = (
            jnp.einsum(
                "hqk,khd->qhd", d_scores, key_heads, preferred_element_type=jnp.float32
            ).reshape(row_count, model_width)
            * 0.125
        )
        d_values = jnp.einsum(
            "hqk,qhd->khd",
            attn_probs.astype(jnp.bfloat16),
            d_heads,
            preferred_element_type=jnp.float32,
        ).reshape(seq_length, model_width)
        d_keys = (
            jnp.einsum(
                "hqk,qhd->khd", d_scores, queries, preferred_element_type=jnp.float32
            ).reshape(seq_length, model_width)
            * 0.125
        )
        d_keys_mine, d_values_mine = (
            lax.psum_scatter(
                d_keys.astype(jnp.bfloat16), "ep", scatter_dimension=0, tiled=True
            ).astype(jnp.float32),
            lax.psum_scatter(
                d_values.astype(jnp.bfloat16), "ep", scatter_dimension=0, tiled=True
            ).astype(jnp.float32),
        )
        d_qkv = jnp.concatenate([d_queries, d_keys_mine, d_values_mine], axis=1).astype(
            jnp.bfloat16
        )
        grad_qkv = jnp.einsum("rd,re->de", normed, d_qkv, preferred_element_type=jnp.float32)
        d_normed = jnp.einsum("re,de->rd", d_qkv, qkv_weight, preferred_element_type=jnp.float32)
        attn_vjp = jax.vjp(rms_scale, token_rows, attn_gain)[1]
        d_tokens_norm, grad_attn_gain = attn_vjp(d_normed)
        input_grads.append(d_residual + d_tokens_norm)
        dense_terms = (
            grad_attn_gain,
            grad_qkv,
            grad_out,
            grad_moe_gain,
            grad_router,
            grad_cproj,
            grad_cvec,
        )
        dense_shares = (
            lax.psum_scatter(dense_terms[0], ("ep", "dp", "fs"), scatter_dimension=0, tiled=True),
            lax.psum_scatter(dense_terms[1], ("ep", "dp", "fs"), scatter_dimension=0, tiled=True),
            lax.psum_scatter(dense_terms[2], ("ep", "dp", "fs"), scatter_dimension=0, tiled=True),
            lax.psum_scatter(dense_terms[3], ("ep", "dp", "fs"), scatter_dimension=0, tiled=True),
            lax.psum_scatter(dense_terms[4], ("ep", "dp", "fs"), scatter_dimension=0, tiled=True),
            lax.psum_scatter(dense_terms[5], ("ep", "dp", "fs"), scatter_dimension=0, tiled=True),
            lax.psum_scatter(dense_terms[6], ("ep", "dp", "fs"), scatter_dimension=0, tiled=True),
        )
        dense_acc = add_tuple(dense_acc, dense_shares)
    expert_shares = (
        lax.psum_scatter(
            expert_acc[0][None].astype(jnp.bfloat16), ("dp", "fs"), scatter_dimension=1, tiled=True
        ).astype(jnp.float32),
        lax.psum_scatter(
            expert_acc[1][None].astype(jnp.bfloat16), ("dp", "fs"), scatter_dimension=1, tiled=True
        ).astype(jnp.float32),
        lax.psum_scatter(
            expert_acc[2][None].astype(jnp.bfloat16), ("dp", "fs"), scatter_dimension=1, tiled=True
        ).astype(jnp.float32),
    )
    return (
        jnp.stack(layer_outputs),
        jnp.stack(input_grads),
        jnp.stack(prev_grads),
        dense_acc[0],
        dense_acc[1],
        dense_acc[2],
        dense_acc[3],
        dense_acc[4],
        dense_acc[5],
        dense_acc[6],
        expert_shares[0],
        expert_shares[1],
        expert_shares[2],
    )


NEG = -1e30
KINDS = 2
SMALL = 16
LANES = 128
F32 = jnp.float32
BF16 = jnp.bfloat16


def dot(lhs, rhs, dims=((1,), (0,)), precision=None):
    return lax.dot_general(
        lhs, rhs, (dims, ((), ())), precision=precision, preferred_element_type=F32
    )


def norm_qkv_kernel(x_ref, gain_ref, w_ref, normed_ref, qkv_ref):
    rows = x_ref[...].astype(F32)
    inverse = lax.rsqrt(jnp.mean(rows * rows, axis=-1, keepdims=True) + NORM_EPS)
    normed = (rows * inverse * gain_ref[...]).astype(BF16)
    normed_ref[...] = normed
    qkv_ref[...] = dot(normed, w_ref[...]).astype(BF16)


def key_span(block, rows, reach):
    start = max(0, block * rows - reach)
    return start, (block + 1) * rows - start


def attend_kernel(rows, reach, q_ref, k_ref, v_ref, segc_ref, segr_ref, att_ref, lse_ref):
    length = q_ref.shape[0]
    for block in range(length // rows):
        start, width = key_span(block, rows, reach)
        queries = q_ref[block * rows : (block + 1) * rows, :]
        keys = k_ref[start : start + width, :]
        values = v_ref[start : start + width, :]
        seg_q = segc_ref[block * rows : (block + 1) * rows, :]
        seg_k = segr_ref[:, start : start + width]
        row_pos = block * rows + lax.broadcasted_iota(jnp.int32, (rows, width), 0)
        col_pos = start + lax.broadcasted_iota(jnp.int32, (rows, width), 1)
        allowed = (seg_q == seg_k) & (col_pos <= row_pos)
        lane = lax.broadcasted_iota(jnp.int32, (rows, LANES), 1)
        outs = []
        logs = []
        for head in range(2):
            mine = (lane // HEAD) == head
            scores = dot(jnp.where(mine, queries, 0), keys, ((1,), (1,))) * 0.125
            scores = jnp.where(allowed, scores, NEG)
            largest = jnp.max(scores, axis=-1, keepdims=True)
            powers = jnp.exp(scores - largest)
            total = jnp.sum(powers, axis=-1, keepdims=True)
            outs.append(dot(powers.astype(BF16), values) / total)
            logs.append(largest + jnp.log(total))
        valid = (seg_q != SEGS - 1).astype(F32)
        att = jnp.where(lane < HEAD, outs[0], outs[1]) * valid
        att_ref[block * rows : (block + 1) * rows, :] = att.astype(BF16)
        both = jnp.where(lane < HEAD, logs[0], logs[1]).T
        lse_ref[0, 0:1, block * rows : (block + 1) * rows] = both[0:1, :]
        lse_ref[0, 1:2, block * rows : (block + 1) * rows] = both[HEAD : HEAD + 1, :]


def attend_back_kernel(
    rows, reach, q_ref, k_ref, v_ref, do_ref, segc_ref, segr_ref, lse_ref,
    dq_ref, dk_ref, dv_ref, dk_sum, dv_sum,
):
    length = q_ref.shape[0]
    dk_sum[...] = jnp.zeros_like(dk_sum)
    dv_sum[...] = jnp.zeros_like(dv_sum)
    keys_turned = k_ref[...].T
    for block in range(length // rows):
        start, width = key_span(block, rows, reach)
        queries = q_ref[block * rows : (block + 1) * rows, :]
        grads = do_ref[block * rows : (block + 1) * rows, :]
        keys = k_ref[start : start + width, :]
        values = v_ref[start : start + width, :]
        seg_k = segc_ref[start : start + width, :]
        seg_q = segr_ref[:, block * rows : (block + 1) * rows]
        key_pos = start + lax.broadcasted_iota(jnp.int32, (width, rows), 0)
        query_pos = block * rows + lax.broadcasted_iota(jnp.int32, (width, rows), 1)
        allowed = (seg_q == seg_k) & (key_pos <= query_pos)
        lane = lax.broadcasted_iota(jnp.int32, (rows, LANES), 1)
        dq_parts = []
        for head in range(2):
            mine = (lane // HEAD) == head
            head_q = jnp.where(mine, queries, 0)
            head_g = jnp.where(mine, grads, 0)
            log_total = lse_ref[0, head : head + 1, block * rows : (block + 1) * rows]
            scores = dot(keys, head_q, ((1,), (1,))) * 0.125
            probs = jnp.exp(jnp.where(allowed, scores, NEG) - log_total)
            d_probs = dot(values, head_g, ((1,), (1,)))
            delta = jnp.sum(probs * d_probs, axis=0, keepdims=True)
            d_scores = (probs * (d_probs - delta)).astype(BF16)
            dv_sum[start : start + width, :] += dot(probs.astype(BF16), head_g)
            dk_sum[start : start + width, :] += dot(d_scores, head_q)
            turned = keys_turned[head * HEAD : (head + 1) * HEAD, start : start + width]
            dq_parts.append(dot(turned, d_scores))
        dq = jnp.concatenate(dq_parts, axis=0).T * 0.125
        dq_ref[block * rows : (block + 1) * rows, :] = dq.astype(BF16)
    dk_ref[...] = (dk_sum[...] * 0.125).astype(BF16)
    dv_ref[...] = dv_sum[...].astype(BF16)


def column(rows, index):
    return rows[:, index : index + 1]


def chosen_of(ctl):
    lane = lax.broadcasted_iota(jnp.int32, ctl.shape, 1).astype(F32)
    return ((lane == column(ctl, 8)) | (lane == column(ctl, 9))).astype(F32)


def finish_kernel(x_ref, own_ref, sib_ref, dres_ref, gain_ref, out_ref, gain_out_ref):
    rows = x_ref[...].astype(F32)
    d_normed = own_ref[...].astype(F32) + sib_ref[...].astype(F32)
    inverse = lax.rsqrt(jnp.mean(rows * rows, axis=-1, keepdims=True) + NORM_EPS)
    scaled = d_normed * gain_ref[...]
    mean = jnp.mean(scaled * rows, axis=-1, keepdims=True)
    out = dres_ref[...] + inverse * scaled - rows * (inverse * inverse * inverse * mean)
    out_ref[...] = out.astype(out_ref.dtype)

    @pl.when(pl.program_id(0) == 0)
    def _():
        gain_out_ref[...] = jnp.zeros_like(gain_out_ref)

    gain_out_ref[0:1, :] += jnp.sum(d_normed * rows * inverse, axis=0, keepdims=True)


def shape(dims, dtype):
    return jax.ShapeDtypeStruct(dims, dtype)


def whole(dims):
    return pl.BlockSpec(dims, lambda *_: (0,) * len(dims))


def per_row(rows, width):
    return pl.BlockSpec((rows, width), lambda i: (i, 0))


def params():
    return pltpu.CompilerParams(vmem_limit_bytes=56 * 1024 * 1024)


def cost(flops, moved):
    return pl.CostEstimate(flops=int(flops), bytes_accessed=int(moved), transcendentals=0)


class Mail:
    def __init__(self, send_sems, recv_sems):
        self.send_sems = send_sems
        self.recv_sems = recv_sems
        self.used = 0

    def copy(self, source, target, device):
        slot = self.used
        self.used = slot + 1
        return pltpu.make_async_remote_copy(
            src_ref=source,
            dst_ref=target,
            send_sem=self.send_sems.at[slot],
            recv_sem=self.recv_sems.at[slot],
            device_id=device,
            device_id_type=pl.DeviceIdType.MESH,
        )


def position():
    place = lax.axis_index("ep")
    return place // 2, place % 2, lax.axis_index("dp"), lax.axis_index("fs")


def greet(devices):
    barrier = pltpu.get_barrier_semaphore()
    total = 0
    for device, present in devices:
        if present is True:
            pl.semaphore_signal(
                barrier, inc=1, device_id=device, device_id_type=pl.DeviceIdType.MESH
            )
            total = total + 1
        else:

            @pl.when(present)
            def _():
                pl.semaphore_signal(
                    barrier, inc=1, device_id=device, device_id_type=pl.DeviceIdType.MESH
                )

            total = total + jnp.where(present, 1, 0)
    pl.semaphore_wait(barrier, total)


class Line:
    def __init__(self, mail, depth, slots):
        self.depth = depth
        self.slots = slots
        self.place = lax.axis_index("dp")
        y, x, z, core = position()
        self.copies = {}
        for way in range(2):
            step_to = 1 if way == 0 else -1
            device = (y * 2 + x, z + step_to, core)
            for step in range(depth - 1):
                for item, (acc, landing) in enumerate(slots):
                    shard = self.shard(way, step)
                    safe = jnp.clip(shard, 0, depth - 1)
                    self.copies[way, step, item] = mail.copy(
                        acc.at[safe], landing.at[way, step], device
                    )

    def shard(self, way, step):
        if way == 0:
            return self.place + self.depth - 1 - step
        return self.place - (self.depth - 1 - step)

    def sends(self, way, step):
        shard = self.shard(way, step)
        if way == 0:
            return (shard <= self.depth - 1) & (self.place < self.depth - 1)
        return (shard >= 0) & (self.place > 0)

    def gets(self, way, step):
        if way == 0:
            return (self.place > 0) & (self.shard(way, step + 1) <= self.depth - 1)
        return (self.place < self.depth - 1) & (self.shard(way, step + 1) >= 0)

    def send(self, step, item):
        for way in range(2):

            @pl.when(self.sends(way, step))
            def _():
                self.copies[way, step, item].start()

    def take(self, step, item):
        acc, landing = self.slots[item]
        for way in range(2):
            shard = jnp.clip(self.shard(way, step + 1), 0, self.depth - 1)

            @pl.when(self.gets(way, step))
            def _():
                self.copies[way, step, item].wait_recv()
                acc[shard] = (
                    acc[shard].astype(F32) + landing[way, step].astype(F32)
                ).astype(BF16)

    def finish(self, item, store):
        acc, landing = self.slots[item]
        store(acc[self.place].astype(F32))
        for way in range(2):

            @pl.when(self.gets(way, self.depth - 2))
            def _():
                self.copies[way, self.depth - 2, item].wait_recv()
                store(landing[way, self.depth - 2].astype(F32), True)

    def close(self):
        for (way, step, item), copy in self.copies.items():

            @pl.when(self.sends(way, step))
            def _():
                copy.wait_send()


def reduce_kernel(
    depth, cut,
    gate_ref, up_ref, down_ref, dense_ref, out_ref, dtok_ref, prev_ref,
    gate_out, up_out, down_out, own_out, sib_out, out_home, dtok_home, prev_home,
    gate_land, up_land, down_land, gate_acc, up_acc, down_acc,
    gate_line, up_line, down_line,
    y1_land, x1_land, y1_acc, x1_acc, x2_land, y2_land, dense_acc, dense_line, dense_sum,
    send_sems, recv_sems, local_sems,
):
    y, x, z, core = position()
    sibling = (y * 2 + x, z, 1 - core)
    across = (y * 2 + 1 - x, z, core)
    along = ((1 - y) * 2 + x, z, core)
    moved = y != core
    near = ((1 - y) * 2 + x, z, 1 - core)
    far = (core * 2 + 1 - x, z, y)
    greet(
        [
            (sibling, True), (across, True), (along, True),
            (near, moved), (far, moved),
            ((y * 2 + x, z + 1, core), z < depth - 1), ((y * 2 + x, z - 1, core), z > 0),
        ]
    )
    mail = Mail(send_sems, recv_sems)
    experts = [
        (gate_ref, gate_land, gate_acc, gate_line, gate_out),
        (up_ref, up_land, up_acc, up_line, up_out),
        (down_ref, down_land, down_acc, down_line, down_out),
    ]
    halves = [
        mail.copy(source.at[:, 1 - core], land, sibling)
        for source, land, _, _, _ in experts
    ]
    line = Line(mail, depth, [(acc, landing) for _, _, acc, landing, _ in experts])
    rest = dense_ref.shape[3] - cut
    left = pl.ds(0, cut)
    right = pl.ds(cut, rest)
    first_y = mail.copy(dense_ref.at[1 - y, :, :, left], y1_land, along)
    first_x = mail.copy(dense_ref.at[:, 1 - x, :, right], x1_land, across)
    second_x = mail.copy(y1_acc.at[1 - x], x2_land, across)
    second_y = mail.copy(x1_acc.at[1 - y], y2_land, along)
    dense = Line(mail, depth, [(dense_acc, dense_line)])
    homes = [(out_ref, out_home), (dtok_ref, dtok_home), (prev_ref, prev_home)]
    nears = [mail.copy(a.at[x], b.at[x], near) for a, b in homes]
    fars = [mail.copy(a.at[1 - x], b.at[x], far) for a, b in homes]
    stays = [
        pltpu.make_async_copy(a.at[x], b.at[x], local_sems.at[k])
        for k, (a, b) in enumerate(homes)
    ]

    for copy in halves:
        copy.start()
    first_y.start()
    first_x.start()
    for item, (source, land, acc, _, _) in enumerate(experts):
        halves[item].wait_recv()
        for shard in range(depth):
            acc[shard] = (source[shard, core].astype(F32) + land[shard].astype(F32)).astype(BF16)
        line.send(0, item)
    first_y.wait_recv()
    for k in range(2):
        y1_acc[k] = (dense_ref[y, k, :, left].astype(F32) + y1_land[k].astype(F32)).astype(BF16)
    second_x.start()
    first_x.wait_recv()
    for k in range(2):
        x1_acc[k] = (dense_ref[k, x, :, right].astype(F32) + x1_land[k].astype(F32)).astype(BF16)
    second_y.start()
    for copy in fars:
        copy.start()

    @pl.when(moved)
    def _():
        for copy in nears:
            copy.start()

    @pl.when(jnp.logical_not(moved))
    def _():
        for copy in stays:
            copy.start()

    for item in range(3):
        line.take(0, item)
        line.send(1, item)
    size = dense_acc.shape[1]
    second_x.wait_recv()
    second_y.wait_recv()
    for shard in range(depth):
        part = pl.ds(shard * size, size)
        dense_acc[shard, :, left] = (
            y1_acc[x, part].astype(F32) + x2_land[part].astype(F32)
        ).astype(BF16)
        dense_acc[shard, :, right] = (
            x1_acc[y, part].astype(F32) + y2_land[part].astype(F32)
        ).astype(BF16)
    dense.send(0, 0)
    for item in range(3):
        line.take(1, item)
        line.send(2, item)
    dense.take(0, 0)
    dense.send(1, 0)
    for item, (_, _, _, _, result) in enumerate(experts):

        def store(value, add=False):
            result[0] = result[0] + value if add else value

        line.finish(item, store)
    dense.take(1, 0)
    dense.send(2, 0)

    def store_dense(value, add=False):
        dense_sum[...] = dense_sum[...] + value if add else value

    dense.finish(0, store_dense)
    half = size // 2
    last = mail.copy(
        dense_sum.at[pl.ds(pl.multiple_of((1 - core) * half, 8), half)], sib_out, sibling
    )
    last.start()
    own_out[...] = dense_sum[pl.ds(pl.multiple_of(core * half, 8), half), :]
    last.wait()
    for copy in halves + [first_y, first_x, second_x, second_y]:
        copy.wait_send()
    line.close()
    dense.close()
    for copy in fars:
        copy.wait()

    @pl.when(moved)
    def _():
        for copy in nears:
            copy.wait()

    @pl.when(jnp.logical_not(moved))
    def _():
        for copy in stays:
            copy.wait()


def reduce_all(grad_gate, grad_up, grad_down, dense, block_out, d_tokens, d_prev):
    depth = lax.axis_size("dp")
    experts = [
        grad.reshape(depth, 2, grad.shape[0] // (2 * depth), grad.shape[1])
        for grad in (grad_gate, grad_up, grad_down)
    ]
    quarter = dense.shape[0] // 4
    columns = dense.shape[1]
    cut = (columns // LANES + 1) // 2 * LANES
    dense = dense.reshape(2, 2, quarter, columns)
    homes = [
        block_out,
        d_tokens.reshape(block_out.shape),
        d_prev,
    ]
    size = quarter // depth
    parts = [grad.shape[2:] for grad in experts]
    vmem = pl.BlockSpec(memory_space=pltpu.VMEM)
    copies = 3 + 2 * (depth - 1) * 4 + 4 + 6 + 1
    outs = pl.pallas_call(
        functools.partial(reduce_kernel, depth, cut),
        in_specs=[vmem] * 7,
        out_specs=[vmem] * 8,
        out_shape=[shape((1,) + part, F32) for part in parts]
        + [shape((size // 2, columns), F32)] * 2
        + [shape(home.shape, home.dtype) for home in homes],
        scratch_shapes=[pltpu.VMEM((depth,) + part, BF16) for part in parts] * 2
        + [pltpu.VMEM((2, depth - 1) + part, BF16) for part in parts]
        + [
            pltpu.VMEM((2, quarter, cut), BF16),
            pltpu.VMEM((2, quarter, columns - cut), BF16),
            pltpu.VMEM((2, quarter, cut), BF16),
            pltpu.VMEM((2, quarter, columns - cut), BF16),
            pltpu.VMEM((quarter, cut), BF16),
            pltpu.VMEM((quarter, columns - cut), BF16),
            pltpu.VMEM((depth, size, columns), BF16),
            pltpu.VMEM((2, depth - 1, size, columns), BF16),
            pltpu.VMEM((size, columns), F32),
            pltpu.SemaphoreType.DMA((copies,)),
            pltpu.SemaphoreType.DMA((copies,)),
            pltpu.SemaphoreType.DMA((3,)),
        ],
        compiler_params=pltpu.CompilerParams(
            collective_id=1, has_side_effects=True, vmem_limit_bytes=60 * 1024 * 1024
        ),
        name="reduce_all",
    )(*experts, dense, *homes)
    return outs


def spread_block(experts, routes, rows, block, refs, send_ref, recv_ref, keep):
    (att_own, att_sib, x_ref, g_ref, ctl_ref, w_own, w_sib, gain_ref, wsm_ref) = refs
    residual_ref, mixed_ref, pm_ref, place_ref = keep
    y, x, z, core = position()
    here = pl.ds(pl.multiple_of(block * rows, rows), rows)
    residual = x_ref[here, :].astype(F32) + (
        dot(att_own[here, :], w_own[...]) + dot(att_sib[here, :], w_sib[...])
    )
    residual_ref[here, :] = residual
    inverse = lax.rsqrt(jnp.mean(residual * residual, axis=-1, keepdims=True) + NORM_EPS)
    mixed = (residual * inverse * gain_ref[...]).astype(BF16)
    mixed_ref[here, :] = mixed
    logits = dot(mixed, wsm_ref[...])
    ctl = ctl_ref[here, :]
    lane = lax.broadcasted_iota(jnp.int32, (rows, LANES), 1)
    is_route = lane < routes
    router = jnp.where(is_route, logits + ctl, NEG)
    powers = jnp.exp(router - jnp.max(router, axis=-1, keepdims=True))
    probs = powers / jnp.sum(powers, axis=-1, keepdims=True)
    probs = jnp.where(is_route, probs, 0.0)
    pm = probs
    for const_index in range(2):
        first = column(logits, 8 + 2 * const_index)
        second = column(logits, 9 + 2 * const_index)
        largest = jnp.maximum(first, second)
        first = jnp.exp(first - largest)
        second = jnp.exp(second - largest)
        total = first + second
        pm = jnp.where(lane == 8 + 2 * const_index, first / total, pm)
        pm = jnp.where(lane == 9 + 2 * const_index, second / total, pm)
    pm_ref[here, :] = pm
    chosen = chosen_of(ctl)
    gated = chosen * probs
    earlier = lax.broadcasted_iota(jnp.int32, (rows, rows), 1) < lax.broadcasted_iota(
        jnp.int32, (rows, rows), 0
    )
    rank = dot(earlier.astype(BF16), chosen.astype(BF16))
    lane_f = lane.astype(F32)
    grads = g_ref[here, :].astype(F32)
    for expert in range(experts):
        place = jnp.where(
            (lane_f == column(rank, expert)) & (column(chosen, expert) > 0.0), 1.0, 0.0
        )
        place_ref[here, expert * LANES : (expert + 1) * LANES] = place.astype(BF16)
        pick = place.T.astype(BF16)
        d_part = (column(gated, expert) * grads).astype(BF16)
        send_ref[block, expert, 0] = dot(pick, mixed).astype(BF16)
        send_ref[block, expert, 1] = dot(pick, d_part).astype(BF16)
    recv_ref[block, y * 2 + x] = send_ref[block, y]


def expert_block(block, recv_ref, result_ref, back_ref, weights, keep):
    gate_w, up_w, down_w = weights
    hidden_ref, d_gate_ref, d_up_ref = keep
    y, x, z, core = position()
    peers, _, capacity, width = recv_ref.shape[1:]
    size = peers * capacity
    here = pl.ds(pl.multiple_of(block * size, size), size)
    rows = recv_ref[block, :, 0].reshape(size, width)
    d_rows = recv_ref[block, :, 1].reshape(size, width)
    gate = dot(rows, gate_w[...])
    up = dot(rows, up_w[...])
    sig = jax.nn.sigmoid(gate)
    active = gate * sig
    hidden = (active * up).astype(BF16)
    hidden_ref[here, :] = hidden
    part = dot(hidden, down_w[...]).astype(BF16)
    result_ref[block, :, 0] = part.reshape(peers, capacity, width)
    d_hidden = dot(d_rows, down_w[...], ((1,), (1,)))
    d_gate = (d_hidden * up * sig * (1.0 + gate * (1.0 - sig))).astype(BF16)
    d_up = (d_hidden * active).astype(BF16)
    d_gate_ref[here, :] = d_gate
    d_up_ref[here, :] = d_up
    d_in = dot(d_gate, gate_w[...], ((1,), (1,))) + dot(d_up, up_w[...], ((1,), (1,)))
    result_ref[block, :, 1] = d_in.astype(BF16).reshape(peers, capacity, width)
    back_ref[block, y * 2 + x] = result_ref[block, y * 2 + x]


def combine_block(experts, routes, rows, block, refs, keep, back_ref, outs, small_ref):
    g_ref, ctl_ref, gain_ref, turned_ref, cvec_ref = refs
    residual_ref, mixed_ref, pm_ref, place_ref = keep
    out_ref, prev_ref, dres_ref, branch_ref = outs
    halves = back_ref.shape[1] // experts
    here = pl.ds(pl.multiple_of(block * rows, rows), rows)
    g_low = g_ref[here, :]
    grads = g_low.astype(F32)
    mixed = mixed_ref[here, :].astype(F32)
    residual = residual_ref[here, :]
    pm = pm_ref[here, :]
    lane = lax.broadcasted_iota(jnp.int32, (rows, LANES), 1)
    chosen = chosen_of(ctl_ref[here, :])
    probs = jnp.where(lane < routes, pm, 0.0)
    gated = chosen * probs
    d_probs = jnp.zeros((rows, LANES), F32)
    result = residual
    d_mixed = None
    for expert in range(experts):
        place = place_ref[here, expert * LANES : (expert + 1) * LANES]
        expert_out = None
        for half in range(halves):
            owner = expert * halves + half
            term = dot(place, back_ref[block, owner, 0])
            expert_out = term if expert_out is None else expert_out + term
            term = dot(place, back_ref[block, owner, 1])
            d_mixed = term if d_mixed is None else d_mixed + term
        result = result + column(gated, expert) * expert_out
        d_gate = jnp.sum(expert_out * grads, axis=-1, keepdims=True)
        d_probs = jnp.where(lane == expert, d_gate, d_probs)
    g_mixed = jnp.sum(grads * mixed, axis=-1, keepdims=True)
    g_const = dot(g_low, cvec_ref[...], ((1,), (1,)))
    copy = experts + 1
    d_probs = jnp.where(lane == copy, g_mixed, d_probs)
    weight = column(gated, copy)
    d_small = jnp.zeros((rows, LANES), F32)
    for const_index in range(2):
        route = copy + 1 + const_index
        first = column(pm, 8 + 2 * const_index)
        second = column(pm, 9 + 2 * const_index)
        gate = column(gated, route)
        g_vec = column(g_const, const_index)
        d_probs = jnp.where(lane == route, first * g_mixed + second * g_vec, d_probs)
        weight = weight + gate * first
        vec = cvec_ref[const_index : const_index + 1, :].astype(F32)
        result = result + (gate * second) * vec
        d_first = gate * g_mixed
        d_second = gate * g_vec
        mean = first * d_first + second * d_second
        d_small = jnp.where(lane == 8 + 2 * const_index, first * (d_first - mean), d_small)
        d_small = jnp.where(lane == 9 + 2 * const_index, second * (d_second - mean), d_small)
        d_small = jnp.where(lane == 12 + const_index, gate * second, d_small)
    result = result + weight * mixed
    out_ref[block] = result.astype(BF16)
    d_probs = d_probs * chosen
    d_logits = probs * (d_probs - jnp.sum(probs * d_probs, axis=-1, keepdims=True))
    d_small = jnp.where(lane < routes, d_logits, d_small)
    d_mixed = d_mixed + weight * grads
    d_mixed = d_mixed + dot(
        jnp.where(lane < 12, d_small, 0.0), turned_ref[...], precision=HIGHEST
    )
    inverse = lax.rsqrt(jnp.mean(residual * residual, axis=-1, keepdims=True) + NORM_EPS)
    scaled = d_mixed * gain_ref[...]
    mean = jnp.mean(scaled * residual, axis=-1, keepdims=True)
    d_residual = grads + inverse * scaled - residual * (inverse * inverse * inverse * mean)
    dres_ref[here, :] = d_residual
    branch_ref[here, :] = d_residual.astype(BF16)
    d_turned = d_small.T[:SMALL, :]
    prev_ref[block] = d_turned[:8, :]
    sub = lax.broadcasted_iota(jnp.int32, (SMALL, rows), 0)
    small = dot(jnp.where(sub < 12, d_turned, 0.0), mixed, precision=HIGHEST)
    small = small + dot(
        jnp.where((sub >= 12) & (sub < 14), d_turned, 0.0), grads, precision=HIGHEST
    )
    d_gain = jnp.sum(d_mixed * residual * inverse, axis=0, keepdims=True)
    which = lax.broadcasted_iota(jnp.int32, small.shape, 0)
    small_ref[...] += jnp.where(which == 14, d_gain, small)


def layer_kernel(
    experts, routes, rows, blocks,
    att_ref, x_ref, g_ref, ctl_ref, w_own, w_sib, gain_ref, wsm_ref, turned_ref, cvec_ref,
    gate_ref, up_ref, down_ref,
    out_ref, prev_ref, dres_ref, branch_ref, small_ref, dgate_out, dup_out, ddown_out,
    att_own, att_sib, gate_w, up_w, down_w, residual_ref, mixed_ref, pm_ref, place_ref,
    send_ref, recv_ref, result_ref, back_ref, hidden_ref, d_gate_ref, d_up_ref,
    head_send, head_recv, local_sems, send_sems, recv_sems, back_send, back_recv,
):
    y, x, z, core = position()
    me = y * 2 + x
    sibling = (me, z, 1 - core)
    partners = [(1 - y) * 2 + 1 - x, y * 2 + 1 - x, (1 - y) * 2 + x]
    wanted = [1 - y, y, 1 - y]
    greet([(sibling, True)] + [((place, z, core), True) for place in partners])
    mine = rows * blocks
    mail = Mail(head_send, head_recv)
    pairs = [(gate_ref, gate_w), (up_ref, up_w), (down_ref, down_w)]
    heads = [mail.copy(att_ref.at[1 - core], att_sib, sibling)]
    locals_ = [pltpu.make_async_copy(att_ref.at[core], att_own, local_sems.at[3])]
    for k, (source, target) in enumerate(pairs):
        size = source.shape[0]
        spot = target.at[pl.ds(pl.multiple_of(core * size, size), size)]
        heads.append(mail.copy(source, spot, sibling))
        locals_.append(pltpu.make_async_copy(source, spot, local_sems.at[k]))
    for copy in heads + locals_:
        copy.start()

    def dispatch(block, k):
        return pltpu.make_async_remote_copy(
            src_ref=send_ref.at[block, wanted[k]],
            dst_ref=recv_ref.at[block, me],
            send_sem=send_sems.at[block, k],
            recv_sem=recv_sems.at[block, k],
            device_id=(partners[k], z, core),
            device_id_type=pl.DeviceIdType.MESH,
        )

    def giveback(block, k):
        return pltpu.make_async_remote_copy(
            src_ref=result_ref.at[block, partners[k]],
            dst_ref=back_ref.at[block, me],
            send_sem=back_send.at[block, k],
            recv_sem=back_recv.at[block, k],
            device_id=(partners[k], z, core),
            device_id_type=pl.DeviceIdType.MESH,
        )

    small_ref[...] = jnp.zeros_like(small_ref)
    heads[0].wait_recv()
    locals_[0].wait()
    keep = (residual_ref, mixed_ref, pm_ref, place_ref)
    spread_refs = (
        att_own, att_sib, x_ref, g_ref, ctl_ref, w_own, w_sib, gain_ref, wsm_ref
    )

    @pl.loop(0, blocks)
    def _(block):
        spread_block(experts, routes, rows, block, spread_refs, send_ref, recv_ref, keep)
        for k in range(3):
            dispatch(block, k).start()

    for copy in heads[1:]:
        copy.wait_recv()
    for copy in locals_[1:]:
        copy.wait()

    @pl.loop(0, blocks)
    def _(block):
        for k in range(3):
            dispatch(block, k).wait_recv()
        expert_block(
            block, recv_ref, result_ref, back_ref, (gate_w, up_w, down_w),
            (hidden_ref, d_gate_ref, d_up_ref),
        )
        for k in range(3):
            giveback(block, k).start()

    peers, _, capacity, width = recv_ref.shape[1:]
    total = blocks * peers * capacity
    step = 2 * LANES

    @pl.loop(0, width // step)
    def _(chunk):
        span = pl.ds(pl.multiple_of(chunk * step, step), step)
        lhs = recv_ref[:, :, 0, :, span].reshape(total, step).T
        dgate_out[span, :] = dot(lhs, d_gate_ref[...]).astype(BF16)
        dup_out[span, :] = dot(lhs, d_up_ref[...]).astype(BF16)

    @pl.loop(0, hidden_ref.shape[1] // step)
    def _(chunk):
        span = pl.ds(pl.multiple_of(chunk * step, step), step)
        lhs = hidden_ref[:, span].T
        rhs = recv_ref[:, :, 1].reshape(total, width)
        ddown_out[span, :] = dot(lhs, rhs).astype(BF16)

    @pl.loop(0, blocks)
    def _(block):
        for k in range(3):
            giveback(block, k).wait_recv()
        combine_block(
            experts, routes, rows, block, (g_ref, ctl_ref, gain_ref, turned_ref, cvec_ref),
            keep, back_ref, (out_ref, prev_ref, dres_ref, branch_ref), small_ref,
        )

    for copy in heads:
        copy.wait_send()
    for block in range(blocks):
        for k in range(3):
            dispatch(block, k).wait_send()
            giveback(block, k).wait_send()


def expert_layer(
    experts, routes, rows, attended, x_own, cot_own, ctl, w_own, w_sib, gain, wsm, turned,
    cvec, w_gate, w_up, w_down,
):
    mine, width = x_own.shape
    blocks = mine // rows
    peers = lax.axis_size("ep")
    span = attended.shape[1]
    hidden = w_gate.shape[1]
    vmem = pl.BlockSpec(memory_space=pltpu.VMEM)
    total = blocks * peers * LANES
    grads = [(2 * w.shape[0], w.shape[1]) for w in (w_gate, w_up, w_down)]
    return pl.pallas_call(
        functools.partial(layer_kernel, experts, routes, rows, blocks),
        in_specs=[vmem] * 13,
        out_specs=[vmem] * 8,
        out_shape=[
            shape((blocks, rows, width), BF16), shape((blocks, 8, rows), F32),
            shape((mine, width), F32), shape((mine, width), BF16), shape((SMALL, width), F32),
        ]
        + [shape(dims, BF16) for dims in grads],
        scratch_shapes=[pltpu.VMEM((mine, span), BF16)] * 2
        + [pltpu.VMEM(dims, BF16) for dims in grads]
        + [
            pltpu.VMEM((mine, width), F32), pltpu.VMEM((mine, width), BF16),
            pltpu.VMEM((mine, LANES), F32), pltpu.VMEM((mine, experts * LANES), BF16),
            pltpu.VMEM((blocks, experts, KINDS, LANES, width), BF16),
        ]
        + [pltpu.VMEM((blocks, peers, KINDS, LANES, width), BF16)] * 3
        + [pltpu.VMEM((total, hidden), BF16)] * 3
        + [
            pltpu.SemaphoreType.DMA((4,)), pltpu.SemaphoreType.DMA((4,)),
            pltpu.SemaphoreType.DMA((4,)),
        ]
        + [pltpu.SemaphoreType.DMA((blocks, 3))] * 4,
        compiler_params=pltpu.CompilerParams(
            collective_id=2, has_side_effects=True, vmem_limit_bytes=62 * 1024 * 1024
        ),
        name="expert_layer",
    )(
        attended.reshape(2, mine, span), x_own, cot_own, ctl, w_own, w_sib, gain, wsm,
        turned, cvec, w_gate, w_up, w_down,
    )


def one_chip(
    tokens,
    prev_logits,
    segments,
    routes,
    cotangent,
    gain_attn,
    w_qkv,
    w_out,
    gain_moe,
    w_router,
    const_proj,
    const_vec,
    w_gate,
    w_up,
    w_down,
):
    rows, width = tokens.shape[1:]
    peers = lax.axis_size("ep")
    place = lax.axis_index("ep")
    core = lax.axis_index("fs")
    cross = place % 2
    route_count = w_router.shape[1]
    experts = route_count - 4
    capacity = LANES
    length = rows * peers
    mine = length // 2
    span = width // 2
    hidden_width = w_gate.shape[2]
    pairs = [[], []]
    for flip in range(2):
        for source in range(peers):
            for side in range(2):
                target = side * 2 + ((source % 2) ^ flip)
                pairs[flip].append((source * 2 + side, target * 2 + source // 2))

    def swap(array):
        return lax.ppermute(array, "fs", [(0, 1), (1, 0)])

    def by_core(own, other, axis=0):
        return jnp.where(
            core == 0,
            jnp.concatenate([own, other], axis=axis),
            jnp.concatenate([other, own], axis=axis),
        )

    def to_chip(array):
        near = lax.ppermute(
            lax.dynamic_index_in_dim(array, cross, 0, False), ("ep", "fs"), pairs[0]
        )
        far = lax.ppermute(
            lax.dynamic_index_in_dim(array, 1 - cross, 0, False), ("ep", "fs"), pairs[1]
        )
        return jnp.where(
            cross == 0, jnp.concatenate([near, far]), jnp.concatenate([far, near])
        )

    x_own = to_chip(tokens)
    x_sib = swap(x_own)
    qkv_split = w_qkv.reshape(span, 3, 2, span)
    qkv_mine = lax.dynamic_index_in_dim(qkv_split, core, 2, False).reshape(span, 3 * span)
    qkv_sent = lax.dynamic_index_in_dim(qkv_split, 1 - core, 2, False).reshape(span, 3 * span)
    qkv_weight = by_core(qkv_mine, swap(qkv_sent))
    out_sib = swap(w_out)
    pad = jnp.zeros((span, 8 - route_count), BF16)
    small_own = jnp.concatenate(
        [w_router, pad, const_proj, const_vec, gain_attn[:, None], gain_moe[:, None]], axis=1
    )
    small_all = by_core(small_own, swap(small_own))
    small_turned = small_all.T.astype(F32)
    attn_gain = small_turned[14:15]
    moe_gain = small_turned[15:16]
    wsm = jnp.pad(small_all[:, :12], ((0, 0), (0, LANES - 12)))
    turned = jnp.pad(small_turned[:12], ((0, LANES - 12), (0, 0)))
    cvec_turned = jnp.pad(small_all[:, 12:14].T, ((0, LANES - 2), (0, 0)))
    seg_sib = swap(segments)
    seg_pair = by_core(segments[None], seg_sib[None])
    seg_row = seg_pair.reshape(4, length)[place][None, :]
    seg_col = seg_row.reshape(length, 1)

    x_all = by_core(x_own, x_sib)
    normed, qkv = pl.pallas_call(
        norm_qkv_kernel,
        grid=(length // rows,),
        in_specs=[per_row(rows, width), whole((1, width)), whole((width, 3 * span))],
        out_specs=[per_row(rows, width), per_row(rows, 3 * span)],
        out_shape=[shape((length, width), BF16), shape((length, 3 * span), BF16)],
        compiler_params=params(),
        cost_estimate=cost(2 * length * width * 3 * span, 6e6),
        name="norm_qkv",
    )(x_all, attn_gain, qkv_weight)

    head_pairs = span // LANES
    reach = length // 2

    def heads_at(offset):
        return pl.BlockSpec((length, LANES), lambda p: (0, offset + p))

    lse_spec = pl.BlockSpec((1, 8, length), lambda p: (p, 0, 0))
    attended, lse = pl.pallas_call(
        functools.partial(attend_kernel, rows, reach),
        grid=(head_pairs,),
        in_specs=[
            heads_at(0), heads_at(head_pairs), heads_at(2 * head_pairs),
            whole((length, 1)), whole((1, length)),
        ],
        out_specs=[heads_at(0), lse_spec],
        out_shape=[shape((length, span), BF16), shape((head_pairs, 8, length), F32)],
        compiler_params=params(),
        cost_estimate=cost(12e9, 4e6),
        name="attend",
    )(qkv, qkv, qkv, seg_col, seg_row)

    cot_own = to_chip(cotangent)
    ctl = jnp.concatenate(
        [
            prev_logits,
            jnp.zeros(prev_logits.shape[:2] + (8 - route_count,), F32),
            routes.astype(F32),
        ],
        axis=2,
    )
    ctl = jnp.pad(to_chip(ctl), ((0, 0), (0, LANES - 10)))
    blocks = mine // rows
    (
        block_out, d_prev, d_residual, d_branch, small, grad_gate, grad_up, grad_down,
    ) = expert_layer(
        experts, route_count, rows, attended, x_own, cot_own, ctl, w_out, out_sib, moe_gain,
        wsm, turned, cvec_turned, w_gate[0], w_up[0], w_down[0],
    )

    branch_all = by_core(d_branch, swap(d_branch))
    valid = (seg_col != SEGS - 1).astype(F32)
    d_att = (dot(branch_all, w_out, ((1,), (1,))) * valid).astype(BF16)
    grad_out = dot(attended, branch_all, ((0,), (0,))).astype(BF16)
    d_queries, d_keys, d_values = pl.pallas_call(
        functools.partial(attend_back_kernel, rows, reach),
        grid=(head_pairs,),
        in_specs=[
            heads_at(0), heads_at(head_pairs), heads_at(2 * head_pairs), heads_at(0),
            whole((length, 1)), whole((1, length)), lse_spec,
        ],
        out_specs=[heads_at(0)] * 3,
        out_shape=[shape((length, span), BF16)] * 3,
        scratch_shapes=[pltpu.VMEM((length, LANES), F32)] * 2,
        compiler_params=params(),
        cost_estimate=cost(30e9, 5e6),
        name="attend_back",
    )(qkv, qkv, qkv, d_att, seg_col, seg_row, lse)
    d_qkv = jnp.concatenate([d_queries, d_keys, d_values], axis=1)
    d_normed = dot(d_qkv, qkv_weight, ((1,), (1,)))
    d_normed_own = lax.dynamic_slice_in_dim(d_normed, core * mine, mine)
    d_normed_sib = swap(
        lax.dynamic_slice_in_dim(d_normed, (1 - core) * mine, mine).astype(BF16)
    )
    grad_qkv = dot(normed, d_qkv, ((0,), (0,))).astype(BF16)
    d_tokens, gain_rows = pl.pallas_call(
        finish_kernel,
        grid=(blocks,),
        in_specs=[per_row(rows, width)] * 4 + [whole((1, width))],
        out_specs=[per_row(rows, width), whole((8, width))],
        out_shape=[shape((mine, width), BF16), shape((8, width), F32)],
        compiler_params=params(),
        cost_estimate=cost(1e8, 6e6),
        name="finish",
    )(x_own, d_normed_own, d_normed_sib, d_residual, attn_gain)

    out_mine = lax.dynamic_slice_in_dim(grad_out, core * span, span, axis=1)
    out_sent = lax.dynamic_slice_in_dim(grad_out, (1 - core) * span, span, axis=1)
    out_cols = by_core(out_mine, swap(out_sent))
    small = jnp.concatenate([small[: SMALL - 1], gain_rows[:1]]).T.astype(BF16)
    dense = jnp.concatenate(
        [grad_qkv, out_cols, jnp.pad(small, ((0, 0), (0, LANES - SMALL)))], axis=1
    )
    shares = reduce_all(
        grad_gate, grad_up, grad_down, dense, block_out, d_tokens, d_prev
    )
    pieces = shares[3:5]
    out_home, dtok_home, prev_home = shares[5:]

    def columns_of(start):
        own, other = (piece[:, start : start + span] for piece in pieces)
        return by_core(own, other, axis=1)

    share_qkv = jnp.concatenate([columns_of(k * span) for k in range(3)], axis=1)
    share_out = columns_of(3 * span)
    share_small = sum(piece[:, 4 * span : 4 * span + SMALL] for piece in pieces)
    return (
        out_home,
        dtok_home.astype(F32),
        jnp.swapaxes(prev_home, 1, 2)[:, :, :route_count],
        share_small[:, 15],
        share_qkv,
        share_out,
        share_small[:, 14],
        share_small[:, :route_count],
        share_small[:, 8:12],
        share_small[:, 12:14],
    ) + tuple(shares[:3])


def suits(mesh, tokens, w_router, w_gate):
    peers = mesh.shape["ep"]
    rows = tokens.shape[1] // peers
    micro = tokens.shape[0] // (mesh.shape["dp"] * mesh.shape["fs"])
    routes = w_router.shape[1]
    return (
        peers == 4
        and mesh.shape["fs"] == 2
        and micro == 2
        and (routes - 4) * 2 == peers
        and 3 * rows // routes == LANES
        and tokens.shape[2] % (2 * LANES) == 0
    )


def solution(mesh):
    placed = (
        P(("dp", "fs"), "ep", None),
        P(("dp", "fs"), "ep", None),
        P(("dp", "fs"), None),
        P(("dp", "fs"), "ep", None),
        P(("dp", "fs"), "ep", None),
        P("fs"),
        P("fs", None),
        P("fs", None),
        P("fs"),
        P("fs", None),
        P("fs", None),
        P("fs", None),
        P("ep", "fs", None),
        P("ep", "fs", None),
        P("ep", "fs", None),
    )
    def layer(*arrays):
        fits = suits(mesh, arrays[0], arrays[9], arrays[12])
        return mapped(one_chip if fits else shards)(*arrays)

    def mapped(body):
        return jax.shard_map(
            body,
            mesh=mesh,
            in_specs=placed,
            out_specs=(
                P(("dp", "fs"), "ep", None),
                P(("dp", "fs"), "ep", None),
                P(("dp", "fs"), "ep", None),
                P(("ep", "dp", "fs")),
                P(("ep", "dp", "fs"), None),
                P(("ep", "dp", "fs"), None),
                P(("ep", "dp", "fs")),
                P(("ep", "dp", "fs"), None),
                P(("ep", "dp", "fs"), None),
                P(("ep", "dp", "fs"), None),
                P("ep", ("dp", "fs"), None),
                P("ep", ("dp", "fs"), None),
                P("ep", ("dp", "fs"), None),
            ),
            check_vma=False,
        )

    return layer
```

profile of v0, /device:TPU:0, one launch (start us, length us, event | category | flops | bytes accessed | tf_op | source)
XLA Modules:
  0.0 275.6 jit_solution(9470332770919262923)
XLA Ops:
  2.6 1.5 concatenate.101
  6.4 2.0 collective-permute-start.8
  8.4 2.9 %collective-permute-start.9 = (f32[256,10]{0,1:T(8,128)}, f32[256,10]{0,1:T(8,128)}, u32[]{:S(2)}, u32[]{:S(2)}) collective-permute-start(f32[256,10]{0,1:T(8,128)} %get-tuple-element.155), channel_id=1, source_target_pairs={{0,8},{1,24},{8,0},{9,16},{16,9},{17,25},{24,1},{25,17},{2,10},{3,... | collective-permute-start | bytes 30728 | tf_op jit(solution)/shard_map/ppermute | solution.py:1211
  11.2 1.3 collective-permute-start.10
  12.5 2.0 dynamic-slice_bitcast_fusion.3
  14.6 1.1 copy.83
  19.5 4.5 %collective-permute-start = (bf16[256,768]{1,0:T(8,128)(2,1)}, bf16[256,768]{1,0:T(8,128)(2,1)}, u32[]{:S(2)}, u32[]{:S(2)}) collective-permute-start(bf16[256,768]{1,0:T(8,128)(2,1)} %get-tuple-element.138), channel_id=1, source_target_pairs={{0,0},{1,16},{8,8},{9,24},{16,1},{17,17},{24,9},{25,25},{2,2},{3,1... | collective-permute-start | bytes 1179656 | tf_op jit(solution)/shard_map/ppermute | solution.py:1208
  28.1 1.6 collective-permute-start.6
  30.6 1.7 collective-permute-start.7
  32.3 3.9 %collective-permute-done.1 = bf16[256,768]{1,0:T(8,128)(2,1)} collective-permute-done((bf16[256,768]{1,0:T(8,128)(2,1)}, bf16[256,768]{1,0:T(8,128)(2,1)}, u32[]{:S(2)}, u32[]{:S(2)}) %collective-permute-start.1) | collective-permute-done | bytes 393248 | tf_op jit(solution)/shard_map/ppermute | solution.py:1211
  36.2 1.5 maximum_select_fusion.3.x_ref
  41.1 3.4 %collective-permute-done.7 = bf16[256,768]{1,0:T(8,128)(2,1)} collective-permute-done((bf16[256,768]{1,0:T(8,128)(2,1)}, bf16[256,768]{1,0:T(8,128)(2,1)}, u32[]{:S(2)}, u32[]{:S(2)}) %collective-permute-start.7) | collective-permute-done | bytes 393248 | tf_op jit(solution)/shard_map/ppermute | solution.py:1211
  44.6 2.2 maximum_select_fusion.4.g_ref
  46.8 3.2 %maximum_select_fusion.w_ref = bf16[768,1152]{1,0:T(8,128)(2,1)} fusion(bf16[384,1152]{1,0:T(8,128)(2,1)} %collective-permute-done.4, bf16[384,1152]{1,0:T(8,128)(2,1)S(1)} %copy.85, pred[]{:T(512)S(6)} %eq.6), kind=kLoop, calls=%fused_computation.4 | loop fusion | flops 7962624 | bytes 3538945 | tf_op jit(solution)/shard_map/jit(_where)/select_n | solution.py:1201
  50.0 3.1 %maximum_select_fusion.1.x_ref = bf16[1024,768]{1,0:T(8,128)(2,1)} fusion(bf16[512,768]{1,0:T(8,128)(2,1)} %collective-permute-done.2, bf16[512,768]{1,0:T(8,128)(2,1)S(1)} %maximum_select_fusion.3.x_ref, pred[]{:T(512)S(6)} %eq.6), kind=kLoop, calls=%fused_computation.5 | loop fusion | flops 7077888 | bytes 3145729 | tf_op jit(solution)/shard_map/jit(_where)/select_n | solution.py:1201
  53.1 6.1 %norm_qkv.1 = (bf16[1024,768]{1,0:T(8,128)(2,1)}, bf16[1024,1152]{1,0:T(8,128)(2,1)}) custom-call(bf16[1024,768]{1,0:T(8,128)(2,1)} %maximum_select_fusion.1.x_ref, f32[1,768]{1,0:T(1,128)} %get-tuple-element.151.gain_ref, bf16[768,1152]{1,0:T(8,128)(2,1)} %maximum_select_fusion.w_ref), custom_call_target="tpu_custom_call" | custom-call | flops 1811939328 | bytes 6000000 | tf_op jit(solution)/shard_map/norm_qkv/pallas_call | solution.py:1242
  59.2 12.9 %attend.1 = (bf16[1024,384]{1,0:T(8,128)(2,1)}, f32[3,8,1024]{2,1,0:T(8,128)}) custom-call(bf16[1024,1152]{1,0:T(8,128)(2,1)} %get-tuple-element.38.q_ref.k_ref.v_ref, bf16[1024,1152]{1,0:T(8,128)(2,1)} %get-tuple-element.38.q_ref.k_ref.v_ref, bf16[1024,1152]{1,0:T(8,128)(2,1)} %get-tuple-element.38.q_ref.k_ref.v_ref, s32[1024,1]{1,0:T(8,128)} %copy.87.segc_ref, ...), custom_call_target="tpu_custom_call" | custom-call | flops 12000000000 | bytes 4000000 | tf_op jit(solution)/shard_map/attend/pallas_call | solution.py:1260
  72.1 86.6 %expert_layer.1 = (bf16[2,256,768]{2,1,0:T(8,128)(2,1)}, f32[2,8,256]{2,1,0:T(8,128)}, f32[512,768]{1,0:T(8,128)}, bf16[512,768]{1,0:T(8,128)(2,1)}, f32[16,768]...) custom-call(bf16[2,512,384]{2,1,0:T(8,128)(2,1)} %bitcast.56, ...), custom_call_target="tpu_custom_call" | custom-call | tf_op jit(solution)/shard_map/expert_layer/pallas_call | solution.py:1128
  159.6 1.7 collective-permute-done.11
  161.3 2.2 convolution_convert_fusion.1
  163.8 1.9 multiply_convert_fusion.do_ref
  165.7 15.9 %attend_back.1 = (bf16[1024,384]{1,0:T(8,128)(2,1)}, bf16[1024,384]{1,0:T(8,128)(2,1)}, bf16[1024,384]{1,0:T(8,128)(2,1)}) custom-call(bf16[1024,1152]{1,0:T(8,128)(2,1)} %get-tuple-element.38.q_ref.k_ref.v_ref, bf16[1024,1152]{1,0:T(8,128)(2,1)} %get-tuple-element.38.q_ref.k_ref.v_ref, bf16[1024,1152]{1,0:T(8,128)(2,1)} %get-tuple-element.38.q_ref.k_ref.v_ref, ...), custom_call_target="tpu_custom_call" | custom-call | flops 30000001024 | bytes 5000000 | tf_op jit(solution)/shard_map/attend_back/pallas_call | solution.py:1296
  181.6 1.3 constant_dynamic-update-slice_fusion.2
  183.3 1.1 copy-done.2
  184.5 2.2 fusion.7
  187.2 2.3 convolution_convert_fusion
  189.5 1.3 constant_dynamic-slice_fusion.own_ref
  191.8 3.4 %finish.1 = (bf16[512,768]{1,0:T(8,128)(2,1)}, f32[8,768]{1,0:T(8,128)}) custom-call(bf16[512,768]{1,0:T(8,128)(2,1)} %copy-done, f32[512,768]{1,0:T(8,128)} %constant_dynamic-slice_fusion.own_ref, bf16[512,768]{1,0:T(8,128)(2,1)} %copy-done.3, f32[512,768]{1,0:T(8,128)} %get-tuple-element.50.dres_ref, f32[1,768]{1,0:T(1,128)} %get-tuple-element.151.gain_ref), custom_call_target="tpu_custom_call" | custom-call | flops 100000000 | bytes 6000000 | tf_op jit(solution)/shard_map/finish/pallas_call | solution.py:1317
  196.2 1.7 fusion.1
  197.9 64.3 %reduce_all.1 = (f32[1,96,1024]{2,1,0:T(8,128)}, f32[1,96,1024]{2,1,0:T(8,128)}, f32[1,128,768]{2,1,0:T(8,128)}, f32[24,1664]{1,0:T(8,128)}, f32[24,1664]{1,0:T(...) custom-call(bf16[4,2,96,1024]{3,2,1,0:T(8,128)(2,1)} %bitcast.49, ...), custom_call_target="tpu_custom_call" | custom-call | tf_op jit(solution)/shard_map/reduce_all/pallas_call | solution.py:815
  267.4 1.3 copy.94
  268.7 2.4 convert_element_type.59
  (106 shorter events, 30.2 us)
Async XLA Ops:
  0.6 13.9 %copy-start.1 = (bf16[384,2304]{1,0:T(8,128)(2,1)S(1)}, bf16[384,2304]{1,0:T(8,128)(2,1)}, u32[]{:S(2)}) copy-start(bf16[384,2304]{1,0:T(8,128)(2,1)} %param.21) | copy-start | bytes 5308420
  0.7 18.8 %collective-permute-start.5 = (s32[2,1024]{1,0:T(2,128)}, s32[2,1024]{1,0:T(2,128)}, u32[]{:S(2)}, u32[]{:S(2)}) collective-permute-start(s32[2,1024]{1,0:T(2,128)} %param.17), channel_id=1, source_target_pairs={{0,1},{1,0},{2,3},{3,2},{4,5},{5,4},{6,7},{7,6},{8,9},{9,8},{10,11... | collective-permute-start | bytes 24584 | tf_op jit(solution)/shard_map/ppermute | solution.py:1198
  4.0 24.1 %collective-permute-start.3 = (bf16[384,16]{0,1:T(8,128)(2,1)S(1)}, bf16[384,16]{0,1:T(8,128)(2,1)}, u32[]{:S(2)}, u32[]{:S(2)}) collective-permute-start(bf16[384,16]{0,1:T(8,128)(2,1)S(1)} %concatenate.101), channel_id=1, source_target_pairs={{0,1},{1,0},{2,3},{3,2},{4,5},{5,4},{6,7},{7,6},{8,9},{9,8},{10,11... | collective-permute-start | bytes 36872 | tf_op jit(solution)/shard_map/ppermute | solution.py:1198
  6.4 19.5 %collective-permute-start.8 = (f32[256,10]{0,1:T(8,128)}, f32[256,10]{0,1:T(8,128)}, u32[]{:S(2)}, u32[]{:S(2)}) collective-permute-start(f32[256,10]{0,1:T(8,128)} %get-tuple-element.154), channel_id=1, source_target_pairs={{0,0},{1,16},{8,8},{9,24},{16,1},{17,17},{24,9},{25,25},{2,2},{3,1... | collective-permute-start | bytes 30728 | tf_op jit(solution)/shard_map/ppermute | solution.py:1208
  8.4 17.9 %collective-permute-start.9 = (f32[256,10]{0,1:T(8,128)}, f32[256,10]{0,1:T(8,128)}, u32[]{:S(2)}, u32[]{:S(2)}) collective-permute-start(f32[256,10]{0,1:T(8,128)} %get-tuple-element.155), channel_id=1, source_target_pairs={{0,8},{1,24},{8,0},{9,16},{16,9},{17,25},{24,1},{25,17},{2,10},{3,... | collective-permute-start | bytes 30728 | tf_op jit(solution)/shard_map/ppermute | solution.py:1211
  11.2 60.9 %collective-permute-start.10 = (bf16[384,768]{1,0:T(8,128)(2,1)}, bf16[384,768]{1,0:T(8,128)(2,1)}, u32[]{:S(2)}, u32[]{:S(2)}) collective-permute-start(bf16[384,768]{1,0:T(8,128)(2,1)} %w_own.1), channel_id=1, source_target_pairs={{0,1},{1,0},{2,3},{3,2},{4,5},{5,4},{6,7},{7,6},{8,9},{9,8},{10,11... | collective-permute-start | bytes 1769480 | tf_op jit(solution)/shard_map/ppermute | solution.py:1198
  15.7 1.1 copy-start.7
  17.7 6.3 %copy-start.14 = (s32[2,1024]{1,0:T(2,128)S(1)}, s32[2,1024]{1,0:T(2,128)}, u32[]{:S(2)}) copy-start(s32[2,1024]{1,0:T(2,128)} %param.17) | copy-start | bytes 24580
  19.5 11.1 %collective-permute-start = (bf16[256,768]{1,0:T(8,128)(2,1)}, bf16[256,768]{1,0:T(8,128)(2,1)}, u32[]{:S(2)}, u32[]{:S(2)}) collective-permute-start(bf16[256,768]{1,0:T(8,128)(2,1)} %get-tuple-element.138), channel_id=1, source_target_pairs={{0,0},{1,16},{8,8},{9,24},{16,1},{17,17},{24,9},{25,25},{2,2},{3,1... | collective-permute-start | bytes 1179656 | tf_op jit(solution)/shard_map/ppermute | solution.py:1208
  24.8 12.9 %copy-start.13 = (s32[1,1024]{1,0:T(1,128)}, s32[1,1024]{1,0:T(1,128)S(1)}, u32[]{:S(2)}) copy-start(s32[1,1024]{1,0:T(1,128)S(1)} %get-tuple-element.131.segr_ref) | copy-start | bytes 12292
  25.9 10.3 %collective-permute-start.1 = (bf16[256,768]{1,0:T(8,128)(2,1)}, bf16[256,768]{1,0:T(8,128)(2,1)}, u32[]{:S(2)}, u32[]{:S(2)}) collective-permute-start(bf16[256,768]{1,0:T(8,128)(2,1)} %get-tuple-element.139), channel_id=1, source_target_pairs={{0,8},{1,24},{8,0},{9,16},{16,9},{17,25},{24,1},{25,17},{2,10},{3,... | collective-permute-start | bytes 1179656 | tf_op jit(solution)/shard_map/ppermute | solution.py:1211
  26.3 20.5 %collective-permute-start.4 = (bf16[384,1152]{1,0:T(8,128)(2,1)S(1)}, bf16[384,1152]{1,0:T(8,128)(2,1)}, u32[]{:S(2)}, u32[]{:S(2)}) collective-permute-start(bf16[384,1152]{1,0:T(8,128)(2,1)S(1)} %copy.84), channel_id=1, source_target_pairs={{0,1},{1,0},{2,3},{3,2},{4,5},{5,4},{6,7},{7,6},{8,9},{9,8},{10,11... | collective-permute-start | bytes 2654216 | tf_op jit(solution)/shard_map/ppermute | solution.py:1198
  28.1 13.0 %collective-permute-start.6 = (bf16[256,768]{1,0:T(8,128)(2,1)}, bf16[256,768]{1,0:T(8,128)(2,1)S(1)}, u32[]{:S(2)}, u32[]{:S(2)}) collective-permute-start(bf16[256,768]{1,0:T(8,128)(2,1)} %get-tuple-element.136), channel_id=1, source_target_pairs={{0,0},{1,16},{8,8},{9,24},{16,1},{17,17},{24,9},{25,25},{2,2},{3,1... | collective-permute-start | bytes 1179656 | tf_op jit(solution)/shard_map/ppermute | solution.py:1208
  30.6 14.0 %collective-permute-start.7 = (bf16[256,768]{1,0:T(8,128)(2,1)}, bf16[256,768]{1,0:T(8,128)(2,1)}, u32[]{:S(2)}, u32[]{:S(2)}) collective-permute-start(bf16[256,768]{1,0:T(8,128)(2,1)} %get-tuple-element.137), channel_id=1, source_target_pairs={{0,8},{1,24},{8,0},{9,16},{16,9},{17,25},{24,1},{25,17},{2,10},{3,... | collective-permute-start | bytes 1179656 | tf_op jit(solution)/shard_map/ppermute | solution.py:1211
  37.7 12.3 %copy-start = (bf16[512,768]{1,0:T(8,128)(2,1)}, bf16[512,768]{1,0:T(8,128)(2,1)S(1)}, u32[]{:S(2)}) copy-start(bf16[512,768]{1,0:T(8,128)(2,1)S(1)} %maximum_select_fusion.3.x_ref) | copy-start | bytes 2359300
  37.7 12.3 %collective-permute-start.2 = (bf16[512,768]{1,0:T(8,128)(2,1)S(1)}, bf16[512,768]{1,0:T(8,128)(2,1)}, u32[]{:S(2)}, u32[]{:S(2)}) collective-permute-start(bf16[512,768]{1,0:T(8,128)(2,1)S(1)} %maximum_select_fusion.3.x_ref), channel_id=1, source_target_pairs={{0,1},{1,0},{2,3},{3,2},{4,5},{5,4},{6,7},{7,6},{8,9},{9,8},{10,11... | collective-permute-start | bytes 2359304 | tf_op jit(solution)/shard_map/ppermute | solution.py:1198
  72.1 89.2 %copy-start.8 = (bf16[1024,384]{1,0:T(8,128)(2,1)S(1)}, bf16[1024,384]{1,0:T(8,128)(2,1)}, u32[]{:S(2)}) copy-start(bf16[1024,384]{1,0:T(8,128)(2,1)} %get-tuple-element.39) | copy-start | bytes 2359300
  158.7 2.6 collective-permute-start.11
  159.6 4.2 %copy-start.9 = (bf16[384,768]{1,0:T(8,128)(2,1)S(1)}, bf16[384,768]{1,0:T(8,128)(2,1)}, u32[]{:S(2)}) copy-start(bf16[384,768]{1,0:T(8,128)(2,1)} %w_own.1) | copy-start | bytes 1769476
  159.6 4.2 %copy-start.15 = (bf16[512,768]{1,0:T(8,128)(2,1)S(1)}, bf16[512,768]{1,0:T(8,128)(2,1)}, u32[]{:S(2)}) copy-start(bf16[512,768]{1,0:T(8,128)(2,1)} %get-tuple-element.44) | copy-start | bytes 2359300
  163.6 27.2 %collective-permute-start.12 = (bf16[384,384]{1,0:T(8,128)(2,1)S(1)}, bf16[384,384]{1,0:T(8,128)(2,1)S(1)}, u32[]{:S(2)}, u32[]{:S(2)}) collective-permute-start(bf16[384,384]{1,0:T(8,128)(2,1)S(1)} %get-tuple-element.141), channel_id=1, source_target_pairs={{0,1},{1,0},{2,3},{3,2},{4,5},{5,4},{6,7},{7,6},{8,9},{9,8},{10,11... | collective-permute-start | bytes 884744 | tf_op jit(solution)/shard_map/ppermute | solution.py:1198
  181.6 1.4 copy-start.6
  181.6 1.6 copy-start.5
  182.9 1.5 copy-start.2
  184.5 2.8 %copy-start.16 = (bf16[1024,768]{1,0:T(8,128)(2,1)S(1)}, bf16[1024,768]{1,0:T(8,128)(2,1)}, u32[]{:S(2)}) copy-start(bf16[1024,768]{1,0:T(8,128)(2,1)} %get-tuple-element.43) | copy-start | bytes 4718596
  186.8 4.2 %collective-permute-start.13 = (bf16[512,768]{1,0:T(8,128)(2,1)S(1)}, bf16[512,768]{1,0:T(8,128)(2,1)S(1)}, u32[]{:S(2)}, u32[]{:S(2)}) collective-permute-start(bf16[512,768]{1,0:T(8,128)(2,1)S(1)} %dynamic-slice_convert_fusion), channel_id=1, source_target_pairs={{0,1},{1,0},{2,3},{3,2},{4,5},{5,4},{6,7},{7,6},{8,9},{9,8},{10,11... | collective-permute-start | bytes 2359304 | tf_op jit(solution)/shard_map/ppermute | solution.py:1198
  191.0 0.9 copy-start.3
  265.4 7.1 %copy-start.4 = (bf16[2,256,768]{2,1,0:T(8,128)(2,1)S(1)}, bf16[2,256,768]{2,1,0:T(8,128)(2,1)}, u32[]{:S(2)}) copy-start(bf16[2,256,768]{2,1,0:T(8,128)(2,1)} %get-tuple-element.173) | copy-start | bytes 2359300
  271.1 2.3 copy-start.12
  271.1 3.0 %copy-start.11 = (f32[1,96,1024]{2,1,0:T(8,128)S(1)}, f32[1,96,1024]{2,1,0:T(8,128)}, u32[]{:S(2)}) copy-start(f32[1,96,1024]{2,1,0:T(8,128)} %get-tuple-element.184) | copy-start | bytes 1179652
  271.8 3.1 %copy-start.10 = (f32[1,128,768]{2,1,0:T(8,128)S(1)}, f32[1,128,768]{2,1,0:T(8,128)}, u32[]{:S(2)}) copy-start(f32[1,128,768]{2,1,0:T(8,128)} %get-tuple-element.185) | copy-start | bytes 1179652
where the time goes:
time: 277 us; the launch traced here: 276 us
  Pallas kernels  189 us (68%)
  local copies, waits for them, and re-layouts  32 us (12%)
  other arithmetic  19.6 us (7%)
  starting transfers between devices  16.3 us (6%)
  waiting for transfers between devices  9.03 us (3%)
  matrix products  8.62 us (3%)
    pallas_call x1, Pallas kernels, expert_layer(): pl.pallas_call(functools.partial(layer_kernel, experts, routes, rows, blo...  86.6 us
    pallas_call x1, Pallas kernels, reduce_all(): pl.pallas_call(functools.partial(reduce_kernel, depth, cut), in_specs=[vm...  64.3 us
    pallas_call x1, Pallas kernels, one_chip(): pl.pallas_call(functools.partial(attend_back_kernel, rows, reach), grid=(...  15.9 us
    unnamed x48, local copies, waits for them, and re-layouts  13.1 us
    pallas_call x1, Pallas kernels, one_chip(): pl.pallas_call(functools.partial(attend_kernel, rows, reach), grid=(head_...  12.9 us
    dot_general x4, matrix products, dot(): lax.dot_general(lhs, rhs, (dims, ((), ())), precision=precision, preferre...  8.62 us
    ppermute x3, starting transfers between devices, to_chip(): lax.ppermute(lax.dynamic_index_in_dim(array, cross, 0, False), ('ep', 'fs...  8.1 us
    select_n x6, other arithmetic, by_core(): jnp.where(core == 0, jnp.concatenate([own, other], axis=axis), jnp.concat...  7.94 us
  transfers between devices with their start and end apart: 14, of which 3 were waited for; matrix products, arithmetic and copies ran while one was open for 14% of the time, Pallas kernels for 13%

commit v1 on v0

--- a/solution.py
+++ b/solution.py
@@ -408,49 +408,9 @@
     )
 
 
-def norm_qkv_kernel(x_ref, gain_ref, w_ref, normed_ref, qkv_ref):
-    rows = x_ref[...].astype(F32)
-    inverse = lax.rsqrt(jnp.mean(rows * rows, axis=-1, keepdims=True) + NORM_EPS)
-    normed = (rows * inverse * gain_ref[...]).astype(BF16)
-    normed_ref[...] = normed
-    qkv_ref[...] = dot(normed, w_ref[...]).astype(BF16)
-
-
 def key_span(block, rows, reach):
     start = max(0, block * rows - reach)
     return start, (block + 1) * rows - start
-
-
-def attend_kernel(rows, reach, q_ref, k_ref, v_ref, segc_ref, segr_ref, att_ref, lse_ref):
-    length = q_ref.shape[0]
-    for block in range(length // rows):
-        start, width = key_span(block, rows, reach)
-        queries = q_ref[block * rows : (block + 1) * rows, :]
-        keys = k_ref[start : start + width, :]
-        values = v_ref[start : start + width, :]
-        seg_q = segc_ref[block * rows : (block + 1) * rows, :]
-        seg_k = segr_ref[:, start : start + width]
-        row_pos = block * rows + lax.broadcasted_iota(jnp.int32, (rows, width), 0)
-        col_pos = start + lax.broadcasted_iota(jnp.int32, (rows, width), 1)
-        allowed = (seg_q == seg_k) & (col_pos <= row_pos)
-        lane = lax.broadcasted_iota(jnp.int32, (rows, LANES), 1)
-        outs = []
-        logs = []
-        for head in range(2):
-            mine = (lane // HEAD) == head
-            scores = dot(jnp.where(mine, queries, 0), keys, ((1,), (1,))) * 0.125
-            scores = jnp.where(allowed, scores, NEG)
-            largest = jnp.max(scores, axis=-1, keepdims=True)
-            powers = jnp.exp(scores - largest)
-            total = jnp.sum(powers, axis=-1, keepdims=True)
-            outs.append(dot(powers.astype(BF16), values) / total)
-            logs.append(largest + jnp.log(total))
-        valid = (seg_q != SEGS - 1).astype(F32)
-        att = jnp.where(lane < HEAD, outs[0], outs[1]) * valid
-        att_ref[block * rows : (block + 1) * rows, :] = att.astype(BF16)
-        both = jnp.where(lane < HEAD, logs[0], logs[1]).T
-        lse_ref[0, 0:1, block * rows : (block + 1) * rows] = both[0:1, :]
-        lse_ref[0, 1:2, block * rows : (block + 1) * rows] = both[HEAD : HEAD + 1, :]
 
 
 def attend_back_kernel(
@@ -467,8 +427,8 @@
         grads = do_ref[block * rows : (block + 1) * rows, :]
         keys = k_ref[start : start + width, :]
         values = v_ref[start : start + width, :]
-        seg_k = segc_ref[start : start + width, :]
-        seg_q = segr_ref[:, block * rows : (block + 1) * rows]
+        seg_k = segc_ref[start : start + width, 0:1]
+        seg_q = segr_ref[0:1, block * rows : (block + 1) * rows]
         key_pos = start + lax.broadcasted_iota(jnp.int32, (width, rows), 0)
         query_pos = block * rows + lax.broadcasted_iota(jnp.int32, (width, rows), 1)
         allowed = (seg_q == seg_k) & (key_pos <= query_pos)
@@ -843,20 +803,257 @@
     return outs
 
 
+def attend_pair(pair, rows, reach, span, qkv_ref, segc_ref, segr_ref, att_ref, lse_ref):
+    length = qkv_ref.shape[0]
+    at_q, at_k, at_v = (
+        pl.ds(pl.multiple_of(part * span + pair * LANES, LANES), LANES) for part in range(3)
+    )
+    for block in range(length // rows):
+        start, width = key_span(block, rows, reach)
+        here = pl.ds(block * rows, rows)
+        there = pl.ds(start, width)
+        queries = qkv_ref[here, at_q]
+        keys = qkv_ref[there, at_k]
+        values = qkv_ref[there, at_v]
+        seg_q = segc_ref[here, 0:1]
+        seg_k = segr_ref[0:1, there]
+        row_pos = block * rows + lax.broadcasted_iota(jnp.int32, (rows, width), 0)
+        col_pos = start + lax.broadcasted_iota(jnp.int32, (rows, width), 1)
+        allowed = (seg_q == seg_k) & (col_pos <= row_pos)
+        lane = lax.broadcasted_iota(jnp.int32, (rows, LANES), 1)
+        outs = []
+        logs = []
+        for head in range(2):
+            mine = (lane // HEAD) == head
+            scores = dot(jnp.where(mine, queries, 0), keys, ((1,), (1,))) * 0.125
+            scores = jnp.where(allowed, scores, NEG)
+            largest = jnp.max(scores, axis=-1, keepdims=True)
+            powers = jnp.exp(scores - largest)
+            total = jnp.sum(powers, axis=-1, keepdims=True)
+            outs.append(dot(powers.astype(BF16), values) / total)
+            logs.append(largest + jnp.log(total))
+        valid = (seg_q != SEGS - 1.0).astype(F32)
+        att = jnp.where(lane < HEAD, outs[0], outs[1]) * valid
+        att_ref[here, at_q] = att.astype(BF16)
+        both = jnp.where(lane < HEAD, logs[0], logs[1]).T
+        lse_ref[pair, 0:1, here] = both[0:1, :]
+        lse_ref[pair, 1:2, here] = both[HEAD : HEAD + 1, :]
+
+
+def gather_kernel(
+    rows, reach, routes,
+    tok_ref, cot_ref, wqkv_ref, wout_ref, prev_ref, route_ref, seg_ref, router_ref, cproj_ref,
+    cvec_ref, gain_a_ref, gain_m_ref,
+    x_all, cot_own, ctl_own, normed_ref, qkv_ref, att_ref, lse_ref, small_all, wqkv_all,
+    wout_sib, segc_ref, segr_ref,
+    ctl_wide, ctl_send, small_wide, small_send, seg_all,
+    near_send, near_recv, far_send, far_recv, core_send, core_recv, local_sems,
+):
+    y, x, z, core = position()
+    me = y * 2 + x
+    sibling = (me, z, 1 - core)
+    moved = y != core
+    near = ((1 - y) * 2 + x, z, 1 - core)
+    far = (core * 2 + 1 - x, z, y)
+    greet([(sibling, True), (far, True), (near, moved)])
+    span = wqkv_ref.shape[0]
+
+    def block_of(index):
+        return pl.ds(pl.multiple_of(index * rows, rows), rows)
+
+    within = block_of(x)
+    homes = [
+        (tok_ref, x_all.at[block_of(me)]),
+        (cot_ref, cot_own.at[within]),
+        (ctl_send, ctl_own.at[x]),
+    ]
+    nears = Mail(near_send, near_recv)
+    fars = Mail(far_send, far_recv)
+    near_copies = [nears.copy(a.at[x], b, near) for a, b in homes]
+    far_copies = [fars.copy(a.at[1 - x], b, far) for a, b in homes]
+    stay_copies = [
+        pltpu.make_async_copy(a.at[x], b, local_sems.at[k]) for k, (a, b) in enumerate(homes)
+    ]
+
+    def send(k):
+        far_copies[k].start()
+
+        @pl.when(moved)
+        def _():
+            near_copies[k].start()
+
+        @pl.when(jnp.logical_not(moved))
+        def _():
+            stay_copies[k].start()
+
+    def take_near(k):
+        @pl.when(moved)
+        def _():
+            near_copies[k].wait_recv()
+
+        @pl.when(jnp.logical_not(moved))
+        def _():
+            stay_copies[k].wait()
+
+    send(0)
+    inner = Mail(core_send, core_recv)
+    weight_copies = []
+    own_copies = []
+    band = pl.ds(pl.multiple_of(core * span, span), span)
+    for part in range(3):
+        columns = pl.ds(part * span, span)
+        for side, copies in ((1 - core, weight_copies), (core, own_copies)):
+            source = wqkv_ref.at[
+                :, pl.ds(pl.multiple_of(part * 2 * span + side * span, LANES), span)
+            ]
+            target = wqkv_all.at[band, columns]
+            if copies is weight_copies:
+                copies.append(inner.copy(source, target, sibling))
+            else:
+                copies.append(
+                    pltpu.make_async_copy(source, target, local_sems.at[3 + part])
+                )
+    out_copy = inner.copy(wout_ref, wout_sib, sibling)
+    seg_copy = inner.copy(seg_ref, seg_all.at[core], sibling)
+    seg_own = pltpu.make_async_copy(seg_ref, seg_all.at[core], local_sems.at[6])
+    small_copy = inner.copy(small_send, small_all.at[:, band], sibling)
+    seg_copy.start()
+    seg_own.start()
+    for copy in weight_copies + own_copies:
+        copy.start()
+
+    small_wide[...] = jnp.zeros_like(small_wide)
+    small_wide[:, 0:routes] = router_ref[...].astype(F32)
+    small_wide[:, 8:12] = cproj_ref[...].astype(F32)
+    small_wide[:, 12:14] = cvec_ref[...].astype(F32)
+    turned = small_wide[...].T[:SMALL, :]
+    which = lax.broadcasted_iota(jnp.int32, (SMALL, span), 0)
+    turned = jnp.where(which == 14, gain_a_ref[...].astype(F32), turned)
+    turned = jnp.where(which == 15, gain_m_ref[...].astype(F32), turned)
+    small_send[...] = turned.astype(BF16)
+    small_all[:, band] = turned.astype(BF16)
+    small_copy.start()
+    out_copy.start()
+    for m in range(2):
+        ctl_wide[...] = jnp.zeros_like(ctl_wide)
+        ctl_wide[:, 0:routes] = prev_ref[m]
+        ctl_wide[:, 8:10] = route_ref[m].astype(F32)
+        ctl_send[m] = ctl_wide[...].T[:SMALL, :]
+    send(2)
+    seg_copy.wait_recv()
+    seg_own.wait()
+    seg_row = seg_all[y, pl.ds(x, 1), :].astype(F32)
+    length = seg_row.shape[1]
+    segr_ref[...] = jnp.broadcast_to(seg_row, segr_ref.shape)
+    segc_ref[...] = jnp.broadcast_to(seg_row, (LANES, length)).T
+    small_copy.wait_recv()
+    for copy in weight_copies:
+        copy.wait_recv()
+    for copy in own_copies:
+        copy.wait()
+    gain = small_all[14:15, :].astype(F32)
+
+    def project(index):
+        here = block_of(index)
+        values = x_all[here, :].astype(F32)
+        inverse = lax.rsqrt(jnp.mean(values * values, axis=-1, keepdims=True) + NORM_EPS)
+        normed = (values * inverse * gain).astype(BF16)
+        normed_ref[here, :] = normed
+        qkv_ref[here, :] = dot(normed, wqkv_all[...]).astype(BF16)
+
+    forward = []
+    for step in range(2):
+        spot = x_all.at[block_of(core * 2 + (x if step == 0 else 1 - x))]
+        forward.append(inner.copy(spot, spot, sibling))
+    take_near(0)
+    forward[0].start()
+    project(core * 2 + x)
+    far_copies[0].wait_recv()
+    forward[1].start()
+    send(1)
+    project(core * 2 + 1 - x)
+    forward[0].wait_recv()
+    project((1 - core) * 2 + x)
+    forward[1].wait_recv()
+    project((1 - core) * 2 + 1 - x)
+
+    @pl.loop(0, span // LANES)
+    def _(pair):
+        attend_pair(pair, rows, reach, span, qkv_ref, segc_ref, segr_ref, att_ref, lse_ref)
+
+    for k in (1, 2):
+        take_near(k)
+        far_copies[k].wait_recv()
+    out_copy.wait_recv()
+    for copy in far_copies + weight_copies + forward + [out_copy, seg_copy, small_copy]:
+        copy.wait_send()
+
+    @pl.when(moved)
+    def _():
+        for copy in near_copies:
+            copy.wait_send()
+
+
+def gather_all(
+    tokens, cotangent, w_qkv, w_out, prev_logits, routes, segments, w_router, const_proj,
+    const_vec, gain_attn, gain_moe,
+):
+    rows, width = tokens.shape[1:]
+    length = segments.shape[1]
+    mine = length // 2
+    span = width // 2
+    vmem = pl.BlockSpec(memory_space=pltpu.VMEM)
+    anywhere = pl.BlockSpec(memory_space=pl.ANY)
+    return pl.pallas_call(
+        functools.partial(gather_kernel, rows, length // 2, w_router.shape[1]),
+        in_specs=[anywhere] * 4 + [vmem] * 8,
+        out_specs=[vmem] * 12,
+        out_shape=[
+            shape((length, width), BF16), shape((mine, width), BF16),
+            shape((2, SMALL, rows), F32), shape((length, width), BF16),
+            shape((length, 3 * span), BF16), shape((length, span), BF16),
+            shape((span // LANES, 8, length), F32), shape((SMALL, width), BF16),
+            shape((width, 3 * span), BF16), shape((span, width), BF16),
+            shape((length, LANES), F32), shape((8, length), F32),
+        ],
+        scratch_shapes=[
+            pltpu.VMEM((rows, LANES), F32), pltpu.VMEM((2, SMALL, rows), F32),
+            pltpu.VMEM((span, LANES), F32), pltpu.VMEM((SMALL, span), BF16),
+            pltpu.VMEM((2, 2, length), jnp.int32),
+        ]
+        + [pltpu.SemaphoreType.DMA((3,))] * 4
+        + [pltpu.SemaphoreType.DMA((8,))] * 2
+        + [pltpu.SemaphoreType.DMA((7,))],
+        compiler_params=pltpu.CompilerParams(
+            collective_id=3, has_side_effects=True, vmem_limit_bytes=60 * 1024 * 1024
+        ),
+        name="gather_all",
+    )(
+        tokens, cotangent, w_qkv, w_out, prev_logits, routes, segments, w_router, const_proj,
+        const_vec, gain_attn[None], gain_moe[None],
+    )
+
+
+def widen(turned):
+    pad = jnp.zeros((LANES - turned.shape[0], turned.shape[1]), turned.dtype)
+    return jnp.concatenate([turned, pad], axis=0).T
+
+
 def spread_block(experts, routes, rows, block, refs, send_ref, recv_ref, keep):
-    (att_own, att_sib, x_ref, g_ref, ctl_ref, w_own, w_sib, gain_ref, wsm_ref) = refs
+    att_own, att_sib, x_ref, g_ref, ctl_ref, w_own, w_sib, small_rows, wide_rows = refs
     residual_ref, mixed_ref, pm_ref, place_ref = keep
     y, x, z, core = position()
     here = pl.ds(pl.multiple_of(block * rows, rows), rows)
-    residual = x_ref[here, :].astype(F32) + (
+    tokens = x_ref[pl.ds(pl.multiple_of((core * 2 + block) * rows, rows), rows), :]
+    residual = tokens.astype(F32) + (
         dot(att_own[here, :], w_own[...]) + dot(att_sib[here, :], w_sib[...])
     )
     residual_ref[here, :] = residual
     inverse = lax.rsqrt(jnp.mean(residual * residual, axis=-1, keepdims=True) + NORM_EPS)
-    mixed = (residual * inverse * gain_ref[...]).astype(BF16)
+    mixed = (residual * inverse * small_rows[15:16, :].astype(F32)).astype(BF16)
     mixed_ref[here, :] = mixed
-    logits = dot(mixed, wsm_ref[...])
-    ctl = ctl_ref[here, :]
+    logits = dot(mixed, wide_rows[...], ((1,), (1,)))
+    ctl = widen(ctl_ref[block])
     lane = lax.broadcasted_iota(jnp.int32, (rows, LANES), 1)
     is_route = lane < routes
     router = jnp.where(is_route, logits + ctl, NEG)
@@ -922,7 +1119,7 @@
 
 
 def combine_block(experts, routes, rows, block, refs, keep, back_ref, outs, small_ref):
-    g_ref, ctl_ref, gain_ref, turned_ref, cvec_ref = refs
+    g_ref, ctl_ref, small_rows, wide_rows = refs
     residual_ref, mixed_ref, pm_ref, place_ref = keep
     out_ref, prev_ref, dres_ref, branch_ref = outs
     halves = back_ref.shape[1] // experts
@@ -933,7 +1130,7 @@
     residual = residual_ref[here, :]
     pm = pm_ref[here, :]
     lane = lax.broadcasted_iota(jnp.int32, (rows, LANES), 1)
-    chosen = chosen_of(ctl_ref[here, :])
+    chosen = chosen_of(widen(ctl_ref[block]))
     probs = jnp.where(lane < routes, pm, 0.0)
     gated = chosen * probs
     d_probs = jnp.zeros((rows, LANES), F32)
@@ -952,7 +1149,7 @@
         d_gate = jnp.sum(expert_out * grads, axis=-1, keepdims=True)
         d_probs = jnp.where(lane == expert, d_gate, d_probs)
     g_mixed = jnp.sum(grads * mixed, axis=-1, keepdims=True)
-    g_const = dot(g_low, cvec_ref[...], ((1,), (1,)))
+    g_const = dot(g_low, wide_rows[...], ((1,), (1,)))
     copy = experts + 1
     d_probs = jnp.where(lane == copy, g_mixed, d_probs)
     weight = column(gated, copy)
@@ -962,10 +1159,10 @@
         first = column(pm, 8 + 2 * const_index)
         second = column(pm, 9 + 2 * const_index)
         gate = column(gated, route)
-        g_vec = column(g_const, const_index)
+        g_vec = column(g_const, 12 + const_index)
         d_probs = jnp.where(lane == route, first * g_mixed + second * g_vec, d_probs)
         weight = weight + gate * first
-        vec = cvec_ref[const_index : const_index + 1, :].astype(F32)
+        vec = small_rows[12 + const_index : 13 + const_index, :].astype(F32)
         result = result + (gate * second) * vec
         d_first = gate * g_mixed
         d_second = gate * g_vec
@@ -980,10 +1177,10 @@
     d_small = jnp.where(lane < routes, d_logits, d_small)
     d_mixed = d_mixed + weight * grads
     d_mixed = d_mixed + dot(
-        jnp.where(lane < 12, d_small, 0.0), turned_ref[...], precision=HIGHEST
+        jnp.where(lane < 12, d_small, 0.0), wide_rows[...].astype(F32), precision=HIGHEST
     )
     inverse = lax.rsqrt(jnp.mean(residual * residual, axis=-1, keepdims=True) + NORM_EPS)
-    scaled = d_mixed * gain_ref[...]
+    scaled = d_mixed * small_rows[15:16, :].astype(F32)
     mean = jnp.mean(scaled * residual, axis=-1, keepdims=True)
     d_residual = grads + inverse * scaled - residual * (inverse * inverse * inverse * mean)
     dres_ref[here, :] = d_residual
@@ -1002,10 +1199,9 @@
 
 def layer_kernel(
     experts, routes, rows, blocks,
-    att_ref, x_ref, g_ref, ctl_ref, w_own, w_sib, gain_ref, wsm_ref, turned_ref, cvec_ref,
-    gate_ref, up_ref, down_ref,
+    att_ref, x_ref, g_ref, ctl_ref, w_own, w_sib, small_rows, gate_ref, up_ref, down_ref,
     out_ref, prev_ref, dres_ref, branch_ref, small_ref, dgate_out, dup_out, ddown_out,
-    att_own, att_sib, gate_w, up_w, down_w, residual_ref, mixed_ref, pm_ref, place_ref,
+    wide_rows, att_own, att_sib, gate_w, up_w, down_w, residual_ref, mixed_ref, pm_ref, place_ref,
     send_ref, recv_ref, result_ref, back_ref, hidden_ref, d_gate_ref, d_up_ref,
     head_send, head_recv, local_sems, send_sems, recv_sems, back_send, back_recv,
 ):
@@ -1049,11 +1245,13 @@
         )
 
     small_ref[...] = jnp.zeros_like(small_ref)
+    wide_rows[...] = jnp.zeros_like(wide_rows)
+    wide_rows[0:SMALL, :] = small_rows[...]
     heads[0].wait_recv()
     locals_[0].wait()
     keep = (residual_ref, mixed_ref, pm_ref, place_ref)
     spread_refs = (
-        att_own, att_sib, x_ref, g_ref, ctl_ref, w_own, w_sib, gain_ref, wsm_ref
+        att_own, att_sib, x_ref, g_ref, ctl_ref, w_own, w_sib, small_rows, wide_rows
     )
 
     @pl.loop(0, blocks)
@@ -1101,7 +1299,7 @@
         for k in range(3):
             giveback(block, k).wait_recv()
         combine_block(
-            experts, routes, rows, block, (g_ref, ctl_ref, gain_ref, turned_ref, cvec_ref),
+            experts, routes, rows, block, (g_ref, ctl_ref, small_rows, wide_rows),
             keep, back_ref, (out_ref, prev_ref, dres_ref, branch_ref), small_ref,
         )
 
@@ -1114,10 +1312,10 @@
 
 
 def expert_layer(
-    experts, routes, rows, attended, x_own, cot_own, ctl, w_own, w_sib, gain, wsm, turned,
-    cvec, w_gate, w_up, w_down,
+    experts, routes, rows, attended, x_all, cot_own, ctl, w_own, w_sib, small_all, w_gate,
+    w_up, w_down,
 ):
-    mine, width = x_own.shape
+    mine, width = cot_own.shape
     blocks = mine // rows
     peers = lax.axis_size("ep")
     span = attended.shape[1]
@@ -1127,14 +1325,15 @@
     grads = [(2 * w.shape[0], w.shape[1]) for w in (w_gate, w_up, w_down)]
     return pl.pallas_call(
         functools.partial(layer_kernel, experts, routes, rows, blocks),
-        in_specs=[vmem] * 13,
+        in_specs=[vmem] * 10,
         out_specs=[vmem] * 8,
         out_shape=[
             shape((blocks, rows, width), BF16), shape((blocks, 8, rows), F32),
             shape((mine, width), F32), shape((mine, width), BF16), shape((SMALL, width), F32),
         ]
         + [shape(dims, BF16) for dims in grads],
-        scratch_shapes=[pltpu.VMEM((mine, span), BF16)] * 2
+        scratch_shapes=[pltpu.VMEM((LANES, width), BF16)]
+        + [pltpu.VMEM((mine, span), BF16)] * 2
         + [pltpu.VMEM(dims, BF16) for dims in grads]
         + [
             pltpu.VMEM((mine, width), F32), pltpu.VMEM((mine, width), BF16),
@@ -1153,8 +1352,8 @@
         ),
         name="expert_layer",
     )(
-        attended.reshape(2, mine, span), x_own, cot_own, ctl, w_own, w_sib, gain, wsm,
-        turned, cvec, w_gate, w_up, w_down,
+        attended.reshape(2, mine, span), x_all, cot_own, ctl, w_own, w_sib, small_all,
+        w_gate, w_up, w_down,
     )
 
 
@@ -1176,23 +1375,13 @@
     w_down,
 ):
     rows, width = tokens.shape[1:]
-    peers = lax.axis_size("ep")
-    place = lax.axis_index("ep")
     core = lax.axis_index("fs")
-    cross = place % 2
     route_count = w_router.shape[1]
     experts = route_count - 4
-    capacity = LANES
-    length = rows * peers
+    length = segments.shape[1]
     mine = length // 2
     span = width // 2
-    hidden_width = w_gate.shape[2]
-    pairs = [[], []]
-    for flip in range(2):
-        for source in range(peers):
-            for side in range(2):
-                target = side * 2 + ((source % 2) ^ flip)
-                pairs[flip].append((source * 2 + side, target * 2 + source // 2))
+    blocks = mine // rows
 
     def swap(array):
         return lax.ppermute(array, "fs", [(0, 1), (1, 0)])
@@ -1204,52 +1393,13 @@
             jnp.concatenate([other, own], axis=axis),
         )
 
-    def to_chip(array):
-        near = lax.ppermute(
-            lax.dynamic_index_in_dim(array, cross, 0, False), ("ep", "fs"), pairs[0]
-        )
-        far = lax.ppermute(
-            lax.dynamic_index_in_dim(array, 1 - cross, 0, False), ("ep", "fs"), pairs[1]
-        )
-        return jnp.where(
-            cross == 0, jnp.concatenate([near, far]), jnp.concatenate([far, near])
-        )
-
-    x_own = to_chip(tokens)
-    x_sib = swap(x_own)
-    qkv_split = w_qkv.reshape(span, 3, 2, span)
-    qkv_mine = lax.dynamic_index_in_dim(qkv_split, core, 2, False).reshape(span, 3 * span)
-    qkv_sent = lax.dynamic_index_in_dim(qkv_split, 1 - core, 2, False).reshape(span, 3 * span)
-    qkv_weight = by_core(qkv_mine, swap(qkv_sent))
-    out_sib = swap(w_out)
-    pad = jnp.zeros((span, 8 - route_count), BF16)
-    small_own = jnp.concatenate(
-        [w_router, pad, const_proj, const_vec, gain_attn[:, None], gain_moe[:, None]], axis=1
-    )
-    small_all = by_core(small_own, swap(small_own))
-    small_turned = small_all.T.astype(F32)
-    attn_gain = small_turned[14:15]
-    moe_gain = small_turned[15:16]
-    wsm = jnp.pad(small_all[:, :12], ((0, 0), (0, LANES - 12)))
-    turned = jnp.pad(small_turned[:12], ((0, LANES - 12), (0, 0)))
-    cvec_turned = jnp.pad(small_all[:, 12:14].T, ((0, LANES - 2), (0, 0)))
-    seg_sib = swap(segments)
-    seg_pair = by_core(segments[None], seg_sib[None])
-    seg_row = seg_pair.reshape(4, length)[place][None, :]
-    seg_col = seg_row.reshape(length, 1)
-
-    x_all = by_core(x_own, x_sib)
-    normed, qkv = pl.pallas_call(
-        norm_qkv_kernel,
-        grid=(length // rows,),
-        in_specs=[per_row(rows, width), whole((1, width)), whole((width, 3 * span))],
-        out_specs=[per_row(rows, width), per_row(rows, 3 * span)],
-        out_shape=[shape((length, width), BF16), shape((length, 3 * span), BF16)],
-        compiler_params=params(),
-        cost_estimate=cost(2 * length * width * 3 * span, 6e6),
-        name="norm_qkv",
-    )(x_all, attn_gain, qkv_weight)
-
+    (
+        x_all, cot_own, ctl, normed, qkv, attended, lse, small_all, qkv_weight, out_sib,
+        seg_col, seg_row,
+    ) = gather_all(
+        tokens, cotangent, w_qkv, w_out, prev_logits, routes, segments, w_router, const_proj,
+        const_vec, gain_attn, gain_moe,
+    )
     head_pairs = span // LANES
     reach = length // 2
 
@@ -1257,40 +1407,17 @@
         return pl.BlockSpec((length, LANES), lambda p: (0, offset + p))
 
     lse_spec = pl.BlockSpec((1, 8, length), lambda p: (p, 0, 0))
-    attended, lse = pl.pallas_call(
-        functools.partial(attend_kernel, rows, reach),
-        grid=(head_pairs,),
-        in_specs=[
-            heads_at(0), heads_at(head_pairs), heads_at(2 * head_pairs),
-            whole((length, 1)), whole((1, length)),
-        ],
-        out_specs=[heads_at(0), lse_spec],
-        out_shape=[shape((length, span), BF16), shape((head_pairs, 8, length), F32)],
-        compiler_params=params(),
-        cost_estimate=cost(12e9, 4e6),
-        name="attend",
-    )(qkv, qkv, qkv, seg_col, seg_row)
-
-    cot_own = to_chip(cotangent)
-    ctl = jnp.concatenate(
-        [
-            prev_logits,
-            jnp.zeros(prev_logits.shape[:2] + (8 - route_count,), F32),
-            routes.astype(F32),
-        ],
-        axis=2,
-    )
-    ctl = jnp.pad(to_chip(ctl), ((0, 0), (0, LANES - 10)))
-    blocks = mine // rows
+    attn_gain = small_all[14:15].astype(F32)
+    x_own = lax.dynamic_slice_in_dim(x_all, core * mine, mine)
     (
         block_out, d_prev, d_residual, d_branch, small, grad_gate, grad_up, grad_down,
     ) = expert_layer(
-        experts, route_count, rows, attended, x_own, cot_own, ctl, w_out, out_sib, moe_gain,
-        wsm, turned, cvec_turned, w_gate[0], w_up[0], w_down[0],
+        experts, route_count, rows, attended, x_all, cot_own, ctl, w_out, out_sib, small_all,
+        w_gate[0], w_up[0], w_down[0],
     )
 
     branch_all = by_core(d_branch, swap(d_branch))
-    valid = (seg_col != SEGS - 1).astype(F32)
+    valid = (seg_col[:, :1] != SEGS - 1.0).astype(F32)
     d_att = (dot(branch_all, w_out, ((1,), (1,))) * valid).astype(BF16)
     grad_out = dot(attended, branch_all, ((0,), (0,))).astype(BF16)
     d_queries, d_keys, d_values = pl.pallas_call(
@@ -1298,7 +1425,7 @@
         grid=(head_pairs,),
         in_specs=[
             heads_at(0), heads_at(head_pairs), heads_at(2 * head_pairs), heads_at(0),
-            whole((length, 1)), whole((1, length)), lse_spec,
+            whole((length, LANES)), whole((8, length)), lse_spec,
         ],
         out_specs=[heads_at(0)] * 3,
         out_shape=[shape((length, span), BF16)] * 3,

time: 277 us -> 252 us (0.910)
  starting transfers between devices: 16.3 us -> 0.82 us
  Pallas kernels: 189 us -> 204 us
  other arithmetic: 19.6 us -> 7.8 us
  waiting for transfers between devices: 9.03 us -> 0.01 us
  local copies, waits for them, and re-layouts: 32 us -> 26.9 us
    pallas_call x2 -> x1, Pallas kernels: 19 us -> 33 us  [gather_all(): pl.pallas_call(functools.partial(gather_kernel, rows, length // 2, w_rout...]
    ppermute x6 -> x0, starting transfers between devices: 13 us -> none  [the longest x3 8.1 us: to_chip(): lax.ppermute(lax.dynamic_index_in_dim(array, cross, 0, False), ('ep', 'fs...]
    ppermute x6 -> x0, waiting for transfers between devices: 7.34 us -> none  [the longest x3 7.33 us: to_chip(): lax.ppermute(lax.dynamic_index_in_dim(array, 1 - cross, 0, False), ('ep',...]
    select_n x6 -> x3, other arithmetic: 7.94 us -> 0.86 us  [by_core(): jnp.where(core == 0, jnp.concatenate([own, other], axis=axis), jnp.concat...]
    unnamed x48 -> x44, local copies, waits for them, and re-layouts: 13.1 us -> 17.7 us
    select_n x3 -> x0, other arithmetic: 3.79 us -> none  [to_chip(): jnp.where(cross == 0, jnp.concatenate([near, far]), jnp.concatenate([far,...]
    squeeze x3 -> x0, local copies, waits for them, and re-layouts: 3.58 us -> none  [to_chip(): lax.dynamic_index_in_dim(array, cross, 0, False)]
    pad x4 -> x0, local copies, waits for them, and re-layouts: 2.9 us -> none  [the longest x1 0.77 us: one_chip(): turned = jnp.pad(small_turned[:12], ((0, LANES - 12), (0, 0)))]
  transfers between devices with their start and end apart: 14 -> 3, of which waited for: 3 -> 0; matrix products, arithmetic and copies ran while one was open for 14% -> 6% of each run, Pallas kernels for 13% -> 6%
where the time goes in v1:
time: 252 us; the launch traced here: 251 us
  Pallas kernels  204 us (81%)
  local copies, waits for them, and re-layouts  26.9 us (11%)
  matrix products  10.1 us (4%)
  other arithmetic  7.8 us (3%)
    pallas_call x1, Pallas kernels, expert_layer(): pl.pallas_call(functools.partial(layer_kernel, experts, routes, rows, blo...  87.4 us
    pallas_call x1, Pallas kernels, reduce_all(): pl.pallas_call(functools.partial(reduce_kernel, depth, cut), in_specs=[vm...  64.6 us
    pallas_call x1, Pallas kernels, gather_all(): pl.pallas_call(functools.partial(gather_kernel, rows, length // 2, w_rout...  33 us
    unnamed x44, local copies, waits for them, and re-layouts  17.7 us
    pallas_call x1, Pallas kernels, one_chip(): pl.pallas_call(functools.partial(attend_back_kernel, rows, reach), grid=(...  16 us
    dot_general x4, matrix products, dot(): lax.dot_general(lhs, rhs, (dims, ((), ())), precision=precision, preferre...  10.1 us
  transfers between devices with their start and end apart: 3, of which 0 were waited for; matrix products, arithmetic and copies ran while one was open for 6% of the time, Pallas kernels for 6%

profile of v1, /device:TPU:0, one launch (start us, length us, event | category | flops | bytes accessed | tf_op | source)
XLA Modules:
  0.0 250.8 jit_solution(12327596352348878766)
XLA Ops:
  0.6 1.2 broadcast_in_dim.6.gain_a_ref
  1.9 1.2 broadcast_in_dim.7.gain_m_ref
  3.1 1.5 copy.40.router_ref
  4.6 1.5 copy.41.cproj_ref
  6.1 1.5 copy.42.cvec_ref
  7.6 1.6 copy.38.prev_ref
  9.1 1.5 copy.39.route_ref
  10.7 33.0 %gather_all.1 = (bf16[1024,768]{1,0:T(8,128)(2,1)}, bf16[512,768]{1,0:T(8,128)(2,1)}, f32[2,16,256]{2,1,0:T(8,128)}, bf16[1024,768]{1,0:T(8,128)(2,1)}, bf16[102...) custom-call(bf16[2,256,768]{2,1,0:T(8,128)(2,1)} %tok_ref.1, ...), custom_call_target="tpu_custom_call" | custom-call | tf_op jit(solution)/shard_map/gather_all/pallas_call | solution.py:1007
  43.7 87.4 %expert_layer.1 = (bf16[2,256,768]{2,1,0:T(8,128)(2,1)}, f32[2,8,256]{2,1,0:T(8,128)}, f32[512,768]{1,0:T(8,128)}, bf16[512,768]{1,0:T(8,128)(2,1)}, f32[16,768]...) custom-call(bf16[2,512,384]{2,1,0:T(8,128)(2,1)} %bitcast.27, ...), custom_call_target="tpu_custom_call" | custom-call | tf_op jit(solution)/shard_map/expert_layer/pallas_call | solution.py:1326
  131.3 0.9 slice.100
  132.2 0.9 constant_dynamic-slice_fusion.1.x_ref
  133.3 1.3 slice_convert_fusion.2.gain_ref
  134.6 2.3 convolution_convert_fusion.1
  137.4 3.3 %multiply_convert_fusion.do_ref = bf16[1024,384]{1,0:T(8,128)(2,1)} fusion(bf16[384,768]{1,0:T(8,128)(2,1)S(1)} %copy-done.1, f32[1024]{0:T(1024)S(1)} %convert_reduce_fusion, bf16[512,768]{1,0:T(8,128)(2,1)} %collective-permute-done, bf16[512,768]{1,0:T(8,128)(2,1)S(1)} %copy-done.13, pred[]{:T(512)S(6)} %eq.2), kind=kOutput, calls=%fused_computation.6 | convolution fusion | flops 611844096 | bytes 2953217 | tf_op jit(solution)/shard_map/dot_general | solution.py:406
  140.6 16.0 %attend_back.1 = (bf16[1024,384]{1,0:T(8,128)(2,1)}, bf16[1024,384]{1,0:T(8,128)(2,1)}, bf16[1024,384]{1,0:T(8,128)(2,1)}) custom-call(bf16[1024,1152]{1,0:T(8,128)(2,1)} %get-tuple-element.56.q_ref.k_ref.v_ref, bf16[1024,1152]{1,0:T(8,128)(2,1)} %get-tuple-element.56.q_ref.k_ref.v_ref, bf16[1024,1152]{1,0:T(8,128)(2,1)} %get-tuple-element.56.q_ref.k_ref.v_ref, ...), custom_call_target="tpu_custom_call" | custom-call | flops 30000001024 | bytes 5000000 | tf_op jit(solution)/shard_map/attend_back/pallas_call | solution.py:1423
  156.6 1.3 constant_dynamic-update-slice_fusion.2
  158.4 1.1 copy-done.11
  159.5 2.2 fusion.6
  162.1 2.3 convolution_convert_fusion
  164.4 1.3 constant_dynamic-slice_fusion.own_ref
  165.8 0.9 copy-done.3
  166.7 3.5 %finish.1 = (bf16[512,768]{1,0:T(8,128)(2,1)}, f32[8,768]{1,0:T(8,128)}) custom-call(bf16[512,768]{1,0:T(8,128)(2,1)} %constant_dynamic-slice_fusion.1.x_ref, f32[512,768]{1,0:T(8,128)} %constant_dynamic-slice_fusion.own_ref, bf16[512,768]{1,0:T(8,128)(2,1)} %copy-done.3, f32[512,768]{1,0:T(8,128)} %get-tuple-element.66.dres_ref, ...), custom_call_target="tpu_custom_call" | custom-call | flops 100000000 | bytes 6000000 | tf_op jit(solution)/shard_map/finish/pallas_call | solution.py:1444
  171.1 1.7 fusion.1
  172.8 64.6 %reduce_all.1 = (f32[1,96,1024]{2,1,0:T(8,128)}, f32[1,96,1024]{2,1,0:T(8,128)}, f32[1,128,768]{2,1,0:T(8,128)}, f32[24,1664]{1,0:T(8,128)}, f32[24,1664]{1,0:T(...) custom-call(bf16[4,2,96,1024]{3,2,1,0:T(8,128)(2,1)} %bitcast.21, ...), custom_call_target="tpu_custom_call" | custom-call | tf_op jit(solution)/shard_map/reduce_all/pallas_call | solution.py:775
  237.4 0.8 fusion.4
  239.0 0.8 fusion.5
  242.6 1.3 copy.44
  243.9 2.4 convert_element_type.31
  247.7 0.9 copy.55
  248.6 0.7 copy.56
  249.3 0.7 copy.57
  250.1 0.7 copy.58
  (51 shorter events, 7.6 us)
Async XLA Ops:
  43.7 88.5 %copy-start = (bf16[1024,768]{1,0:T(8,128)(2,1)S(1)}, bf16[1024,768]{1,0:T(8,128)(2,1)}, u32[]{:S(2)}) copy-start(bf16[1024,768]{1,0:T(8,128)(2,1)} %get-tuple-element.47.x_ref) | copy-start | bytes 4718596
  131.1 2.1 copy-start.7
  131.1 3.5 %copy-start.2 = (bf16[1024,384]{1,0:T(8,128)(2,1)S(1)}, bf16[1024,384]{1,0:T(8,128)(2,1)}, u32[]{:S(2)}) copy-start(bf16[1024,384]{1,0:T(8,128)(2,1)} %get-tuple-element.46) | copy-start | bytes 2359300
  131.1 3.5 %collective-permute-start = (bf16[512,768]{1,0:T(8,128)(2,1)}, bf16[512,768]{1,0:T(8,128)(2,1)}, u32[]{:S(2)}, u32[]{:S(2)}) collective-permute-start(bf16[512,768]{1,0:T(8,128)(2,1)} %get-tuple-element.57), channel_id=1, source_target_pairs={{0,1},{1,0},{2,3},{3,2},{4,5},{5,4},{6,7},{7,6},{8,9},{9,8},{10,11... | collective-permute-start | bytes 2359304 | tf_op jit(solution)/shard_map/ppermute | solution.py:1387
  132.2 2.4 copy-start.13
  134.6 2.8 %copy-start.1 = (bf16[384,768]{1,0:T(8,128)(2,1)S(1)}, bf16[384,768]{1,0:T(8,128)(2,1)}, u32[]{:S(2)}) copy-start(bf16[384,768]{1,0:T(8,128)(2,1)} %w_own.1) | copy-start | bytes 1769476
  137.0 28.6 %collective-permute-start.1 = (bf16[384,384]{1,0:T(8,128)(2,1)S(1)}, bf16[384,384]{1,0:T(8,128)(2,1)S(1)}, u32[]{:S(2)}, u32[]{:S(2)}) collective-permute-start(bf16[384,384]{1,0:T(8,128)(2,1)S(1)} %get-tuple-element.108), channel_id=1, source_target_pairs={{0,1},{1,0},{2,3},{3,2},{4,5},{5,4},{6,7},{7,6},{8,9},{9,8},{10,11... | collective-permute-start | bytes 884744 | tf_op jit(solution)/shard_map/ppermute | solution.py:1387
  156.6 1.4 copy-start.6
  156.6 1.6 copy-start.5
  157.9 1.5 copy-start.11
  159.5 2.6 %copy-start.12 = (bf16[1024,768]{1,0:T(8,128)(2,1)S(1)}, bf16[1024,768]{1,0:T(8,128)(2,1)}, u32[]{:S(2)}) copy-start(bf16[1024,768]{1,0:T(8,128)(2,1)} %get-tuple-element.55) | copy-start | bytes 4718596
  161.8 4.0 %collective-permute-start.2 = (bf16[512,768]{1,0:T(8,128)(2,1)S(1)}, bf16[512,768]{1,0:T(8,128)(2,1)S(1)}, u32[]{:S(2)}, u32[]{:S(2)}) collective-permute-start(bf16[512,768]{1,0:T(8,128)(2,1)S(1)} %dynamic-slice_convert_fusion), channel_id=1, source_target_pairs={{0,1},{1,0},{2,3},{3,2},{4,5},{5,4},{6,7},{7,6},{8,9},{9,8},{10,11... | collective-permute-start | bytes 2359304 | tf_op jit(solution)/shard_map/ppermute | solution.py:1387
  165.8 0.9 copy-start.3
  240.6 7.1 %copy-start.4 = (bf16[2,256,768]{2,1,0:T(8,128)(2,1)S(1)}, bf16[2,256,768]{2,1,0:T(8,128)(2,1)}, u32[]{:S(2)}) copy-start(bf16[2,256,768]{2,1,0:T(8,128)(2,1)} %get-tuple-element.134) | copy-start | bytes 2359300
  246.3 2.3 copy-start.10
  246.3 3.0 %copy-start.9 = (f32[1,96,1024]{2,1,0:T(8,128)S(1)}, f32[1,96,1024]{2,1,0:T(8,128)}, u32[]{:S(2)}) copy-start(f32[1,96,1024]{2,1,0:T(8,128)} %get-tuple-element.145) | copy-start | bytes 1179652
  247.0 3.1 %copy-start.8 = (f32[1,128,768]{2,1,0:T(8,128)S(1)}, f32[1,128,768]{2,1,0:T(8,128)}, u32[]{:S(2)}) copy-start(f32[1,128,768]{2,1,0:T(8,128)} %get-tuple-element.146) | copy-start | bytes 1179652

commit v2 on v1

--- a/solution.py
+++ b/solution.py
@@ -413,47 +413,6 @@
     return start, (block + 1) * rows - start
 
 
-def attend_back_kernel(
-    rows, reach, q_ref, k_ref, v_ref, do_ref, segc_ref, segr_ref, lse_ref,
-    dq_ref, dk_ref, dv_ref, dk_sum, dv_sum,
-):
-    length = q_ref.shape[0]
-    dk_sum[...] = jnp.zeros_like(dk_sum)
-    dv_sum[...] = jnp.zeros_like(dv_sum)
-    keys_turned = k_ref[...].T
-    for block in range(length // rows):
-        start, width = key_span(block, rows, reach)
-        queries = q_ref[block * rows : (block + 1) * rows, :]
-        grads = do_ref[block * rows : (block + 1) * rows, :]
-        keys = k_ref[start : start + width, :]
-        values = v_ref[start : start + width, :]
-        seg_k = segc_ref[start : start + width, 0:1]
-        seg_q = segr_ref[0:1, block * rows : (block + 1) * rows]
-        key_pos = start + lax.broadcasted_iota(jnp.int32, (width, rows), 0)
-        query_pos = block * rows + lax.broadcasted_iota(jnp.int32, (width, rows), 1)
-        allowed = (seg_q == seg_k) & (key_pos <= query_pos)
-        lane = lax.broadcasted_iota(jnp.int32, (rows, LANES), 1)
-        dq_parts = []
-        for head in range(2):
-            mine = (lane // HEAD) == head
-            head_q = jnp.where(mine, queries, 0)
-            head_g = jnp.where(mine, grads, 0)
-            log_total = lse_ref[0, head : head + 1, block * rows : (block + 1) * rows]
-            scores = dot(keys, head_q, ((1,), (1,))) * 0.125
-            probs = jnp.exp(jnp.where(allowed, scores, NEG) - log_total)
-            d_probs = dot(values, head_g, ((1,), (1,)))
-            delta = jnp.sum(probs * d_probs, axis=0, keepdims=True)
-            d_scores = (probs * (d_probs - delta)).astype(BF16)
-            dv_sum[start : start + width, :] += dot(probs.astype(BF16), head_g)
-            dk_sum[start : start + width, :] += dot(d_scores, head_q)
-            turned = keys_turned[head * HEAD : (head + 1) * HEAD, start : start + width]
-            dq_parts.append(dot(turned, d_scores))
-        dq = jnp.concatenate(dq_parts, axis=0).T * 0.125
-        dq_ref[block * rows : (block + 1) * rows, :] = dq.astype(BF16)
-    dk_ref[...] = (dk_sum[...] * 0.125).astype(BF16)
-    dv_ref[...] = dv_sum[...].astype(BF16)
-
-
 def column(rows, index):
     return rows[:, index : index + 1]
 
@@ -461,22 +420,6 @@
 def chosen_of(ctl):
     lane = lax.broadcasted_iota(jnp.int32, ctl.shape, 1).astype(F32)
     return ((lane == column(ctl, 8)) | (lane == column(ctl, 9))).astype(F32)
-
-
-def finish_kernel(x_ref, own_ref, sib_ref, dres_ref, gain_ref, out_ref, gain_out_ref):
-    rows = x_ref[...].astype(F32)
-    d_normed = own_ref[...].astype(F32) + sib_ref[...].astype(F32)
-    inverse = lax.rsqrt(jnp.mean(rows * rows, axis=-1, keepdims=True) + NORM_EPS)
-    scaled = d_normed * gain_ref[...]
-    mean = jnp.mean(scaled * rows, axis=-1, keepdims=True)
-    out = dres_ref[...] + inverse * scaled - rows * (inverse * inverse * inverse * mean)
-    out_ref[...] = out.astype(out_ref.dtype)
-
-    @pl.when(pl.program_id(0) == 0)
-    def _():
-        gain_out_ref[...] = jnp.zeros_like(gain_out_ref)
-
-    gain_out_ref[0:1, :] += jnp.sum(d_normed * rows * inverse, axis=0, keepdims=True)
 
 
 def shape(dims, dtype):
@@ -542,265 +485,6 @@
 
             total = total + jnp.where(present, 1, 0)
     pl.semaphore_wait(barrier, total)
-
-
-class Line:
-    def __init__(self, mail, depth, slots):
-        self.depth = depth
-        self.slots = slots
-        self.place = lax.axis_index("dp")
-        y, x, z, core = position()
-        self.copies = {}
-        for way in range(2):
-            step_to = 1 if way == 0 else -1
-            device = (y * 2 + x, z + step_to, core)
-            for step in range(depth - 1):
-                for item, (acc, landing) in enumerate(slots):
-                    shard = self.shard(way, step)
-                    safe = jnp.clip(shard, 0, depth - 1)
-                    self.copies[way, step, item] = mail.copy(
-                        acc.at[safe], landing.at[way, step], device
-                    )
-
-    def shard(self, way, step):
-        if way == 0:
-            return self.place + self.depth - 1 - step
-        return self.place - (self.depth - 1 - step)
-
-    def sends(self, way, step):
-        shard = self.shard(way, step)
-        if way == 0:
-            return (shard <= self.depth - 1) & (self.place < self.depth - 1)
-        return (shard >= 0) & (self.place > 0)
-
-    def gets(self, way, step):
-        if way == 0:
-            return (self.place > 0) & (self.shard(way, step + 1) <= self.depth - 1)
-        return (self.place < self.depth - 1) & (self.shard(way, step + 1) >= 0)
-
-    def send(self, step, item):
-        for way in range(2):
-
-            @pl.when(self.sends(way, step))
-            def _():
-                self.copies[way, step, item].start()
-
-    def take(self, step, item):
-        acc, landing = self.slots[item]
-        for way in range(2):
-            shard = jnp.clip(self.shard(way, step + 1), 0, self.depth - 1)
-
-            @pl.when(self.gets(way, step))
-            def _():
-                self.copies[way, step, item].wait_recv()
-                acc[shard] = (
-                    acc[shard].astype(F32) + landing[way, step].astype(F32)
-                ).astype(BF16)
-
-    def finish(self, item, store):
-        acc, landing = self.slots[item]
-        store(acc[self.place].astype(F32))
-        for way in range(2):
-
-            @pl.when(self.gets(way, self.depth - 2))
-            def _():
-                self.copies[way, self.depth - 2, item].wait_recv()
-                store(landing[way, self.depth - 2].astype(F32), True)
-
-    def close(self):
-        for (way, step, item), copy in self.copies.items():
-
-            @pl.when(self.sends(way, step))
-            def _():
-                copy.wait_send()
-
-
-def reduce_kernel(
-    depth, cut,
-    gate_ref, up_ref, down_ref, dense_ref, out_ref, dtok_ref, prev_ref,
-    gate_out, up_out, down_out, own_out, sib_out, out_home, dtok_home, prev_home,
-    gate_land, up_land, down_land, gate_acc, up_acc, down_acc,
-    gate_line, up_line, down_line,
-    y1_land, x1_land, y1_acc, x1_acc, x2_land, y2_land, dense_acc, dense_line, dense_sum,
-    send_sems, recv_sems, local_sems,
-):
-    y, x, z, core = position()
-    sibling = (y * 2 + x, z, 1 - core)
-    across = (y * 2 + 1 - x, z, core)
-    along = ((1 - y) * 2 + x, z, core)
-    moved = y != core
-    near = ((1 - y) * 2 + x, z, 1 - core)
-    far = (core * 2 + 1 - x, z, y)
-    greet(
-        [
-            (sibling, True), (across, True), (along, True),
-            (near, moved), (far, moved),
-            ((y * 2 + x, z + 1, core), z < depth - 1), ((y * 2 + x, z - 1, core), z > 0),
-        ]
-    )
-    mail = Mail(send_sems, recv_sems)
-    experts = [
-        (gate_ref, gate_land, gate_acc, gate_line, gate_out),
-        (up_ref, up_land, up_acc, up_line, up_out),
-        (down_ref, down_land, down_acc, down_line, down_out),
-    ]
-    halves = [
-        mail.copy(source.at[:, 1 - core], land, sibling)
-        for source, land, _, _, _ in experts
-    ]
-    line = Line(mail, depth, [(acc, landing) for _, _, acc, landing, _ in experts])
-    rest = dense_ref.shape[3] - cut
-    left = pl.ds(0, cut)
-    right = pl.ds(cut, rest)
-    first_y = mail.copy(dense_ref.at[1 - y, :, :, left], y1_land, along)
-    first_x = mail.copy(dense_ref.at[:, 1 - x, :, right], x1_land, across)
-    second_x = mail.copy(y1_acc.at[1 - x], x2_land, across)
-    second_y = mail.copy(x1_acc.at[1 - y], y2_land, along)
-    dense = Line(mail, depth, [(dense_acc, dense_line)])
-    homes = [(out_ref, out_home), (dtok_ref, dtok_home), (prev_ref, prev_home)]
-    nears = [mail.copy(a.at[x], b.at[x], near) for a, b in homes]
-    fars = [mail.copy(a.at[1 - x], b.at[x], far) for a, b in homes]
-    stays = [
-        pltpu.make_async_copy(a.at[x], b.at[x], local_sems.at[k])
-        for k, (a, b) in enumerate(homes)
-    ]
-
-    for copy in halves:
-        copy.start()
-    first_y.start()
-    first_x.start()
-    for item, (source, land, acc, _, _) in enumerate(experts):
-        halves[item].wait_recv()
-        for shard in range(depth):
-            acc[shard] = (source[shard, core].astype(F32) + land[shard].astype(F32)).astype(BF16)
-        line.send(0, item)
-    first_y.wait_recv()
-    for k in range(2):
-        y1_acc[k] = (dense_ref[y, k, :, left].astype(F32) + y1_land[k].astype(F32)).astype(BF16)
-    second_x.start()
-    first_x.wait_recv()
-    for k in range(2):
-        x1_acc[k] = (dense_ref[k, x, :, right].astype(F32) + x1_land[k].astype(F32)).astype(BF16)
-    second_y.start()
-    for copy in fars:
-        copy.start()
-
-    @pl.when(moved)
-    def _():
-        for copy in nears:
-            copy.start()
-
-    @pl.when(jnp.logical_not(moved))
-    def _():
-        for copy in stays:
-            copy.start()
-
-    for item in range(3):
-        line.take(0, item)
-        line.send(1, item)
-    size = dense_acc.shape[1]
-    second_x.wait_recv()
-    second_y.wait_recv()
-    for shard in range(depth):
-        part = pl.ds(shard * size, size)
-        dense_acc[shard, :, left] = (
-            y1_acc[x, part].astype(F32) + x2_land[part].astype(F32)
-        ).astype(BF16)
-        dense_acc[shard, :, right] = (
-            x1_acc[y, part].astype(F32) + y2_land[part].astype(F32)
-        ).astype(BF16)
-    dense.send(0, 0)
-    for item in range(3):
-        line.take(1, item)
-        line.send(2, item)
-    dense.take(0, 0)
-    dense.send(1, 0)
-    for item, (_, _, _, _, result) in enumerate(experts):
-
-        def store(value, add=False):
-            result[0] = result[0] + value if add else value
-
-        line.finish(item, store)
-    dense.take(1, 0)
-    dense.send(2, 0)
-
-    def store_dense(value, add=False):
-        dense_sum[...] = dense_sum[...] + value if add else value
-
-    dense.finish(0, store_dense)
-    half = size // 2
-    last = mail.copy(
-        dense_sum.at[pl.ds(pl.multiple_of((1 - core) * half, 8), half)], sib_out, sibling
-    )
-    last.start()
-    own_out[...] = dense_sum[pl.ds(pl.multiple_of(core * half, 8), half), :]
-    last.wait()
-    for copy in halves + [first_y, first_x, second_x, second_y]:
-        copy.wait_send()
-    line.close()
-    dense.close()
-    for copy in fars:
-        copy.wait()
-
-    @pl.when(moved)
-    def _():
-        for copy in nears:
-            copy.wait()
-
-    @pl.when(jnp.logical_not(moved))
-    def _():
-        for copy in stays:
-            copy.wait()
-
-
-def reduce_all(grad_gate, grad_up, grad_down, dense, block_out, d_tokens, d_prev):
-    depth = lax.axis_size("dp")
-    experts = [
-        grad.reshape(depth, 2, grad.shape[0] // (2 * depth), grad.shape[1])
-        for grad in (grad_gate, grad_up, grad_down)
-    ]
-    quarter = dense.shape[0] // 4
-    columns = dense.shape[1]
-    cut = (columns // LANES + 1) // 2 * LANES
-    dense = dense.reshape(2, 2, quarter, columns)
-    homes = [
-        block_out,
-        d_tokens.reshape(block_out.shape),
-        d_prev,
-    ]
-    size = quarter // depth
-    parts = [grad.shape[2:] for grad in experts]
-    vmem = pl.BlockSpec(memory_space=pltpu.VMEM)
-    copies = 3 + 2 * (depth - 1) * 4 + 4 + 6 + 1
-    outs = pl.pallas_call(
-        functools.partial(reduce_kernel, depth, cut),
-        in_specs=[vmem] * 7,
-        out_specs=[vmem] * 8,
-        out_shape=[shape((1,) + part, F32) for part in parts]
-        + [shape((size // 2, columns), F32)] * 2
-        + [shape(home.shape, home.dtype) for home in homes],
-        scratch_shapes=[pltpu.VMEM((depth,) + part, BF16) for part in parts] * 2
-        + [pltpu.VMEM((2, depth - 1) + part, BF16) for part in parts]
-        + [
-            pltpu.VMEM((2, quarter, cut), BF16),
-            pltpu.VMEM((2, quarter, columns - cut), BF16),
-            pltpu.VMEM((2, quarter, cut), BF16),
-            pltpu.VMEM((2, quarter, columns - cut), BF16),
-            pltpu.VMEM((quarter, cut), BF16),
-            pltpu.VMEM((quarter, columns - cut), BF16),
-            pltpu.VMEM((depth, size, columns), BF16),
-            pltpu.VMEM((2, depth - 1, size, columns), BF16),
-            pltpu.VMEM((size, columns), F32),
-            pltpu.SemaphoreType.DMA((copies,)),
-            pltpu.SemaphoreType.DMA((copies,)),
-            pltpu.SemaphoreType.DMA((3,)),
-        ],
-        compiler_params=pltpu.CompilerParams(
-            collective_id=1, has_side_effects=True, vmem_limit_bytes=60 * 1024 * 1024
-        ),
-        name="reduce_all",
-    )(*experts, dense, *homes)
-    return outs
 
 
 def attend_pair(pair, rows, reach, span, qkv_ref, segc_ref, segr_ref, att_ref, lse_ref):
@@ -1357,6 +1041,568 @@
     )
 
 
+class Line:
+    def __init__(self, mail, depth, slots):
+        self.depth = depth
+        self.slots = slots
+        self.place = lax.axis_index("dp")
+        y, x, z, core = position()
+        self.copies = {}
+        for way in range(2):
+            step_to = 1 if way == 0 else -1
+            device = (y * 2 + x, z + step_to, core)
+            for step in range(depth - 1):
+                for item, (acc, landing) in enumerate(slots):
+                    shard = self.shard(way, step)
+                    safe = jnp.clip(shard, 0, depth - 1)
+                    self.copies[way, step, item] = mail.copy(
+                        acc.at[safe], landing.at[way, step], device
+                    )
+
+    def shard(self, way, step):
+        if way == 0:
+            return self.place + self.depth - 1 - step
+        return self.place - (self.depth - 1 - step)
+
+    def edge(self, way):
+        return self.place == (0 if way == 0 else self.depth - 1)
+
+    def sends(self, way, step):
+        shard = self.shard(way, step)
+        if way == 0:
+            return (shard <= self.depth - 1) & (self.place < self.depth - 1)
+        return (shard >= 0) & (self.place > 0)
+
+    def gets(self, way, step):
+        if way == 0:
+            return (self.place > 0) & (self.shard(way, step + 1) <= self.depth - 1)
+        return (self.place < self.depth - 1) & (self.shard(way, step + 1) >= 0)
+
+    def send(self, step, item):
+        for way in range(2):
+            wanted = self.sends(way, step)
+            if step > 0:
+                wanted = wanted & jnp.logical_not(self.edge(way))
+
+            @pl.when(wanted)
+            def _():
+                self.copies[way, step, item].start()
+
+    def send_edge(self, step, item):
+        for way in range(2):
+
+            @pl.when(self.sends(way, step) & self.edge(way))
+            def _():
+                self.copies[way, step, item].start()
+
+    def take(self, step, item):
+        acc, landing = self.slots[item]
+        for way in range(2):
+            shard = jnp.clip(self.shard(way, step + 1), 0, self.depth - 1)
+
+            @pl.when(self.gets(way, step))
+            def _():
+                self.copies[way, step, item].wait_recv()
+                acc[shard] = (
+                    acc[shard].astype(F32) + landing[way, step].astype(F32)
+                ).astype(BF16)
+
+    def finish(self, item, store):
+        acc, landing = self.slots[item]
+        store(acc[self.place].astype(F32))
+        for way in range(2):
+
+            @pl.when(self.gets(way, self.depth - 2))
+            def _():
+                self.copies[way, self.depth - 2, item].wait_recv()
+                store(landing[way, self.depth - 2].astype(F32), True)
+
+    def close(self):
+        for (way, step, item), copy in self.copies.items():
+
+            @pl.when(self.sends(way, step))
+            def _():
+                copy.wait_send()
+
+
+class Plane:
+    def __init__(self, mail, source, buffers, total):
+        y, x, z, core = position()
+        self.place = y, x
+        self.source = source
+        self.buffers = buffers
+        self.total = total
+        y1_land, x1_land, y1_acc, x1_acc, x2_land, y2_land = buffers
+        half = x2_land.shape[0]
+        self.low = pl.ds(0, half)
+        self.high = pl.ds(half, half)
+        across = (y * 2 + 1 - x, z, core)
+        along = ((1 - y) * 2 + x, z, core)
+        self.first = [
+            mail.copy(source.at[1 - y, :, self.low], y1_land, along),
+            mail.copy(source.at[:, 1 - x, self.high], x1_land, across),
+        ]
+        self.second = [
+            mail.copy(y1_acc.at[1 - x], x2_land, across),
+            mail.copy(x1_acc.at[1 - y], y2_land, along),
+        ]
+
+    def start(self):
+        for copy in self.first:
+            copy.start()
+
+    def middle(self):
+        y, x = self.place
+        y1_land, x1_land, y1_acc, x1_acc, _, _ = self.buffers
+        self.first[0].wait_recv()
+        for k in range(2):
+            y1_acc[k] = (
+                self.source[y, k, self.low].astype(F32) + y1_land[k].astype(F32)
+            ).astype(BF16)
+        self.second[0].start()
+        self.first[1].wait_recv()
+        for k in range(2):
+            x1_acc[k] = (
+                self.source[k, x, self.high].astype(F32) + x1_land[k].astype(F32)
+            ).astype(BF16)
+        self.second[1].start()
+
+    def end(self):
+        y, x = self.place
+        _, _, y1_acc, x1_acc, x2_land, y2_land = self.buffers
+        shards, size = self.total.shape[0] // 2, self.total.shape[1]
+        self.second[0].wait_recv()
+        for shard in range(shards):
+            part = pl.ds(shard * size, size)
+            self.total[shard] = (
+                y1_acc[x, part].astype(F32) + x2_land[part].astype(F32)
+            ).astype(BF16)
+        self.second[1].wait_recv()
+        for shard in range(shards):
+            part = pl.ds(shard * size, size)
+            self.total[shards + shard] = (
+                x1_acc[y, part].astype(F32) + y2_land[part].astype(F32)
+            ).astype(BF16)
+
+    def close(self):
+        for copy in self.first + self.second:
+            copy.wait_send()
+
+
+def back_pair(
+    pair, rows, reach, span, qkv_ref, datt_ref, segc_ref, segr_ref, lse_ref, dqkv_ref,
+    dk_sum, dv_sum,
+):
+    length = qkv_ref.shape[0]
+    at_q, at_k, at_v = (
+        pl.ds(pl.multiple_of(part * span + pair * LANES, LANES), LANES) for part in range(3)
+    )
+    dk_sum[...] = jnp.zeros_like(dk_sum)
+    dv_sum[...] = jnp.zeros_like(dv_sum)
+    keys_turned = qkv_ref[:, at_k].T
+    for block in range(length // rows):
+        start, width = key_span(block, rows, reach)
+        here = pl.ds(block * rows, rows)
+        there = pl.ds(start, width)
+        queries = qkv_ref[here, at_q]
+        grads = datt_ref[here, at_q]
+        keys = qkv_ref[there, at_k]
+        values = qkv_ref[there, at_v]
+        seg_k = segc_ref[there, 0:1]
+        seg_q = segr_ref[0:1, here]
+        key_pos = start + lax.broadcasted_iota(jnp.int32, (width, rows), 0)
+        query_pos = block * rows + lax.broadcasted_iota(jnp.int32, (width, rows), 1)
+        allowed = (seg_q == seg_k) & (key_pos <= query_pos)
+        lane = lax.broadcasted_iota(jnp.int32, (rows, LANES), 1)
+        dq_parts = []
+        for head in range(2):
+            mine = (lane // HEAD) == head
+            head_q = jnp.where(mine, queries, 0)
+            head_g = jnp.where(mine, grads, 0)
+            log_total = lse_ref[pair, head : head + 1, here]
+            scores = dot(keys, head_q, ((1,), (1,))) * 0.125
+            probs = jnp.exp(jnp.where(allowed, scores, NEG) - log_total)
+            d_probs = dot(values, head_g, ((1,), (1,)))
+            delta = jnp.sum(probs * d_probs, axis=0, keepdims=True)
+            d_scores = (probs * (d_probs - delta)).astype(BF16)
+            dv_sum[there, :] += dot(probs.astype(BF16), head_g)
+            dk_sum[there, :] += dot(d_scores, head_q)
+            turned = keys_turned[head * HEAD : (head + 1) * HEAD, start : start + width]
+            dq_parts.append(dot(turned, d_scores))
+        dq = jnp.concatenate(dq_parts, axis=0).T * 0.125
+        dqkv_ref[here, at_q] = dq.astype(BF16)
+    dqkv_ref[:, at_k] = (dk_sum[...] * 0.125).astype(BF16)
+    dqkv_ref[:, at_v] = dv_sum[...].astype(BF16)
+
+
+def back_kernel(depth, rows, reach, *refs):
+    (
+        gate_any, up_any, down_any, branch_any, wout_any, att_any, qkv_any, segc_any, normed_any,
+        wqkv_any, x_any, dres_any, out_ref, prev_ref, lse_ref, segr_ref, small_ref, small_rows,
+        gate_out, up_out, down_out, qkv_out, wout_out, small_out, out_home, dtok_home, prev_home,
+        gate_land, up_land, down_land, gate_acc, up_acc, down_acc, gate_line, up_line, down_line,
+        branch_ref, wout_ref, att_ref, qkv_ref, segc_ref, normed_ref, wqkv_ref, x_ref, dres_ref,
+        normed_turned, datt_ref, turned_ref, dqkv_ref, dk_sum, dv_sum, dn_send, dn_recv, dtok_ref,
+        dense_ref, y1_land, x1_land, y1_acc, x1_acc, x2_land, y2_land, dense_acc, dense_line,
+        tail_ref, ty1_land, tx1_land, ty1_acc, tx1_acc, tx2_land, ty2_land, tail_acc, tail_line,
+        dense_sum, dense_sib, tail_sum, tail_sib, small_wide,
+        send_sems, recv_sems, local_sems,
+    ) = refs
+    y, x, z, core = position()
+    sibling = (y * 2 + x, z, 1 - core)
+    across = (y * 2 + 1 - x, z, core)
+    along = ((1 - y) * 2 + x, z, core)
+    moved = y != core
+    near = ((1 - y) * 2 + x, z, 1 - core)
+    far = (core * 2 + 1 - x, z, y)
+    greet(
+        [
+            (sibling, True), (across, True), (along, True),
+            (near, moved), (far, moved),
+            ((y * 2 + x, z + 1, core), z < depth - 1), ((y * 2 + x, z - 1, core), z > 0),
+        ]
+    )
+    mail = Mail(send_sems, recv_sems)
+    length, width = normed_ref.shape
+    mine = length // 2
+    span = wout_ref.shape[0]
+    pairs = span // LANES
+    own_rows = pl.ds(pl.multiple_of(core * mine, mine), mine)
+    experts = [
+        (gate_any, gate_land, gate_acc, gate_line, gate_out),
+        (up_any, up_land, up_acc, up_line, up_out),
+        (down_any, down_land, down_acc, down_line, down_out),
+    ]
+    halves = [mail.copy(source.at[:, 1 - core], land, sibling) for source, land, _, _, _ in experts]
+    line = Line(mail, depth, [(acc, landing) for _, _, acc, landing, _ in experts])
+    branch_copy = mail.copy(branch_any, branch_ref.at[own_rows], sibling)
+    loads = [
+        pltpu.make_async_copy(source, target, local_sems.at[k])
+        for k, (source, target) in enumerate(
+            [
+                (gate_any.at[:, core], gate_acc), (up_any.at[:, core], up_acc),
+                (down_any.at[:, core], down_acc), (branch_any, branch_ref.at[own_rows]),
+                (normed_any, normed_ref), (att_any, att_ref), (wout_any, wout_ref),
+                (segc_any, segc_ref), (qkv_any, qkv_ref), (wqkv_any, wqkv_ref),
+                (x_any.at[own_rows], x_ref), (dres_any, dres_ref),
+            ]
+        )
+    ]
+    homes = [(out_ref, out_home), (prev_ref, prev_home), (dtok_ref, dtok_home)]
+    nears = [mail.copy(a.at[x], b.at[x], near) for a, b in homes]
+    fars = [mail.copy(a.at[1 - x], b.at[x], far) for a, b in homes]
+    stays = [
+        pltpu.make_async_copy(a.at[x], b.at[x], local_sems.at[len(loads) + k])
+        for k, (a, b) in enumerate(homes)
+    ]
+
+    def go_near(k):
+        @pl.when(moved)
+        def _():
+            nears[k].start()
+
+        @pl.when(jnp.logical_not(moved))
+        def _():
+            stays[k].start()
+
+    half_copy = mail.copy(turned_ref.at[1 - core], dense_ref.at[0, core], sibling)
+    planes = [
+        Plane(
+            mail, dense_ref.at[c],
+            [b.at[c] for b in (y1_land, x1_land, y1_acc, x1_acc, x2_land, y2_land)],
+            dense_acc.at[c],
+        )
+        for c in range(pairs + 1)
+    ] + [
+        Plane(
+            mail, tail_ref, (ty1_land, tx1_land, ty1_acc, tx1_acc, tx2_land, ty2_land), tail_acc
+        )
+    ]
+    dense = Line(
+        mail, depth,
+        [(dense_acc.at[c], dense_line.at[c]) for c in range(pairs + 1)] + [(tail_acc, tail_line)],
+    )
+    chunks = pairs + 2
+    size = tail_sum.shape[0]
+    half = size // 2
+    other = pl.ds(pl.multiple_of((1 - core) * half, 8), half)
+    ours = pl.ds(pl.multiple_of(core * half, 8), half)
+    sums = [(dense_sum.at[c], dense_sib.at[c]) for c in range(pairs + 1)] + [(tail_sum, tail_sib)]
+    lasts = [mail.copy(a.at[other], b, sibling) for a, b in sums]
+    dn_copies = [mail.copy(dn_send.at[b], dn_recv.at[b], sibling) for b in range(2)]
+
+    for copy in halves[:1] + [branch_copy] + halves[1:]:
+        copy.start()
+    for copy in loads:
+        copy.start()
+    fars[0].start()
+    fars[1].start()
+    go_near(0)
+    go_near(1)
+
+    loads[4].wait()
+    normed_turned[...] = normed_ref[...].T
+    for item, (_, land, acc, _, _) in enumerate(experts):
+        loads[item].wait()
+        halves[item].wait_recv()
+        for shard in range(depth):
+            acc[shard] = (acc[shard].astype(F32) + land[shard].astype(F32)).astype(BF16)
+        line.send(0, item)
+    for item in range(3):
+        line.send_edge(1, item)
+    for k in (3, 5, 6, 7):
+        loads[k].wait()
+    branch_copy.wait_recv()
+
+    @pl.loop(0, length // rows)
+    def _(block):
+        here = pl.ds(pl.multiple_of(block * rows, rows), rows)
+        valid = (segc_ref[here, 0:1] != SEGS - 1.0).astype(F32)
+        datt_ref[here, :] = (
+            dot(branch_ref[here, :], wout_ref[...], ((1,), (1,))) * valid
+        ).astype(BF16)
+
+    att_turned = att_ref[...].T
+    for side in range(2):
+        part = dot(att_turned, branch_ref[:, side * span : (side + 1) * span]).astype(BF16)
+        turned_ref[side] = part.reshape(turned_ref.shape[1:])
+    half_copy.start()
+    dense_ref[0, core] = turned_ref[core]
+    for k in (8, 9):
+        loads[k].wait()
+    small_wide[...] = jnp.zeros_like(small_wide)
+
+    quarter = width // 4
+
+    @pl.loop(0, pairs)
+    def _(pair):
+        back_pair(
+            pair, rows, reach, span, qkv_ref, datt_ref, segc_ref, segr_ref, lse_ref, dqkv_ref,
+            dk_sum, dv_sum,
+        )
+        columns = [
+            pl.ds(pl.multiple_of(part * span + pair * LANES, LANES), LANES) for part in range(3)
+        ]
+
+        @pl.loop(0, 4)
+        def _(fourth):
+            here = pl.ds(pl.multiple_of(fourth * quarter, quarter), quarter)
+            d_pair = jnp.concatenate([dqkv_ref[:, at] for at in columns], axis=1)
+            weights = jnp.concatenate([wqkv_ref[here, at] for at in columns], axis=1)
+            grads = dot(normed_turned[here, :], d_pair)
+            dense_ref[1 + pair, fourth // 2, fourth % 2] = grads.astype(BF16)
+            gain = jnp.sum(grads * weights.astype(F32), axis=1, keepdims=True)
+            lane = lax.broadcasted_iota(jnp.int32, (quarter, LANES), 1)
+            small_wide[here, :] += jnp.where(lane == SMALL - 1, gain, 0.0)
+
+        for now in range(pairs):
+
+            @pl.when(pair == now)
+            def _():
+                planes[now + 1].start()
+                if now == 0:
+                    half_copy.wait_recv()
+                    planes[0].start()
+                    for item in range(2):
+                        line.take(0, item)
+                        line.send(1, item)
+                if now >= 1:
+                    planes[now - 1].middle()
+                if now >= 2:
+                    planes[now - 2].end()
+                    dense.send(0, now - 2)
+                    for step in range(1, depth - 1):
+                        dense.send_edge(step, now - 2)
+                if now == 1:
+                    line.take(0, 2)
+                    line.send(1, 2)
+                if now == 2:
+                    for item in range(2):
+                        line.take(1, item)
+                        line.send(2, item)
+
+    small_all = small_rows[...].astype(F32)
+    gain_column = column(widen(small_all), SMALL - 2)
+    lane = lax.broadcasted_iota(jnp.int32, (width, LANES), 1)
+    small_grads = jnp.where(
+        lane < SMALL - 1, widen(small_ref[...]), small_wide[...] / gain_column
+    )
+    tail_ref[...] = small_grads.astype(BF16).reshape(tail_ref.shape)
+    planes[chunks - 1].start()
+
+    def partial(start, step):
+        b = 1 - x if step == 0 else x
+        here = pl.ds(pl.multiple_of(start * mine + b * rows, rows), rows)
+        return b, dot(dqkv_ref[here, :], wqkv_ref[...], ((1,), (1,)))
+
+    def launch(c):
+        planes[c].end()
+        dense.send(0, c)
+        for step in range(1, depth - 1):
+            dense.send_edge(step, c)
+
+    for step in range(2):
+        b, value = partial(1 - core, step)
+        dn_send[step] = value.astype(BF16)
+        dn_copies[step].start()
+    planes[pairs - 1].middle()
+    launch(pairs - 2)
+    for item in range(3):
+        line.send_edge(2, item)
+    planes[pairs].middle()
+    launch(pairs - 1)
+    planes[pairs + 1].middle()
+    loads[10].wait()
+    loads[11].wait()
+    gain_row = small_all[SMALL - 2 : SMALL - 1, :]
+    for step in range(2):
+        b, value = partial(core, step)
+        here = pl.ds(pl.multiple_of(b * rows, rows), rows)
+        values = x_ref[here, :].astype(F32)
+        dn_copies[step].wait_recv()
+        d_normed = value + dn_recv[step].astype(F32)
+        inverse = lax.rsqrt(jnp.mean(values * values, axis=-1, keepdims=True) + NORM_EPS)
+        scaled = d_normed * gain_row
+        mean = jnp.mean(scaled * values, axis=-1, keepdims=True)
+        result = dres_ref[here, :] + inverse * scaled
+        result = result - values * (inverse * inverse * inverse * mean)
+        dtok_ref[b] = result.astype(BF16)
+        if step == 0:
+            fars[2].start()
+            launch(pairs)
+            launch(pairs + 1)
+        else:
+            go_near(2)
+    line.take(1, 2)
+    line.send(2, 2)
+    for step in range(depth - 2):
+        for c in range(chunks):
+            dense.take(step, c)
+            dense.send(step + 1, c)
+    for item, (_, _, _, _, result) in enumerate(experts):
+
+        def store(value, add=False):
+            result[0] = result[0] + value if add else value
+
+        line.finish(item, store)
+    for c, (total, _) in enumerate(sums):
+
+        def store(value, add=False):
+            total[...] = total[...] + value if add else value
+
+        dense.finish(c, store)
+        lasts[c].start()
+    for c, (total, land) in enumerate(sums):
+        own = total[ours]
+        lasts[c].wait_recv()
+        theirs = land[...]
+        if c == 0:
+            for side, value in ((core, own), (1 - core, theirs)):
+                wout_out[:, pl.ds(pl.multiple_of(side * span, LANES), span)] = value
+        elif c <= pairs:
+            for part in range(3):
+                for side, value in ((core, own), (1 - core, theirs)):
+                    at = part * 2 * span + side * span + (c - 1) * LANES
+                    qkv_out[:, pl.ds(pl.multiple_of(at, LANES), LANES)] = value[
+                        :, part * LANES : (part + 1) * LANES
+                    ]
+        else:
+            small_out[...] = own + theirs
+    for copy in halves + [branch_copy, half_copy] + lasts + dn_copies:
+        copy.wait_send()
+    for plane in planes:
+        plane.close()
+    line.close()
+    dense.close()
+    for copy in fars:
+        copy.wait()
+
+    @pl.when(moved)
+    def _():
+        for copy in nears:
+            copy.wait()
+
+    @pl.when(jnp.logical_not(moved))
+    def _():
+        for copy in stays:
+            copy.wait()
+
+
+def back_all(
+    grad_gate, grad_up, grad_down, d_branch, w_out, attended, qkv, seg_col, normed, qkv_weight,
+    x_all, d_residual, block_out, d_prev, lse, seg_row, small, small_all,
+):
+    depth = lax.axis_size("dp")
+    experts = [
+        grad.reshape(depth, 2, grad.shape[0] // (2 * depth), grad.shape[1])
+        for grad in (grad_gate, grad_up, grad_down)
+    ]
+    length, width = x_all.shape
+    mine = length // 2
+    span = width // 2
+    rows = block_out.shape[1]
+    groups = span // LANES + 1
+    wide = 3 * LANES
+    quarter = width // 4
+    size = quarter // depth
+    parts = [grad.shape[2:] for grad in experts]
+    vmem = pl.BlockSpec(memory_space=pltpu.VMEM)
+    anywhere = pl.BlockSpec(memory_space=pl.ANY)
+    homes = [block_out.shape, block_out.shape, d_prev.shape]
+    kinds = [block_out.dtype, BF16, d_prev.dtype]
+    steps = 2 * (depth - 1)
+    copies = 3 + 3 * steps + 2 + 6 + (groups + 1) * (4 + steps + 1) + 2
+
+    def plane_buffers(lead, columns):
+        return [
+            pltpu.VMEM(lead + dims + (columns,), BF16)
+            for dims in (
+                [(2, 2, quarter)] + [(2, quarter // 2)] * 4 + [(quarter // 2,)] * 2
+                + [(depth, size), (2, depth - 1, size)]
+            )
+        ]
+
+    return pl.pallas_call(
+        functools.partial(back_kernel, depth, rows, length // 2),
+        in_specs=[anywhere] * 12 + [vmem] * 6,
+        out_specs=[vmem] * 6 + [anywhere] * 3,
+        out_shape=[shape((1,) + part, F32) for part in parts]
+        + [shape((size // 2, 6 * span), F32), shape((size // 2, width), F32)]
+        + [shape((size // 2, LANES), F32)]
+        + [shape(dims, kind) for dims, kind in zip(homes, kinds)],
+        scratch_shapes=[pltpu.VMEM((depth,) + part, BF16) for part in parts] * 2
+        + [pltpu.VMEM((2, depth - 1) + part, BF16) for part in parts]
+        + [
+            pltpu.VMEM((length, width), BF16), pltpu.VMEM((span, width), BF16),
+            pltpu.VMEM((length, span), BF16), pltpu.VMEM((length, 3 * span), BF16),
+            pltpu.VMEM((length, LANES), F32), pltpu.VMEM((length, width), BF16),
+            pltpu.VMEM((width, 3 * span), BF16), pltpu.VMEM((mine, width), BF16),
+            pltpu.VMEM((mine, width), F32), pltpu.VMEM((width, length), BF16),
+            pltpu.VMEM((length, span), BF16), pltpu.VMEM((2, 2, quarter, span), BF16),
+            pltpu.VMEM((length, 3 * span), BF16), pltpu.VMEM((length, LANES), F32),
+            pltpu.VMEM((length, LANES), F32), pltpu.VMEM((2, rows, width), BF16),
+            pltpu.VMEM((2, rows, width), BF16), pltpu.VMEM((2, rows, width), BF16),
+        ]
+        + plane_buffers((groups,), wide)
+        + plane_buffers((), LANES)
+        + [
+            pltpu.VMEM((groups, size, wide), F32), pltpu.VMEM((groups, size // 2, wide), F32),
+            pltpu.VMEM((size, LANES), F32), pltpu.VMEM((size // 2, LANES), F32),
+            pltpu.VMEM((width, LANES), F32),
+            pltpu.SemaphoreType.DMA((copies,)),
+            pltpu.SemaphoreType.DMA((copies,)),
+            pltpu.SemaphoreType.DMA((15,)),
+        ],
+        compiler_params=pltpu.CompilerParams(
+            collective_id=1, has_side_effects=True, vmem_limit_bytes=62 * 1024 * 1024
+        ),
+        name="back_all",
+    )(
+        *experts, d_branch, w_out, attended, qkv, seg_col, normed, qkv_weight, x_all, d_residual,
+        block_out, d_prev, lse, seg_row, small, small_all,
+    )
+
+
 def one_chip(
     tokens,
     prev_logits,
@@ -1374,25 +1620,9 @@
     w_up,
     w_down,
 ):
-    rows, width = tokens.shape[1:]
-    core = lax.axis_index("fs")
+    rows = tokens.shape[1]
     route_count = w_router.shape[1]
     experts = route_count - 4
-    length = segments.shape[1]
-    mine = length // 2
-    span = width // 2
-    blocks = mine // rows
-
-    def swap(array):
-        return lax.ppermute(array, "fs", [(0, 1), (1, 0)])
-
-    def by_core(own, other, axis=0):
-        return jnp.where(
-            core == 0,
-            jnp.concatenate([own, other], axis=axis),
-            jnp.concatenate([other, own], axis=axis),
-        )
-
     (
         x_all, cot_own, ctl, normed, qkv, attended, lse, small_all, qkv_weight, out_sib,
         seg_col, seg_row,
@@ -1400,15 +1630,6 @@
         tokens, cotangent, w_qkv, w_out, prev_logits, routes, segments, w_router, const_proj,
         const_vec, gain_attn, gain_moe,
     )
-    head_pairs = span // LANES
-    reach = length // 2
-
-    def heads_at(offset):
-        return pl.BlockSpec((length, LANES), lambda p: (0, offset + p))
-
-    lse_spec = pl.BlockSpec((1, 8, length), lambda p: (p, 0, 0))
-    attn_gain = small_all[14:15].astype(F32)
-    x_own = lax.dynamic_slice_in_dim(x_all, core * mine, mine)
     (
         block_out, d_prev, d_residual, d_branch, small, grad_gate, grad_up, grad_down,
     ) = expert_layer(
@@ -1416,62 +1637,13 @@
         w_gate[0], w_up[0], w_down[0],
     )
 
-    branch_all = by_core(d_branch, swap(d_branch))
-    valid = (seg_col[:, :1] != SEGS - 1.0).astype(F32)
-    d_att = (dot(branch_all, w_out, ((1,), (1,))) * valid).astype(BF16)
-    grad_out = dot(attended, branch_all, ((0,), (0,))).astype(BF16)
-    d_queries, d_keys, d_values = pl.pallas_call(
-        functools.partial(attend_back_kernel, rows, reach),
-        grid=(head_pairs,),
-        in_specs=[
-            heads_at(0), heads_at(head_pairs), heads_at(2 * head_pairs), heads_at(0),
-            whole((length, LANES)), whole((8, length)), lse_spec,
-        ],
-        out_specs=[heads_at(0)] * 3,
-        out_shape=[shape((length, span), BF16)] * 3,
-        scratch_shapes=[pltpu.VMEM((length, LANES), F32)] * 2,
-        compiler_params=params(),
-        cost_estimate=cost(30e9, 5e6),
-        name="attend_back",
-    )(qkv, qkv, qkv, d_att, seg_col, seg_row, lse)
-    d_qkv = jnp.concatenate([d_queries, d_keys, d_values], axis=1)
-    d_normed = dot(d_qkv, qkv_weight, ((1,), (1,)))
-    d_normed_own = lax.dynamic_slice_in_dim(d_normed, core * mine, mine)
-    d_normed_sib = swap(
-        lax.dynamic_slice_in_dim(d_normed, (1 - core) * mine, mine).astype(BF16)
-    )
-    grad_qkv = dot(normed, d_qkv, ((0,), (0,))).astype(BF16)
-    d_tokens, gain_rows = pl.pallas_call(
-        finish_kernel,
-        grid=(blocks,),
-        in_specs=[per_row(rows, width)] * 4 + [whole((1, width))],
-        out_specs=[per_row(rows, width), whole((8, width))],
-        out_shape=[shape((mine, width), BF16), shape((8, width), F32)],
-        compiler_params=params(),
-        cost_estimate=cost(1e8, 6e6),
-        name="finish",
-    )(x_own, d_normed_own, d_normed_sib, d_residual, attn_gain)
-
-    out_mine = lax.dynamic_slice_in_dim(grad_out, core * span, span, axis=1)
-    out_sent = lax.dynamic_slice_in_dim(grad_out, (1 - core) * span, span, axis=1)
-    out_cols = by_core(out_mine, swap(out_sent))
-    small = jnp.concatenate([small[: SMALL - 1], gain_rows[:1]]).T.astype(BF16)
-    dense = jnp.concatenate(
-        [grad_qkv, out_cols, jnp.pad(small, ((0, 0), (0, LANES - SMALL)))], axis=1
-    )
-    shares = reduce_all(
-        grad_gate, grad_up, grad_down, dense, block_out, d_tokens, d_prev
-    )
-    pieces = shares[3:5]
-    out_home, dtok_home, prev_home = shares[5:]
-
-    def columns_of(start):
-        own, other = (piece[:, start : start + span] for piece in pieces)
-        return by_core(own, other, axis=1)
-
-    share_qkv = jnp.concatenate([columns_of(k * span) for k in range(3)], axis=1)
-    share_out = columns_of(3 * span)
-    share_small = sum(piece[:, 4 * span : 4 * span + SMALL] for piece in pieces)
+    (
+        share_gate, share_up, share_down, share_qkv, share_out, share_small, out_home, dtok_home,
+        prev_home,
+    ) = back_all(
+        grad_gate, grad_up, grad_down, d_branch, w_out, attended, qkv, seg_col, normed,
+        qkv_weight, x_all, d_residual, block_out, d_prev, lse, seg_row, small, small_all,
+    )
     return (
         out_home,
         dtok_home.astype(F32),
@@ -1483,7 +1655,10 @@
         share_small[:, :route_count],
         share_small[:, 8:12],
         share_small[:, 12:14],
-    ) + tuple(shares[:3])
+        share_gate,
+        share_up,
+        share_down,
+    )
 
 
 def suits(mesh, tokens, w_router, w_gate):
@@ -1495,6 +1670,7 @@
         peers == 4
         and mesh.shape["fs"] == 2
         and micro == 2
+        and mesh.shape["dp"] % 2 == 0
         and (routes - 4) * 2 == peers
         and 3 * rows // routes == LANES
         and tokens.shape[2] % (2 * LANES) == 0

time: 252 us -> 217 us (0.86)
  Pallas kernels: 204 us -> 191 us
  matrix products: 10.1 us -> 0 us
  local copies, waits for them, and re-layouts: 26.9 us -> 21.5 us
  other arithmetic: 7.8 us -> 2.42 us
    pallas_call x3 -> x1, Pallas kernels: 84 us -> 70.8 us  [back_all(): pl.pallas_call(functools.partial(back_kernel, depth, rows, length // 2),...]
    dot_general x4 -> x0, matrix products: 10.1 us -> none  [dot(): lax.dot_general(lhs, rhs, (dims, ((), ())), precision=precision, preferre...]
    slice x4 -> x0, local copies, waits for them, and re-layouts: 3.32 us -> none  [the longest x2 1.67 us: columns_of(): own, other = (piece[:, start:start + span] for piece in pieces)]
    unnamed x44 -> x27, local copies, waits for them, and re-layouts: 17.7 us -> 16 us
  transfers between devices with their start and end apart: 3 -> 0, of which waited for: 0 -> 0; matrix products, arithmetic and copies ran while one was open for 6% -> 0% of each run, Pallas kernels for 6% -> 0%
where the time goes in v2:
time: 217 us; the launch traced here: 216 us
  Pallas kernels  191 us (88%)
  local copies, waits for them, and re-layouts  21.5 us (10%)
  other arithmetic  2.42 us (1%)
    pallas_call x1, Pallas kernels, expert_layer(): pl.pallas_call(functools.partial(layer_kernel, experts, routes, rows, blo...  87.3 us
    pallas_call x1, Pallas kernels, back_all(): pl.pallas_call(functools.partial(back_kernel, depth, rows, length // 2),...  70.8 us
    pallas_call x1, Pallas kernels, gather_all(): pl.pallas_call(functools.partial(gather_kernel, rows, length // 2, w_rout...  33 us
    unnamed x27, local copies, waits for them, and re-layouts  16 us

profile of v2, /device:TPU:0, one launch (start us, length us, event | category | flops | bytes accessed | tf_op | source)
XLA Modules:
  0.0 215.7 jit_solution(16758098916023690060)
XLA Ops:
  0.6 1.2 broadcast_in_dim.6.gain_a_ref
  1.9 1.2 broadcast_in_dim.7.gain_m_ref
  3.1 1.5 copy.39.router_ref
  4.6 1.5 copy.40.cproj_ref
  6.1 1.5 copy.41.cvec_ref
  7.6 1.6 copy.37.prev_ref
  9.1 1.5 copy.38.route_ref
  10.7 33.0 %gather_all.1 = (bf16[1024,768]{1,0:T(8,128)(2,1)}, bf16[512,768]{1,0:T(8,128)(2,1)}, f32[2,16,256]{2,1,0:T(8,128)}, bf16[1024,768]{1,0:T(8,128)(2,1)}, bf16[102...) custom-call(bf16[2,256,768]{2,1,0:T(8,128)(2,1)} %tok_ref.1, ...), custom_call_target="tpu_custom_call" | custom-call | tf_op jit(solution)/shard_map/gather_all/pallas_call | solution.py:691
  43.7 87.3 %expert_layer.1 = (bf16[2,256,768]{2,1,0:T(8,128)(2,1)}, f32[2,8,256]{2,1,0:T(8,128)}, f32[512,768]{1,0:T(8,128)}, bf16[512,768]{1,0:T(8,128)(2,1)}, f32[16,768]...) custom-call(bf16[2,512,384]{2,1,0:T(8,128)(2,1)} %bitcast.10, ...), custom_call_target="tpu_custom_call" | custom-call | tf_op jit(solution)/shard_map/expert_layer/pallas_call | solution.py:1010
  130.9 70.8 %back_all.1 = (f32[1,96,1024]{2,1,0:T(8,128)}, f32[1,96,1024]{2,1,0:T(8,128)}, f32[1,128,768]{2,1,0:T(8,128)}, f32[24,2304]{1,0:T(8,128)}, f32[24,768]{1,0:T(8,1...) custom-call(bf16[4,2,96,1024]{3,2,1,0:T(8,128)(2,1)} %bitcast.11, ...), custom_call_target="tpu_custom_call" | custom-call | tf_op jit(solution)/shard_map/back_all/pallas_call | solution.py:1565
  201.8 0.0 copy-start
  201.8 1.5 slice_reduce_fusion
  203.3 1.4 copy.43
  204.7 1.3 copy.42
  206.0 0.8 slice.22
  206.8 0.7 copy.44
  207.4 0.8 slice.23
  208.2 0.6 copy.45
  208.8 2.4 %convert_element_type.3 = f32[2,256,768]{2,1,0:T(8,128)} convert(bf16[2,256,768]{2,1,0:T(8,128)(2,1)} %get-tuple-element.63) | non-fusion elementwise | flops 393216 | bytes 2359296 | tf_op jit(solution)/shard_map/convert_element_type | solution.py:1649
  211.3 0.0 copy-done
  211.3 0.0 copy-start.1
  211.3 0.9 copy.52
  212.2 0.0 copy-done.4
  212.2 0.7 copy.53
  212.9 0.0 copy-done.5
  212.9 0.6 copy.54
  213.5 0.0 copy-done.3
  213.5 0.7 copy.55
  214.2 0.0 copy-done.2
  214.3 0.7 copy.56
  215.0 0.0 copy-done.1
  215.0 0.7 copy.57
  (4 shorter events, 0.0 us)
Async XLA Ops:
  201.8 9.5 %copy-start = (bf16[2,256,768]{2,1,0:T(8,128)(2,1)S(1)}, bf16[2,256,768]{2,1,0:T(8,128)(2,1)}, u32[]{:S(2)}) copy-start(bf16[2,256,768]{2,1,0:T(8,128)(2,1)} %get-tuple-element.112) | copy-start | bytes 2359300
  208.8 3.3 %copy-start.4 = (f32[24,2304]{1,0:T(8,128)S(1)}, f32[24,2304]{1,0:T(8,128)}, u32[]{:S(2)}) copy-start(f32[24,2304]{1,0:T(8,128)} %get-tuple-element.116) | copy-start | bytes 663556
  211.3 1.6 copy-start.5
  211.3 2.2 %copy-start.3 = (f32[1,96,1024]{2,1,0:T(8,128)S(1)}, f32[1,96,1024]{2,1,0:T(8,128)}, u32[]{:S(2)}) copy-start(f32[1,96,1024]{2,1,0:T(8,128)} %get-tuple-element.122) | copy-start | bytes 1179652
  211.3 3.0 %copy-start.2 = (f32[1,96,1024]{2,1,0:T(8,128)S(1)}, f32[1,96,1024]{2,1,0:T(8,128)}, u32[]{:S(2)}) copy-start(f32[1,96,1024]{2,1,0:T(8,128)} %get-tuple-element.123) | copy-start | bytes 1179652
  211.3 3.7 %copy-start.1 = (f32[1,128,768]{2,1,0:T(8,128)S(1)}, f32[1,128,768]{2,1,0:T(8,128)}, u32[]{:S(2)}) copy-start(f32[1,128,768]{2,1,0:T(8,128)} %get-tuple-element.124) | copy-start | bytes 1179652

commit v3 on v2

--- a/solution.py
+++ b/solution.py
@@ -530,7 +530,7 @@
     cvec_ref, gain_a_ref, gain_m_ref,
     x_all, cot_own, ctl_own, normed_ref, qkv_ref, att_ref, lse_ref, small_all, wqkv_all,
     wout_sib, segc_ref, segr_ref,
-    ctl_wide, ctl_send, small_wide, small_send, seg_all,
+    ctl_send, small_wide, small_send, seg_all,
     near_send, near_recv, far_send, far_recv, core_send, core_recv, local_sems,
 ):
     y, x, z, core = position()
@@ -607,22 +607,21 @@
         copy.start()
 
     small_wide[...] = jnp.zeros_like(small_wide)
-    small_wide[:, 0:routes] = router_ref[...].astype(F32)
-    small_wide[:, 8:12] = cproj_ref[...].astype(F32)
-    small_wide[:, 12:14] = cvec_ref[...].astype(F32)
-    turned = small_wide[...].T[:SMALL, :]
-    which = lax.broadcasted_iota(jnp.int32, (SMALL, span), 0)
-    turned = jnp.where(which == 14, gain_a_ref[...].astype(F32), turned)
-    turned = jnp.where(which == 15, gain_m_ref[...].astype(F32), turned)
+    small_wide[0:routes, :] = router_ref[...].astype(F32)
+    small_wide[8:12, :] = cproj_ref[...].astype(F32)
+    small_wide[12:14, :] = cvec_ref[...].astype(F32)
+    small_wide[14:15, :] = gain_a_ref[...].astype(F32).reshape(1, span)
+    small_wide[15:16, :] = gain_m_ref[...].astype(F32).reshape(1, span)
+    turned = small_wide[...]
     small_send[...] = turned.astype(BF16)
     small_all[:, band] = turned.astype(BF16)
     small_copy.start()
     out_copy.start()
+    ctl_send[...] = jnp.zeros_like(ctl_send)
     for m in range(2):
-        ctl_wide[...] = jnp.zeros_like(ctl_wide)
-        ctl_wide[:, 0:routes] = prev_ref[m]
-        ctl_wide[:, 8:10] = route_ref[m].astype(F32)
-        ctl_send[m] = ctl_wide[...].T[:SMALL, :]
+        for route in range(routes):
+            ctl_send[m, route : route + 1, :] = prev_ref[route, m : m + 1, :]
+        ctl_send[m, 8:10, :] = route_ref[m].astype(F32)
     send(2)
     seg_copy.wait_recv()
     seg_own.wait()
@@ -701,8 +700,8 @@
             shape((length, LANES), F32), shape((8, length), F32),
         ],
         scratch_shapes=[
-            pltpu.VMEM((rows, LANES), F32), pltpu.VMEM((2, SMALL, rows), F32),
-            pltpu.VMEM((span, LANES), F32), pltpu.VMEM((SMALL, span), BF16),
+            pltpu.VMEM((2, SMALL, rows), F32),
+            pltpu.VMEM((SMALL, span), F32), pltpu.VMEM((SMALL, span), BF16),
             pltpu.VMEM((2, 2, length), jnp.int32),
         ]
         + [pltpu.SemaphoreType.DMA((3,))] * 4
@@ -713,8 +712,9 @@
         ),
         name="gather_all",
     )(
-        tokens, cotangent, w_qkv, w_out, prev_logits, routes, segments, w_router, const_proj,
-        const_vec, gain_attn[None], gain_moe[None],
+        tokens, cotangent, w_qkv, w_out, jnp.transpose(prev_logits, (2, 0, 1)),
+        jnp.swapaxes(routes, 1, 2), segments, w_router.T, const_proj.T, const_vec.T, gain_attn,
+        gain_moe,
     )
 
 
@@ -1603,6 +1603,50 @@
     )
 
 
+def deliver_kernel(
+    routes,
+    out_ref, dtok_ref, prev_ref, qkv_ref, wout_ref, small_ref, gate_ref, up_ref, down_ref,
+    out_end, tokens_end, prev_end, gain_a_end, qkv_end, wout_end, gain_m_end, router_end,
+    cproj_end, cvec_end, gate_end, up_end, down_end,
+):
+    for source, target in (
+        (out_ref, out_end), (qkv_ref, qkv_end), (wout_ref, wout_end), (gate_ref, gate_end),
+        (up_ref, up_end), (down_ref, down_end),
+    ):
+        target[...] = source[...]
+    tokens_end[...] = dtok_ref[...].astype(F32)
+    for m in range(2):
+        for route in range(routes):
+            prev_end[route, m : m + 1, :] = prev_ref[m, route : route + 1, :]
+    count = small_ref.shape[0]
+    turned = widen(small_ref[...])
+    router_end[...] = turned[0:routes, 0:count]
+    cproj_end[...] = turned[8:12, 0:count]
+    cvec_end[...] = turned[12:14, 0:count]
+    gain_m_end[...] = turned[14:15, 0:count].reshape(count)
+    gain_a_end[...] = turned[15:16, 0:count].reshape(count)
+
+
+def deliver(routes, out, dtok, prev, qkv, wout, small, gate, up, down):
+    count = small.shape[0]
+    vmem = pl.BlockSpec(memory_space=pltpu.VMEM)
+    return pl.pallas_call(
+        functools.partial(deliver_kernel, routes),
+        in_specs=[vmem] * 9,
+        out_specs=[vmem] * 13,
+        out_shape=[
+            shape(out.shape, BF16), shape(dtok.shape, F32), shape((routes, 2, prev.shape[2]), F32),
+            shape((count,), F32), shape(qkv.shape, F32), shape(wout.shape, F32),
+            shape((count,), F32), shape((routes, count), F32), shape((4, count), F32),
+            shape((2, count), F32), shape(gate.shape, F32), shape(up.shape, F32),
+            shape(down.shape, F32),
+        ],
+        compiler_params=params(),
+        cost_estimate=cost(1e6, 8e6),
+        name="deliver",
+    )(out, dtok, prev, qkv, wout, small, gate, up, down)
+
+
 def one_chip(
     tokens,
     prev_logits,
@@ -1644,20 +1688,16 @@
         grad_gate, grad_up, grad_down, d_branch, w_out, attended, qkv, seg_col, normed,
         qkv_weight, x_all, d_residual, block_out, d_prev, lse, seg_row, small, small_all,
     )
+    (
+        block_out, grad_tokens, grad_prev, gain_a, grad_qkv, grad_out, gain_m, grad_router,
+        grad_cproj, grad_cvec, grad_gate, grad_up, grad_down,
+    ) = deliver(
+        route_count, out_home, dtok_home, prev_home, share_qkv, share_out, share_small,
+        share_gate, share_up, share_down,
+    )
     return (
-        out_home,
-        dtok_home.astype(F32),
-        jnp.swapaxes(prev_home, 1, 2)[:, :, :route_count],
-        share_small[:, 15],
-        share_qkv,
-        share_out,
-        share_small[:, 14],
-        share_small[:, :route_count],
-        share_small[:, 8:12],
-        share_small[:, 12:14],
-        share_gate,
-        share_up,
-        share_down,
+        block_out, grad_tokens, jnp.transpose(grad_prev, (1, 2, 0)), gain_a, grad_qkv, grad_out,
+        gain_m, grad_router.T, grad_cproj.T, grad_cvec.T, grad_gate, grad_up, grad_down,
     )
 
 

time: 217 us -> 196 us (0.903)
  local copies, waits for them, and re-layouts: 21.5 us -> 0 us
  Pallas kernels: 191 us -> 195 us
  other arithmetic: 2.42 us -> 0 us
    unnamed x27 -> x0, local copies, waits for them, and re-layouts: 16 us -> none
    pallas_call x0 -> x1, Pallas kernels: none -> 3.84 us  [deliver(): pl.pallas_call(functools.partial(deliver_kernel, routes), in_specs=[vmem]...]
    slice x3 -> x0, local copies, waits for them, and re-layouts: 3.06 us -> none  [the longest x1 1.5 us: one_chip(): share_small[:, 14]]
    broadcast_in_dim x2 -> x0, local copies, waits for them, and re-layouts: 2.49 us -> none  [the longest x1 1.24 us: gather_all(): gain_attn[None]]
    convert_element_type x1 -> x0, other arithmetic: 2.42 us -> none  [one_chip(): dtok_home.astype(F32)]
where the time goes in v3:
time: 196 us; the launch traced here: 195 us
  Pallas kernels  195 us (99%)
    pallas_call x1, Pallas kernels, expert_layer(): pl.pallas_call(functools.partial(layer_kernel, experts, routes, rows, blo...  87.3 us
    pallas_call x1, Pallas kernels, back_all(): pl.pallas_call(functools.partial(back_kernel, depth, rows, length // 2),...  70.8 us
    pallas_call x1, Pallas kernels, gather_all(): pl.pallas_call(functools.partial(gather_kernel, rows, length // 2, w_rout...  32.6 us

profile of v3, /device:TPU:0, one launch (start us, length us, event | category | flops | bytes accessed | tf_op | source)
XLA Modules:
  0.0 195.4 jit_solution(4681431734699032483)
XLA Ops:
  0.6 32.6 %gather_all.1 = (bf16[1024,768]{1,0:T(8,128)(2,1)}, bf16[512,768]{1,0:T(8,128)(2,1)}, f32[2,16,256]{2,1,0:T(8,128)}, bf16[1024,768]{1,0:T(8,128)(2,1)}, bf16[102...) custom-call(bf16[2,256,768]{2,1,0:T(8,128)(2,1)} %tok_ref.1, ...), custom_call_target="tpu_custom_call" | custom-call | tf_op jit(solution)/shard_map/gather_all/pallas_call | solution.py:690
  33.3 87.3 %expert_layer.1 = (bf16[2,256,768]{2,1,0:T(8,128)(2,1)}, f32[2,8,256]{2,1,0:T(8,128)}, f32[512,768]{1,0:T(8,128)}, bf16[512,768]{1,0:T(8,128)(2,1)}, f32[16,768]...) custom-call(bf16[2,512,384]{2,1,0:T(8,128)(2,1)} %bitcast.16, ...), custom_call_target="tpu_custom_call" | custom-call | tf_op jit(solution)/shard_map/expert_layer/pallas_call | solution.py:1010
  120.6 70.8 %back_all.1 = (f32[1,96,1024]{2,1,0:T(8,128)}, f32[1,96,1024]{2,1,0:T(8,128)}, f32[1,128,768]{2,1,0:T(8,128)}, f32[24,2304]{1,0:T(8,128)}, f32[24,768]{1,0:T(8,1...) custom-call(bf16[4,2,96,1024]{3,2,1,0:T(8,128)(2,1)} %bitcast.17, ...), custom_call_target="tpu_custom_call" | custom-call | tf_op jit(solution)/shard_map/back_all/pallas_call | solution.py:1565
  191.4 3.8 %deliver.1 = (bf16[2,256,768]{2,1,0:T(8,128)(2,1)}, f32[2,256,768]{2,1,0:T(8,128)}, f32[6,2,256]{2,1,0:T(2,128)}, f32[24]{0:T(128)}, f32[24,2304]{1,0:T(8,128)},...) custom-call(bf16[2,256,768]{2,1,0:T(8,128)(2,1)} %get-tuple-element., ...), custom_call_target="tpu_custom_call" | custom-call | flops 1000000 | bytes 8000000 | tf_op jit(solution)/shard_map/deliver/pallas_call | solution.py:1633

commit v4 on v3

--- a/solution.py
+++ b/solution.py
@@ -525,13 +525,14 @@
 
 
 def gather_kernel(
-    rows, reach, routes,
+    rows, reach, routes, experts,
     tok_ref, cot_ref, wqkv_ref, wout_ref, prev_ref, route_ref, seg_ref, router_ref, cproj_ref,
     cvec_ref, gain_a_ref, gain_m_ref,
     x_all, cot_own, ctl_own, normed_ref, qkv_ref, att_ref, lse_ref, small_all, wqkv_all,
-    wout_sib, segc_ref, segr_ref,
-    ctl_send, small_wide, small_send, seg_all,
+    wout_sib, segc_ref, segr_ref, g_rows,
+    cot_wide, g_send, ctl_send, small_wide, small_send, seg_all,
     near_send, near_recv, far_send, far_recv, core_send, core_recv, local_sems,
+    pack_send, pack_recv,
 ):
     y, x, z, core = position()
     me = y * 2 + x
@@ -539,8 +540,28 @@
     moved = y != core
     near = ((1 - y) * 2 + x, z, 1 - core)
     far = (core * 2 + 1 - x, z, y)
-    greet([(sibling, True), (far, True), (near, moved)])
+    plane = [((y + k // 2) % 2 * 2 + (x + k) % 2) for k in range(4)]
+    greet([((plane[k], z, (core + c) % 2), True) for k in range(4) for c in range(2) if k + c > 0])
     span = wqkv_ref.shape[0]
+    halves = 4 // experts
+
+    def pack(m, k, target=None):
+        return pltpu.make_async_remote_copy(
+            src_ref=g_send.at[m, plane[k] // halves],
+            dst_ref=g_rows.at[x, core * 2 + m] if target is None else g_rows.at[target],
+            send_sem=pack_send.at[m, k],
+            recv_sem=pack_recv.at[x, core * 2 + m] if target is None else pack_recv.at[target],
+            device_id=(plane[k], z, y),
+            device_id_type=pl.DeviceIdType.MESH,
+        )
+
+    pack_stays = [
+        pltpu.make_async_copy(
+            g_send.at[m, y // (halves // 2)], g_rows.at[x, core * 2 + m], local_sems.at[7 + m]
+        )
+        for m in range(2)
+    ]
+    cot_load = pltpu.make_async_copy(cot_ref, cot_wide, local_sems.at[9])
 
     def block_of(index):
         return pl.ds(pl.multiple_of(index * rows, rows), rows)
@@ -580,6 +601,7 @@
             stay_copies[k].wait()
 
     send(0)
+    cot_load.start()
     inner = Mail(core_send, core_recv)
     weight_copies = []
     own_copies = []
@@ -623,6 +645,29 @@
             ctl_send[m, route : route + 1, :] = prev_ref[route, m : m + 1, :]
         ctl_send[m, 8:10, :] = route_ref[m].astype(F32)
     send(2)
+    cot_load.wait()
+    earlier = lax.broadcasted_iota(jnp.int32, (rows, rows), 0) < lax.broadcasted_iota(
+        jnp.int32, (rows, rows), 1
+    )
+    slot = lax.broadcasted_iota(jnp.int32, (LANES, rows), 0).astype(F32)
+    number = lax.broadcasted_iota(jnp.int32, (8, rows), 0)
+    for m in range(2):
+        chosen = ((number == route_ref[m, 0:1, :]) | (number == route_ref[m, 1:2, :])).astype(F32)
+        rank = dot(chosen.astype(BF16), earlier.astype(BF16))
+        for expert in range(experts):
+            hit = (slot == rank[expert : expert + 1, :]) & (chosen[expert : expert + 1, :] > 0.0)
+            g_send[m, expert] = dot(hit.astype(BF16), cot_wide[m]).astype(BF16)
+        for k in range(1, 4):
+            pack(m, k).start()
+
+        @pl.when(moved)
+        def _():
+            pack(m, 0).start()
+
+        @pl.when(jnp.logical_not(moved))
+        def _():
+            pack_stays[m].start()
+
     seg_copy.wait_recv()
     seg_own.wait()
     seg_row = seg_all[y, pl.ds(x, 1), :].astype(F32)
@@ -667,6 +712,26 @@
     for k in (1, 2):
         take_near(k)
         far_copies[k].wait_recv()
+    for there in range(2):
+        for peer in range(4):
+            kept = (y == core) & (x == there) & (core == peer // 2)
+
+            @pl.when(jnp.logical_not(kept))
+            def _():
+                pack(0, 0, (there, peer)).wait_recv()
+
+    for m in range(2):
+        for k in range(1, 4):
+            pack(m, k).wait_send()
+
+        @pl.when(moved)
+        def _():
+            pack(m, 0).wait_send()
+
+        @pl.when(jnp.logical_not(moved))
+        def _():
+            pack_stays[m].wait()
+
     out_copy.wait_recv()
     for copy in far_copies + weight_copies + forward + [out_copy, seg_copy, small_copy]:
         copy.wait_send()
@@ -678,7 +743,7 @@
 
 
 def gather_all(
-    tokens, cotangent, w_qkv, w_out, prev_logits, routes, segments, w_router, const_proj,
+    experts, tokens, cotangent, w_qkv, w_out, prev_logits, routes, segments, w_router, const_proj,
     const_vec, gain_attn, gain_moe,
 ):
     rows, width = tokens.shape[1:]
@@ -688,9 +753,9 @@
     vmem = pl.BlockSpec(memory_space=pltpu.VMEM)
     anywhere = pl.BlockSpec(memory_space=pl.ANY)
     return pl.pallas_call(
-        functools.partial(gather_kernel, rows, length // 2, w_router.shape[1]),
+        functools.partial(gather_kernel, rows, length // 2, w_router.shape[1], experts),
         in_specs=[anywhere] * 4 + [vmem] * 8,
-        out_specs=[vmem] * 12,
+        out_specs=[vmem] * 13,
         out_shape=[
             shape((length, width), BF16), shape((mine, width), BF16),
             shape((2, SMALL, rows), F32), shape((length, width), BF16),
@@ -698,15 +763,18 @@
             shape((span // LANES, 8, length), F32), shape((SMALL, width), BF16),
             shape((width, 3 * span), BF16), shape((span, width), BF16),
             shape((length, LANES), F32), shape((8, length), F32),
+            shape((2, 4, LANES, width), BF16),
         ],
         scratch_shapes=[
+            pltpu.VMEM((2, rows, width), BF16), pltpu.VMEM((2, experts, LANES, width), BF16),
             pltpu.VMEM((2, SMALL, rows), F32),
             pltpu.VMEM((SMALL, span), F32), pltpu.VMEM((SMALL, span), BF16),
             pltpu.VMEM((2, 2, length), jnp.int32),
         ]
         + [pltpu.SemaphoreType.DMA((3,))] * 4
         + [pltpu.SemaphoreType.DMA((8,))] * 2
-        + [pltpu.SemaphoreType.DMA((7,))],
+        + [pltpu.SemaphoreType.DMA((10,))]
+        + [pltpu.SemaphoreType.DMA((2, 4))] * 2,
         compiler_params=pltpu.CompilerParams(
             collective_id=3, has_side_effects=True, vmem_limit_bytes=60 * 1024 * 1024
         ),
@@ -723,8 +791,10 @@
     return jnp.concatenate([turned, pad], axis=0).T
 
 
-def spread_block(experts, routes, rows, block, refs, send_ref, recv_ref, keep):
-    att_own, att_sib, x_ref, g_ref, ctl_ref, w_own, w_sib, small_rows, wide_rows = refs
+def spread_block(experts, routes, rows, block, refs, sent, got, keep):
+    send_ref, gate_send = sent
+    recv_ref, gate_recv = got
+    att_own, att_sib, x_ref, ctl_ref, w_own, w_sib, small_rows, wide_rows = refs
     residual_ref, mixed_ref, pm_ref, place_ref = keep
     y, x, z, core = position()
     here = pl.ds(pl.multiple_of(block * rows, rows), rows)
@@ -762,28 +832,28 @@
     )
     rank = dot(earlier.astype(BF16), chosen.astype(BF16))
     lane_f = lane.astype(F32)
-    grads = g_ref[here, :].astype(F32)
     for expert in range(experts):
         place = jnp.where(
             (lane_f == column(rank, expert)) & (column(chosen, expert) > 0.0), 1.0, 0.0
         )
         place_ref[here, expert * LANES : (expert + 1) * LANES] = place.astype(BF16)
         pick = place.T.astype(BF16)
-        d_part = (column(gated, expert) * grads).astype(BF16)
-        send_ref[block, expert, 0] = dot(pick, mixed).astype(BF16)
-        send_ref[block, expert, 1] = dot(pick, d_part).astype(BF16)
+        send_ref[block, expert] = dot(pick, mixed).astype(BF16)
+        gates = jnp.sum(place * column(gated, expert), axis=0, keepdims=True)
+        gate_send[block, expert] = jnp.broadcast_to(gates, gate_send.shape[2:])
     recv_ref[block, y * 2 + x] = send_ref[block, y]
-
-
-def expert_block(block, recv_ref, result_ref, back_ref, weights, keep):
+    gate_recv[block, y * 2 + x] = gate_send[block, y]
+
+
+def expert_block(block, got, result_ref, back_ref, weights, keep, send):
+    recv_ref, gate_recv, g_rows = got
     gate_w, up_w, down_w = weights
-    hidden_ref, d_gate_ref, d_up_ref = keep
+    hidden_ref, d_gate_ref, d_up_ref, d_rows_ref = keep
     y, x, z, core = position()
-    peers, _, capacity, width = recv_ref.shape[1:]
+    peers, capacity, width = recv_ref.shape[1:]
     size = peers * capacity
     here = pl.ds(pl.multiple_of(block * size, size), size)
-    rows = recv_ref[block, :, 0].reshape(size, width)
-    d_rows = recv_ref[block, :, 1].reshape(size, width)
+    rows = recv_ref[block].reshape(size, width)
     gate = dot(rows, gate_w[...])
     up = dot(rows, up_w[...])
     sig = jax.nn.sigmoid(gate)
@@ -792,6 +862,13 @@
     hidden_ref[here, :] = hidden
     part = dot(hidden, down_w[...]).astype(BF16)
     result_ref[block, :, 0] = part.reshape(peers, capacity, width)
+    send(0)
+    for peer in range(peers):
+        spread = jnp.concatenate([gate_recv[block, peer]] * (capacity // 8), axis=0).T
+        d_part = column(spread, 0) * g_rows[block, peer].astype(F32)
+        at = pl.ds(pl.multiple_of(block * size + peer * capacity, capacity), capacity)
+        d_rows_ref[at, :] = d_part.astype(BF16)
+    d_rows = d_rows_ref[here, :]
     d_hidden = dot(d_rows, down_w[...], ((1,), (1,)))
     d_gate = (d_hidden * up * sig * (1.0 + gate * (1.0 - sig))).astype(BF16)
     d_up = (d_hidden * active).astype(BF16)
@@ -799,6 +876,7 @@
     d_up_ref[here, :] = d_up
     d_in = dot(d_gate, gate_w[...], ((1,), (1,))) + dot(d_up, up_w[...], ((1,), (1,)))
     result_ref[block, :, 1] = d_in.astype(BF16).reshape(peers, capacity, width)
+    send(1)
     back_ref[block, y * 2 + x] = result_ref[block, y * 2 + x]
 
 
@@ -883,18 +961,52 @@
 
 def layer_kernel(
     experts, routes, rows, blocks,
-    att_ref, x_ref, g_ref, ctl_ref, w_own, w_sib, small_rows, gate_ref, up_ref, down_ref,
-    out_ref, prev_ref, dres_ref, branch_ref, small_ref, dgate_out, dup_out, ddown_out,
+    att_ref, x_ref, g_ref, ctl_ref, w_own, w_sib, small_rows, gate_ref, up_ref, down_ref, g_rows,
+    out_ref, prev_ref, dres_ref, branch_ref, small_ref, gate_acc, up_acc, down_acc,
+    dgate_out, dup_out, ddown_out, gate_land, up_land, down_land, gate_line, up_line, down_line,
     wide_rows, att_own, att_sib, gate_w, up_w, down_w, residual_ref, mixed_ref, pm_ref, place_ref,
-    send_ref, recv_ref, result_ref, back_ref, hidden_ref, d_gate_ref, d_up_ref,
-    head_send, head_recv, local_sems, send_sems, recv_sems, back_send, back_recv,
+    send_ref, gate_send, gate_recv, recv_ref, result_ref, back_ref, hidden_ref, d_gate_ref,
+    d_up_ref, d_rows_ref,
+    head_send, head_recv, local_sems, send_sems, recv_sems, back_send, back_recv, sum_send, sum_recv,
 ):
     y, x, z, core = position()
     me = y * 2 + x
     sibling = (me, z, 1 - core)
     partners = [(1 - y) * 2 + 1 - x, y * 2 + 1 - x, (1 - y) * 2 + x]
     wanted = [1 - y, y, 1 - y]
-    greet([(sibling, True)] + [((place, z, core), True) for place in partners])
+    depth = lax.axis_size("dp")
+    greet(
+        [(sibling, True)] + [((place, z, core), True) for place in partners]
+        + [((me, z + 1, core), z < depth - 1), ((me, z - 1, core), z > 0)]
+    )
+    sums = Mail(sum_send, sum_recv)
+    grads = [
+        (dgate_out, gate_land, gate_acc, gate_line), (dup_out, up_land, up_acc, up_line),
+        (ddown_out, down_land, down_acc, down_line),
+    ]
+
+    def share(ref, shard, side):
+        size = ref.shape[0] // (2 * depth)
+        return pl.ds(pl.multiple_of((shard * 2 + side) * size, size), size)
+
+    halves = [
+        [
+            sums.copy(ref.at[share(ref, shard, 1 - core)], land.at[shard], sibling)
+            for shard in range(depth)
+        ]
+        for ref, land, _, _ in grads
+    ]
+    line = Line(sums, depth, [(acc, landing) for _, _, acc, landing in grads], depth - 2)
+
+    def add_halves(item):
+        ref, land, acc, _ = grads[item]
+        for shard in range(depth):
+            halves[item][shard].wait_recv()
+            acc[shard] = (
+                ref[share(ref, shard, core)].astype(F32) + land[shard].astype(F32)
+            ).astype(BF16)
+        line.send(0, item)
+
     mine = rows * blocks
     mail = Mail(head_send, head_recv)
     pairs = [(gate_ref, gate_w), (up_ref, up_w), (down_ref, down_w)]
@@ -908,26 +1020,28 @@
     for copy in heads + locals_:
         copy.start()
 
-    def dispatch(block, k):
+    def dispatch(block, k, kind):
+        source, target = ((send_ref, recv_ref), (gate_send, gate_recv))[kind]
         return pltpu.make_async_remote_copy(
-            src_ref=send_ref.at[block, wanted[k]],
-            dst_ref=recv_ref.at[block, me],
-            send_sem=send_sems.at[block, k],
-            recv_sem=recv_sems.at[block, k],
+            src_ref=source.at[block, wanted[k]],
+            dst_ref=target.at[block, me],
+            send_sem=send_sems.at[block, k, kind],
+            recv_sem=recv_sems.at[block, k, kind],
             device_id=(partners[k], z, core),
             device_id_type=pl.DeviceIdType.MESH,
         )
 
-    def giveback(block, k):
+    def giveback(block, k, kind):
         return pltpu.make_async_remote_copy(
-            src_ref=result_ref.at[block, partners[k]],
-            dst_ref=back_ref.at[block, me],
-            send_sem=back_send.at[block, k],
-            recv_sem=back_recv.at[block, k],
+            src_ref=result_ref.at[block, partners[k], kind],
+            dst_ref=back_ref.at[block, me, kind],
+            send_sem=back_send.at[block, k, kind],
+            recv_sem=back_recv.at[block, k, kind],
             device_id=(partners[k], z, core),
             device_id_type=pl.DeviceIdType.MESH,
         )
 
+    every = [(k, kind) for kind in range(KINDS) for k in range(3)]
     small_ref[...] = jnp.zeros_like(small_ref)
     wide_rows[...] = jnp.zeros_like(wide_rows)
     wide_rows[0:SMALL, :] = small_rows[...]
@@ -935,14 +1049,17 @@
     locals_[0].wait()
     keep = (residual_ref, mixed_ref, pm_ref, place_ref)
     spread_refs = (
-        att_own, att_sib, x_ref, g_ref, ctl_ref, w_own, w_sib, small_rows, wide_rows
+        att_own, att_sib, x_ref, ctl_ref, w_own, w_sib, small_rows, wide_rows
     )
 
     @pl.loop(0, blocks)
     def _(block):
-        spread_block(experts, routes, rows, block, spread_refs, send_ref, recv_ref, keep)
-        for k in range(3):
-            dispatch(block, k).start()
+        spread_block(
+            experts, routes, rows, block, spread_refs, (send_ref, gate_send),
+            (recv_ref, gate_recv), keep,
+        )
+        for k, kind in every:
+            dispatch(block, k, kind).start()
 
     for copy in heads[1:]:
         copy.wait_recv()
@@ -951,53 +1068,76 @@
 
     @pl.loop(0, blocks)
     def _(block):
-        for k in range(3):
-            dispatch(block, k).wait_recv()
+        for k, kind in every:
+            dispatch(block, k, kind).wait_recv()
+
+        def send(kind):
+            for k in range(3):
+                giveback(block, k, kind).start()
+
         expert_block(
-            block, recv_ref, result_ref, back_ref, (gate_w, up_w, down_w),
-            (hidden_ref, d_gate_ref, d_up_ref),
-        )
-        for k in range(3):
-            giveback(block, k).start()
-
-    peers, _, capacity, width = recv_ref.shape[1:]
+            block, (recv_ref, gate_recv, g_rows), result_ref, back_ref, (gate_w, up_w, down_w),
+            (hidden_ref, d_gate_ref, d_up_ref, d_rows_ref), send,
+        )
+
+    peers, capacity, width = recv_ref.shape[1:]
     total = blocks * peers * capacity
     step = 2 * LANES
 
     @pl.loop(0, width // step)
     def _(chunk):
         span = pl.ds(pl.multiple_of(chunk * step, step), step)
-        lhs = recv_ref[:, :, 0, :, span].reshape(total, step).T
+        lhs = recv_ref[:, :, :, span].reshape(total, step).T
         dgate_out[span, :] = dot(lhs, d_gate_ref[...]).astype(BF16)
         dup_out[span, :] = dot(lhs, d_up_ref[...]).astype(BF16)
+
+    for copy in halves[0] + halves[1]:
+        copy.start()
 
     @pl.loop(0, hidden_ref.shape[1] // step)
     def _(chunk):
         span = pl.ds(pl.multiple_of(chunk * step, step), step)
         lhs = hidden_ref[:, span].T
-        rhs = recv_ref[:, :, 1].reshape(total, width)
-        ddown_out[span, :] = dot(lhs, rhs).astype(BF16)
+        ddown_out[span, :] = dot(lhs, d_rows_ref[...]).astype(BF16)
+
+    for copy in halves[2]:
+        copy.start()
+    for item in range(3):
+        add_halves(item)
+    for step in range(1, depth - 2):
+        for item in range(3):
+            line.send_edge(step, item)
 
     @pl.loop(0, blocks)
     def _(block):
-        for k in range(3):
-            giveback(block, k).wait_recv()
+        for k, kind in every:
+            giveback(block, k, kind).wait_recv()
         combine_block(
             experts, routes, rows, block, (g_ref, ctl_ref, small_rows, wide_rows),
             keep, back_ref, (out_ref, prev_ref, dres_ref, branch_ref), small_ref,
         )
 
-    for copy in heads:
+        @pl.when(block == 0)
+        def _():
+            for step in range(depth - 3):
+                for item in range(3):
+                    line.take(step, item)
+                    line.send(step + 1, item)
+
+    for item in range(3):
+        line.take(depth - 3, item)
+    for copy in heads + halves[0] + halves[1] + halves[2]:
         copy.wait_send()
+    line.close()
     for block in range(blocks):
-        for k in range(3):
-            dispatch(block, k).wait_send()
-            giveback(block, k).wait_send()
+        for k, kind in every:
+            dispatch(block, k, kind).wait_send()
+            giveback(block, k, kind).wait_send()
 
 
 def expert_layer(
     experts, routes, rows, attended, x_all, cot_own, ctl, w_own, w_sib, small_all, w_gate,
-    w_up, w_down,
+    w_up, w_down, g_rows,
 ):
     mine, width = cot_own.shape
     blocks = mine // rows
@@ -1007,42 +1147,52 @@
     vmem = pl.BlockSpec(memory_space=pltpu.VMEM)
     total = blocks * peers * LANES
     grads = [(2 * w.shape[0], w.shape[1]) for w in (w_gate, w_up, w_down)]
+    depth = lax.axis_size("dp")
+    parts = [(dims[0] // (2 * depth), dims[1]) for dims in grads]
+    sums = 3 * depth + 6 * (depth - 2)
     return pl.pallas_call(
         functools.partial(layer_kernel, experts, routes, rows, blocks),
-        in_specs=[vmem] * 10,
+        in_specs=[vmem] * 11,
         out_specs=[vmem] * 8,
         out_shape=[
             shape((blocks, rows, width), BF16), shape((blocks, 8, rows), F32),
             shape((mine, width), F32), shape((mine, width), BF16), shape((SMALL, width), F32),
         ]
-        + [shape(dims, BF16) for dims in grads],
-        scratch_shapes=[pltpu.VMEM((LANES, width), BF16)]
+        + [shape((depth,) + part, BF16) for part in parts],
+        scratch_shapes=[pltpu.VMEM(dims, BF16) for dims in grads]
+        + [pltpu.VMEM((depth,) + part, BF16) for part in parts]
+        + [pltpu.VMEM((2, depth - 2) + part, BF16) for part in parts]
+        + [pltpu.VMEM((LANES, width), BF16)]
         + [pltpu.VMEM((mine, span), BF16)] * 2
         + [pltpu.VMEM(dims, BF16) for dims in grads]
         + [
             pltpu.VMEM((mine, width), F32), pltpu.VMEM((mine, width), BF16),
             pltpu.VMEM((mine, LANES), F32), pltpu.VMEM((mine, experts * LANES), BF16),
-            pltpu.VMEM((blocks, experts, KINDS, LANES, width), BF16),
+            pltpu.VMEM((blocks, experts, LANES, width), BF16),
+            pltpu.VMEM((blocks, experts, 8, LANES), F32), pltpu.VMEM((blocks, peers, 8, LANES), F32),
+            pltpu.VMEM((blocks, peers, LANES, width), BF16),
         ]
-        + [pltpu.VMEM((blocks, peers, KINDS, LANES, width), BF16)] * 3
+        + [pltpu.VMEM((blocks, peers, KINDS, LANES, width), BF16)] * 2
         + [pltpu.VMEM((total, hidden), BF16)] * 3
+        + [pltpu.VMEM((total, width), BF16)]
         + [
             pltpu.SemaphoreType.DMA((4,)), pltpu.SemaphoreType.DMA((4,)),
             pltpu.SemaphoreType.DMA((4,)),
         ]
-        + [pltpu.SemaphoreType.DMA((blocks, 3))] * 4,
+        + [pltpu.SemaphoreType.DMA((blocks, 3, KINDS))] * 4
+        + [pltpu.SemaphoreType.DMA((sums,))] * 2,
         compiler_params=pltpu.CompilerParams(
             collective_id=2, has_side_effects=True, vmem_limit_bytes=62 * 1024 * 1024
         ),
         name="expert_layer",
     )(
         attended.reshape(2, mine, span), x_all, cot_own, ctl, w_own, w_sib, small_all,
-        w_gate, w_up, w_down,
+        w_gate, w_up, w_down, g_rows,
     )
 
 
 class Line:
-    def __init__(self, mail, depth, slots):
+    def __init__(self, mail, depth, slots, steps):
         self.depth = depth
         self.slots = slots
         self.place = lax.axis_index("dp")
@@ -1051,7 +1201,7 @@
         for way in range(2):
             step_to = 1 if way == 0 else -1
             device = (y * 2 + x, z + step_to, core)
-            for step in range(depth - 1):
+            for step in range(steps):
                 for item, (acc, landing) in enumerate(slots):
                     shard = self.shard(way, step)
                     safe = jnp.clip(shard, 0, depth - 1)
@@ -1121,6 +1271,51 @@
         for (way, step, item), copy in self.copies.items():
 
             @pl.when(self.sends(way, step))
+            def _():
+                copy.wait_send()
+
+
+class Final:
+    def __init__(self, mail, depth, slots):
+        self.place = lax.axis_index("dp")
+        self.depth = depth
+        self.slots = slots
+        y, x, z, core = position()
+        self.copies = {}
+        for way in range(2):
+            target = z + (1 if way == 0 else -1)
+            safe = jnp.clip(target, 0, depth - 1)
+            for item, (acc, landing, _) in enumerate(slots):
+                self.copies[way, item] = mail.copy(
+                    acc.at[safe], landing.at[way], (y * 2 + x, target, core)
+                )
+
+    def sends(self, way):
+        return self.place < self.depth - 1 if way == 0 else self.place > 0
+
+    def gets(self, way):
+        return self.place > 0 if way == 0 else self.place < self.depth - 1
+
+    def start(self):
+        for (way, item), copy in self.copies.items():
+
+            @pl.when(self.sends(way))
+            def _():
+                copy.start()
+
+    def finish(self, item):
+        _, landing, result = self.slots[item]
+        for way in range(2):
+
+            @pl.when(self.gets(way))
+            def _():
+                self.copies[way, item].wait_recv()
+                result[0] = result[0] + landing[way].astype(F32)
+
+    def close(self):
+        for (way, item), copy in self.copies.items():
+
+            @pl.when(self.sends(way))
             def _():
                 copy.wait_send()
 
@@ -1240,8 +1435,7 @@
         gate_any, up_any, down_any, branch_any, wout_any, att_any, qkv_any, segc_any, normed_any,
         wqkv_any, x_any, dres_any, out_ref, prev_ref, lse_ref, segr_ref, small_ref, small_rows,
         gate_out, up_out, down_out, qkv_out, wout_out, small_out, out_home, dtok_home, prev_home,
-        gate_land, up_land, down_land, gate_acc, up_acc, down_acc, gate_line, up_line, down_line,
-        branch_ref, wout_ref, att_ref, qkv_ref, segc_ref, normed_ref, wqkv_ref, x_ref, dres_ref,
+        gate_land, up_land, down_land, gate_own, up_own, down_own, branch_ref, wout_ref, att_ref, qkv_ref, segc_ref, normed_ref, wqkv_ref, x_ref, dres_ref,
         normed_turned, datt_ref, turned_ref, dqkv_ref, dk_sum, dv_sum, dn_send, dn_recv, dtok_ref,
         dense_ref, y1_land, x1_land, y1_acc, x1_acc, x2_land, y2_land, dense_acc, dense_line,
         tail_ref, ty1_land, tx1_land, ty1_acc, tx1_acc, tx2_land, ty2_land, tail_acc, tail_line,
@@ -1268,20 +1462,20 @@
     span = wout_ref.shape[0]
     pairs = span // LANES
     own_rows = pl.ds(pl.multiple_of(core * mine, mine), mine)
-    experts = [
-        (gate_any, gate_land, gate_acc, gate_line, gate_out),
-        (up_any, up_land, up_acc, up_line, up_out),
-        (down_any, down_land, down_acc, down_line, down_out),
-    ]
-    halves = [mail.copy(source.at[:, 1 - core], land, sibling) for source, land, _, _, _ in experts]
-    line = Line(mail, depth, [(acc, landing) for _, _, acc, landing, _ in experts])
+    final = Final(
+        mail, depth,
+        [
+            (gate_any, gate_land, gate_out), (up_any, up_land, up_out),
+            (down_any, down_land, down_out),
+        ],
+    )
     branch_copy = mail.copy(branch_any, branch_ref.at[own_rows], sibling)
     loads = [
         pltpu.make_async_copy(source, target, local_sems.at[k])
         for k, (source, target) in enumerate(
             [
-                (gate_any.at[:, core], gate_acc), (up_any.at[:, core], up_acc),
-                (down_any.at[:, core], down_acc), (branch_any, branch_ref.at[own_rows]),
+                (gate_any.at[z], gate_own), (up_any.at[z], up_own),
+                (down_any.at[z], down_own), (branch_any, branch_ref.at[own_rows]),
                 (normed_any, normed_ref), (att_any, att_ref), (wout_any, wout_ref),
                 (segc_any, segc_ref), (qkv_any, qkv_ref), (wqkv_any, wqkv_ref),
                 (x_any.at[own_rows], x_ref), (dres_any, dres_ref),
@@ -1321,6 +1515,7 @@
     dense = Line(
         mail, depth,
         [(dense_acc.at[c], dense_line.at[c]) for c in range(pairs + 1)] + [(tail_acc, tail_line)],
+        depth - 1,
     )
     chunks = pairs + 2
     size = tail_sum.shape[0]
@@ -1331,9 +1526,9 @@
     lasts = [mail.copy(a.at[other], b, sibling) for a, b in sums]
     dn_copies = [mail.copy(dn_send.at[b], dn_recv.at[b], sibling) for b in range(2)]
 
-    for copy in halves[:1] + [branch_copy] + halves[1:]:
-        copy.start()
-    for copy in loads:
+    branch_copy.start()
+    final.start()
+    for copy in loads[3:] + loads[:3]:
         copy.start()
     fars[0].start()
     fars[1].start()
@@ -1342,14 +1537,6 @@
 
     loads[4].wait()
     normed_turned[...] = normed_ref[...].T
-    for item, (_, land, acc, _, _) in enumerate(experts):
-        loads[item].wait()
-        halves[item].wait_recv()
-        for shard in range(depth):
-            acc[shard] = (acc[shard].astype(F32) + land[shard].astype(F32)).astype(BF16)
-        line.send(0, item)
-    for item in range(3):
-        line.send_edge(1, item)
     for k in (3, 5, 6, 7):
         loads[k].wait()
     branch_copy.wait_recv()
@@ -1403,9 +1590,6 @@
                 if now == 0:
                     half_copy.wait_recv()
                     planes[0].start()
-                    for item in range(2):
-                        line.take(0, item)
-                        line.send(1, item)
                 if now >= 1:
                     planes[now - 1].middle()
                 if now >= 2:
@@ -1413,13 +1597,6 @@
                     dense.send(0, now - 2)
                     for step in range(1, depth - 1):
                         dense.send_edge(step, now - 2)
-                if now == 1:
-                    line.take(0, 2)
-                    line.send(1, 2)
-                if now == 2:
-                    for item in range(2):
-                        line.take(1, item)
-                        line.send(2, item)
 
     small_all = small_rows[...].astype(F32)
     gain_column = column(widen(small_all), SMALL - 2)
@@ -1447,8 +1624,6 @@
         dn_copies[step].start()
     planes[pairs - 1].middle()
     launch(pairs - 2)
-    for item in range(3):
-        line.send_edge(2, item)
     planes[pairs].middle()
     launch(pairs - 1)
     planes[pairs + 1].middle()
@@ -1473,18 +1648,16 @@
             launch(pairs + 1)
         else:
             go_near(2)
-    line.take(1, 2)
-    line.send(2, 2)
+    for item, (own, result) in enumerate(
+        ((gate_own, gate_out), (up_own, up_out), (down_own, down_out))
+    ):
+        loads[item].wait()
+        result[0] = own[...].astype(F32)
+        final.finish(item)
     for step in range(depth - 2):
         for c in range(chunks):
             dense.take(step, c)
             dense.send(step + 1, c)
-    for item, (_, _, _, _, result) in enumerate(experts):
-
-        def store(value, add=False):
-            result[0] = result[0] + value if add else value
-
-        line.finish(item, store)
     for c, (total, _) in enumerate(sums):
 
         def store(value, add=False):
@@ -1508,11 +1681,11 @@
                     ]
         else:
             small_out[...] = own + theirs
-    for copy in halves + [branch_copy, half_copy] + lasts + dn_copies:
+    for copy in [branch_copy, half_copy] + lasts + dn_copies:
         copy.wait_send()
     for plane in planes:
         plane.close()
-    line.close()
+    final.close()
     dense.close()
     for copy in fars:
         copy.wait()
@@ -1533,10 +1706,6 @@
     x_all, d_residual, block_out, d_prev, lse, seg_row, small, small_all,
 ):
     depth = lax.axis_size("dp")
-    experts = [
-        grad.reshape(depth, 2, grad.shape[0] // (2 * depth), grad.shape[1])
-        for grad in (grad_gate, grad_up, grad_down)
-    ]
     length, width = x_all.shape
     mine = length // 2
     span = width // 2
@@ -1545,13 +1714,13 @@
     wide = 3 * LANES
     quarter = width // 4
     size = quarter // depth
-    parts = [grad.shape[2:] for grad in experts]
+    parts = [grad.shape[1:] for grad in (grad_gate, grad_up, grad_down)]
     vmem = pl.BlockSpec(memory_space=pltpu.VMEM)
     anywhere = pl.BlockSpec(memory_space=pl.ANY)
     homes = [block_out.shape, block_out.shape, d_prev.shape]
     kinds = [block_out.dtype, BF16, d_prev.dtype]
     steps = 2 * (depth - 1)
-    copies = 3 + 3 * steps + 2 + 6 + (groups + 1) * (4 + steps + 1) + 2
+    copies = 6 + 2 + 6 + (groups + 1) * (4 + steps + 1) + 2
 
     def plane_buffers(lead, columns):
         return [
@@ -1570,8 +1739,8 @@
         + [shape((size // 2, 6 * span), F32), shape((size // 2, width), F32)]
         + [shape((size // 2, LANES), F32)]
         + [shape(dims, kind) for dims, kind in zip(homes, kinds)],
-        scratch_shapes=[pltpu.VMEM((depth,) + part, BF16) for part in parts] * 2
-        + [pltpu.VMEM((2, depth - 1) + part, BF16) for part in parts]
+        scratch_shapes=[pltpu.VMEM((2,) + part, BF16) for part in parts]
+        + [pltpu.VMEM(part, BF16) for part in parts]
         + [
             pltpu.VMEM((length, width), BF16), pltpu.VMEM((span, width), BF16),
             pltpu.VMEM((length, span), BF16), pltpu.VMEM((length, 3 * span), BF16),
@@ -1598,7 +1767,7 @@
         ),
         name="back_all",
     )(
-        *experts, d_branch, w_out, attended, qkv, seg_col, normed, qkv_weight, x_all, d_residual,
+        grad_gate, grad_up, grad_down, d_branch, w_out, attended, qkv, seg_col, normed, qkv_weight, x_all, d_residual,
         block_out, d_prev, lse, seg_row, small, small_all,
     )
 
@@ -1669,16 +1838,16 @@
     experts = route_count - 4
     (
         x_all, cot_own, ctl, normed, qkv, attended, lse, small_all, qkv_weight, out_sib,
-        seg_col, seg_row,
+        seg_col, seg_row, g_rows,
     ) = gather_all(
-        tokens, cotangent, w_qkv, w_out, prev_logits, routes, segments, w_router, const_proj,
+        experts, tokens, cotangent, w_qkv, w_out, prev_logits, routes, segments, w_router, const_proj,
         const_vec, gain_attn, gain_moe,
     )
     (
         block_out, d_prev, d_residual, d_branch, small, grad_gate, grad_up, grad_down,
     ) = expert_layer(
         experts, route_count, rows, attended, x_all, cot_own, ctl, w_out, out_sib, small_all,
-        w_gate[0], w_up[0], w_down[0],
+        w_gate[0], w_up[0], w_down[0], g_rows,
     )
 
     (
@@ -1710,7 +1879,7 @@
         peers == 4
         and mesh.shape["fs"] == 2
         and micro == 2
-        and mesh.shape["dp"] % 2 == 0
+        and mesh.shape["dp"] == 4
         and (routes - 4) * 2 == peers
         and 3 * rows // routes == LANES
         and tokens.shape[2] % (2 * LANES) == 0

time: 196 us -> 180 us (0.918)
  Pallas kernels: 195 us -> 179 us
    pallas_call x1, Pallas kernels: 87.3 us -> 71.6 us  [expert_layer(): pl.pallas_call(functools.partial(layer_kernel, experts, routes, rows, blo...]
    pallas_call x1, Pallas kernels: 70.8 us -> 58 us  [back_all(): pl.pallas_call(functools.partial(back_kernel, depth, rows, length // 2),...]
    pallas_call x1, Pallas kernels: 32.6 us -> 45.4 us  [gather_all(): pl.pallas_call(functools.partial(gather_kernel, rows, length // 2, w_rout...]
where the time goes in v4:
time: 180 us
  Pallas kernels  179 us (99%)
    pallas_call x1, Pallas kernels, expert_layer(): pl.pallas_call(functools.partial(layer_kernel, experts, routes, rows, blo...  71.6 us
    pallas_call x1, Pallas kernels, back_all(): pl.pallas_call(functools.partial(back_kernel, depth, rows, length // 2),...  58 us
    pallas_call x1, Pallas kernels, gather_all(): pl.pallas_call(functools.partial(gather_kernel, rows, length // 2, w_rout...  45.4 us
    pallas_call x1, Pallas kernels, deliver(): pl.pallas_call(functools.partial(deliver_kernel, routes), in_specs=[vmem]...  3.84 us

profile of v4, /device:TPU:0, one launch (start us, length us, event | category | flops | bytes accessed | tf_op | source)
XLA Modules:
  0.0 179.7 jit_solution(2784069032598841465)
XLA Ops:
  0.6 45.4 %gather_all.1 = (bf16[1024,768]{1,0:T(8,128)(2,1)}, bf16[512,768]{1,0:T(8,128)(2,1)}, f32[2,16,256]{2,1,0:T(8,128)}, bf16[1024,768]{1,0:T(8,128)(2,1)}, bf16[102...) custom-call(bf16[2,256,768]{2,1,0:T(8,128)(2,1)} %tok_ref.1, ...), custom_call_target="tpu_custom_call" | custom-call | tf_op jit(solution)/shard_map/gather_all/pallas_call | solution.py:755
  46.1 71.6 %expert_layer.1 = (bf16[2,256,768]{2,1,0:T(8,128)(2,1)}, f32[2,8,256]{2,1,0:T(8,128)}, f32[512,768]{1,0:T(8,128)}, bf16[512,768]{1,0:T(8,128)(2,1)}, f32[16,768]...) custom-call(bf16[2,512,384]{2,1,0:T(8,128)(2,1)} %bitcast.13, ...), custom_call_target="tpu_custom_call" | custom-call | tf_op jit(solution)/shard_map/expert_layer/pallas_call | solution.py:1153
  117.7 58.0 %back_all.1 = (f32[1,96,1024]{2,1,0:T(8,128)}, f32[1,96,1024]{2,1,0:T(8,128)}, f32[1,128,768]{2,1,0:T(8,128)}, f32[24,2304]{1,0:T(8,128)}, f32[24,768]{1,0:T(8,1...) custom-call(bf16[4,96,1024]{2,1,0:T(8,128)(2,1)} %get-tuple-element., ...), custom_call_target="tpu_custom_call" | custom-call | tf_op jit(solution)/shard_map/back_all/pallas_call | solution.py:1734
  175.7 3.8 %deliver.1 = (bf16[2,256,768]{2,1,0:T(8,128)(2,1)}, f32[2,256,768]{2,1,0:T(8,128)}, f32[6,2,256]{2,1,0:T(2,128)}, f32[24]{0:T(128)}, f32[24,2304]{1,0:T(8,128)},...) custom-call(bf16[2,256,768]{2,1,0:T(8,128)(2,1)} %get-tuple-element., ...), custom_call_target="tpu_custom_call" | custom-call | flops 1000000 | bytes 8000000 | tf_op jit(solution)/shard_map/deliver/pallas_call | solution.py:1802

commit v5 on v4

--- a/solution.py
+++ b/solution.py
@@ -496,21 +496,29 @@
         start, width = key_span(block, rows, reach)
         here = pl.ds(block * rows, rows)
         there = pl.ds(start, width)
-        queries = qkv_ref[here, at_q]
+        queries = qkv_ref[here, at_q] * 0.125
         keys = qkv_ref[there, at_k]
         values = qkv_ref[there, at_v]
         seg_q = segc_ref[here, 0:1]
         seg_k = segr_ref[0:1, there]
-        row_pos = block * rows + lax.broadcasted_iota(jnp.int32, (rows, width), 0)
-        col_pos = start + lax.broadcasted_iota(jnp.int32, (rows, width), 1)
-        allowed = (seg_q == seg_k) & (col_pos <= row_pos)
+        past = width - rows
+        order = lax.broadcasted_iota(jnp.int32, (rows, rows), 1) <= lax.broadcasted_iota(
+            jnp.int32, (rows, rows), 0
+        )
+
+        def masked(scores):
+            near = jnp.where((seg_q == seg_k[:, past:]) & order, scores[:, past:], NEG)
+            if past == 0:
+                return near
+            far = jnp.where(seg_q == seg_k[:, :past], scores[:, :past], NEG)
+            return jnp.concatenate([far, near], axis=1)
+
         lane = lax.broadcasted_iota(jnp.int32, (rows, LANES), 1)
         outs = []
         logs = []
         for head in range(2):
             mine = (lane // HEAD) == head
-            scores = dot(jnp.where(mine, queries, 0), keys, ((1,), (1,))) * 0.125
-            scores = jnp.where(allowed, scores, NEG)
+            scores = masked(dot(jnp.where(mine, queries, 0), keys, ((1,), (1,))))
             largest = jnp.max(scores, axis=-1, keepdims=True)
             powers = jnp.exp(scores - largest)
             total = jnp.sum(powers, axis=-1, keepdims=True)
@@ -528,9 +536,9 @@
     rows, reach, routes, experts,
     tok_ref, cot_ref, wqkv_ref, wout_ref, prev_ref, route_ref, seg_ref, router_ref, cproj_ref,
     cvec_ref, gain_a_ref, gain_m_ref,
-    x_all, cot_own, ctl_own, normed_ref, qkv_ref, att_ref, lse_ref, small_all, wqkv_all,
+    x_out, ctl_own, normed_out, qkv_out, att_ref, lse_ref, small_all, wqkv_out,
     wout_sib, segc_ref, segr_ref, g_rows,
-    cot_wide, g_send, ctl_send, small_wide, small_send, seg_all,
+    x_all, normed_ref, qkv_ref, wqkv_all, cot_wide, g_send, ctl_send, small_wide, small_send, seg_all,
     near_send, near_recv, far_send, far_recv, core_send, core_recv, local_sems,
     pack_send, pack_recv,
 ):
@@ -566,10 +574,8 @@
     def block_of(index):
         return pl.ds(pl.multiple_of(index * rows, rows), rows)
 
-    within = block_of(x)
     homes = [
         (tok_ref, x_all.at[block_of(me)]),
-        (cot_ref, cot_own.at[within]),
         (ctl_send, ctl_own.at[x]),
     ]
     nears = Mail(near_send, near_recv)
@@ -644,7 +650,7 @@
         for route in range(routes):
             ctl_send[m, route : route + 1, :] = prev_ref[route, m : m + 1, :]
         ctl_send[m, 8:10, :] = route_ref[m].astype(F32)
-    send(2)
+    send(1)
     cot_load.wait()
     earlier = lax.broadcasted_iota(jnp.int32, (rows, rows), 0) < lax.broadcasted_iota(
         jnp.int32, (rows, rows), 1
@@ -657,16 +663,19 @@
         for expert in range(experts):
             hit = (slot == rank[expert : expert + 1, :]) & (chosen[expert : expert + 1, :] > 0.0)
             g_send[m, expert] = dot(hit.astype(BF16), cot_wide[m]).astype(BF16)
-        for k in range(1, 4):
-            pack(m, k).start()
-
-        @pl.when(moved)
-        def _():
-            pack(m, 0).start()
-
-        @pl.when(jnp.logical_not(moved))
-        def _():
-            pack_stays[m].start()
+
+    def send_packs():
+        for m in range(2):
+            for k in range(1, 4):
+                pack(m, k).start()
+
+            @pl.when(moved)
+            def _():
+                pack(m, 0).start()
+
+            @pl.when(jnp.logical_not(moved))
+            def _():
+                pack_stays[m].start()
 
     seg_copy.wait_recv()
     seg_own.wait()
@@ -698,20 +707,34 @@
     project(core * 2 + x)
     far_copies[0].wait_recv()
     forward[1].start()
-    send(1)
+    send_packs()
     project(core * 2 + 1 - x)
     forward[0].wait_recv()
     project((1 - core) * 2 + x)
     forward[1].wait_recv()
     project((1 - core) * 2 + 1 - x)
 
+    own_rows = pl.ds(pl.multiple_of(core * 2 * rows, rows), 2 * rows)
+    results = [
+        pltpu.make_async_copy(source, target, local_sems.at[10 + k])
+        for k, (source, target) in enumerate(
+            (
+                (x_all.at[own_rows], x_out), (normed_ref, normed_out), (qkv_ref, qkv_out),
+                (wqkv_all, wqkv_out),
+            )
+        )
+    ]
+    for copy in results:
+        copy.start()
+
     @pl.loop(0, span // LANES)
     def _(pair):
         attend_pair(pair, rows, reach, span, qkv_ref, segc_ref, segr_ref, att_ref, lse_ref)
 
-    for k in (1, 2):
-        take_near(k)
-        far_copies[k].wait_recv()
+    for copy in results:
+        copy.wait()
+    take_near(1)
+    far_copies[1].wait_recv()
     for there in range(2):
         for peer in range(4):
             kept = (y == core) & (x == there) & (core == peer // 2)
@@ -748,16 +771,17 @@
 ):
     rows, width = tokens.shape[1:]
     length = segments.shape[1]
-    mine = length // 2
     span = width // 2
     vmem = pl.BlockSpec(memory_space=pltpu.VMEM)
     anywhere = pl.BlockSpec(memory_space=pl.ANY)
     return pl.pallas_call(
         functools.partial(gather_kernel, rows, length // 2, w_router.shape[1], experts),
         in_specs=[anywhere] * 4 + [vmem] * 8,
-        out_specs=[vmem] * 13,
+        out_specs=[anywhere, vmem, anywhere, anywhere, vmem, vmem, vmem, anywhere, anywhere]
+        + [vmem] * 2
+        + [anywhere],
         out_shape=[
-            shape((length, width), BF16), shape((mine, width), BF16),
+            shape((length // 2, width), BF16),
             shape((2, SMALL, rows), F32), shape((length, width), BF16),
             shape((length, 3 * span), BF16), shape((length, span), BF16),
             shape((span // LANES, 8, length), F32), shape((SMALL, width), BF16),
@@ -766,6 +790,8 @@
             shape((2, 4, LANES, width), BF16),
         ],
         scratch_shapes=[
+            pltpu.VMEM((length, width), BF16), pltpu.VMEM((length, width), BF16),
+            pltpu.VMEM((length, 3 * span), BF16), pltpu.VMEM((width, 3 * span), BF16),
             pltpu.VMEM((2, rows, width), BF16), pltpu.VMEM((2, experts, LANES, width), BF16),
             pltpu.VMEM((2, SMALL, rows), F32),
             pltpu.VMEM((SMALL, span), F32), pltpu.VMEM((SMALL, span), BF16),
@@ -773,7 +799,7 @@
         ]
         + [pltpu.SemaphoreType.DMA((3,))] * 4
         + [pltpu.SemaphoreType.DMA((8,))] * 2
-        + [pltpu.SemaphoreType.DMA((10,))]
+        + [pltpu.SemaphoreType.DMA((14,))]
         + [pltpu.SemaphoreType.DMA((2, 4))] * 2,
         compiler_params=pltpu.CompilerParams(
             collective_id=3, has_side_effects=True, vmem_limit_bytes=60 * 1024 * 1024
@@ -798,7 +824,7 @@
     residual_ref, mixed_ref, pm_ref, place_ref = keep
     y, x, z, core = position()
     here = pl.ds(pl.multiple_of(block * rows, rows), rows)
-    tokens = x_ref[pl.ds(pl.multiple_of((core * 2 + block) * rows, rows), rows), :]
+    tokens = x_ref[here, :]
     residual = tokens.astype(F32) + (
         dot(att_own[here, :], w_own[...]) + dot(att_sib[here, :], w_sib[...])
     )
@@ -880,7 +906,7 @@
     back_ref[block, y * 2 + x] = result_ref[block, y * 2 + x]
 
 
-def combine_block(experts, routes, rows, block, refs, keep, back_ref, outs, small_ref):
+def combine_forward(experts, routes, rows, block, refs, keep, back_ref, outs, small_ref):
     g_ref, ctl_ref, small_rows, wide_rows = refs
     residual_ref, mixed_ref, pm_ref, place_ref = keep
     out_ref, prev_ref, dres_ref, branch_ref = outs
@@ -897,16 +923,12 @@
     gated = chosen * probs
     d_probs = jnp.zeros((rows, LANES), F32)
     result = residual
-    d_mixed = None
     for expert in range(experts):
         place = place_ref[here, expert * LANES : (expert + 1) * LANES]
         expert_out = None
         for half in range(halves):
-            owner = expert * halves + half
-            term = dot(place, back_ref[block, owner, 0])
+            term = dot(place, back_ref[block, expert * halves + half, 0])
             expert_out = term if expert_out is None else expert_out + term
-            term = dot(place, back_ref[block, owner, 1])
-            d_mixed = term if d_mixed is None else d_mixed + term
         result = result + column(gated, expert) * expert_out
         d_gate = jnp.sum(expert_out * grads, axis=-1, keepdims=True)
         d_probs = jnp.where(lane == expert, d_gate, d_probs)
@@ -937,37 +959,51 @@
     d_probs = d_probs * chosen
     d_logits = probs * (d_probs - jnp.sum(probs * d_probs, axis=-1, keepdims=True))
     d_small = jnp.where(lane < routes, d_logits, d_small)
-    d_mixed = d_mixed + weight * grads
-    d_mixed = d_mixed + dot(
+    dres_ref[here, :] = weight * grads + dot(
         jnp.where(lane < 12, d_small, 0.0), wide_rows[...].astype(F32), precision=HIGHEST
     )
+    d_turned = d_small.T[:SMALL, :]
+    prev_ref[block] = d_turned[:8, :]
+    sub = lax.broadcasted_iota(jnp.int32, (SMALL, rows), 0)
+    small = dot(jnp.where(sub < 12, d_turned, 0.0), mixed, precision=HIGHEST)
+    small_ref[...] += small + dot(
+        jnp.where((sub >= 12) & (sub < 14), d_turned, 0.0), grads, precision=HIGHEST
+    )
+
+
+def combine_backward(experts, rows, block, refs, keep, back_ref, outs, small_ref):
+    g_ref, ctl_ref, small_rows, wide_rows = refs
+    residual_ref, mixed_ref, pm_ref, place_ref = keep
+    out_ref, prev_ref, dres_ref, branch_ref = outs
+    halves = back_ref.shape[1] // experts
+    here = pl.ds(pl.multiple_of(block * rows, rows), rows)
+    grads = g_ref[here, :].astype(F32)
+    residual = residual_ref[here, :]
+    d_mixed = dres_ref[here, :]
+    for expert in range(experts):
+        place = place_ref[here, expert * LANES : (expert + 1) * LANES]
+        for half in range(halves):
+            d_mixed = d_mixed + dot(place, back_ref[block, expert * halves + half, 1])
     inverse = lax.rsqrt(jnp.mean(residual * residual, axis=-1, keepdims=True) + NORM_EPS)
     scaled = d_mixed * small_rows[15:16, :].astype(F32)
     mean = jnp.mean(scaled * residual, axis=-1, keepdims=True)
     d_residual = grads + inverse * scaled - residual * (inverse * inverse * inverse * mean)
     dres_ref[here, :] = d_residual
     branch_ref[here, :] = d_residual.astype(BF16)
-    d_turned = d_small.T[:SMALL, :]
-    prev_ref[block] = d_turned[:8, :]
-    sub = lax.broadcasted_iota(jnp.int32, (SMALL, rows), 0)
-    small = dot(jnp.where(sub < 12, d_turned, 0.0), mixed, precision=HIGHEST)
-    small = small + dot(
-        jnp.where((sub >= 12) & (sub < 14), d_turned, 0.0), grads, precision=HIGHEST
-    )
-    d_gain = jnp.sum(d_mixed * residual * inverse, axis=0, keepdims=True)
-    which = lax.broadcasted_iota(jnp.int32, small.shape, 0)
-    small_ref[...] += jnp.where(which == 14, d_gain, small)
+    small_ref[14:15, :] += jnp.sum(d_mixed * residual * inverse, axis=0, keepdims=True)
 
 
 def layer_kernel(
     experts, routes, rows, blocks,
-    att_ref, x_ref, g_ref, ctl_ref, w_own, w_sib, small_rows, gate_ref, up_ref, down_ref, g_rows,
+    ctl_ref, small_rows, att_ref, cot_ref, x_any, own_any, sib_any, g_any, gate_ref, up_ref,
+    down_ref,
     out_ref, prev_ref, dres_ref, branch_ref, small_ref, gate_acc, up_acc, down_acc,
     dgate_out, dup_out, ddown_out, gate_land, up_land, down_land, gate_line, up_line, down_line,
     wide_rows, att_own, att_sib, gate_w, up_w, down_w, residual_ref, mixed_ref, pm_ref, place_ref,
     send_ref, gate_send, gate_recv, recv_ref, result_ref, back_ref, hidden_ref, d_gate_ref,
-    d_up_ref, d_rows_ref,
+    d_up_ref, d_rows_ref, g_ref, x_ref, w_own, w_sib, g_rows,
     head_send, head_recv, local_sems, send_sems, recv_sems, back_send, back_recv, sum_send, sum_recv,
+    g_sends, g_recvs,
 ):
     y, x, z, core = position()
     me = y * 2 + x
@@ -975,10 +1011,27 @@
     partners = [(1 - y) * 2 + 1 - x, y * 2 + 1 - x, (1 - y) * 2 + x]
     wanted = [1 - y, y, 1 - y]
     depth = lax.axis_size("dp")
+    plane = [((y + k // 2) % 2 * 2 + (x + k) % 2) for k in range(4)]
     greet(
-        [(sibling, True)] + [((place, z, core), True) for place in partners]
+        [((plane[k], z, (core + c) % 2), True) for k in range(4) for c in range(2) if k + c > 0]
         + [((me, z + 1, core), z < depth - 1), ((me, z - 1, core), z > 0)]
     )
+    moved = y != core
+    g_place = g_ref.at[pl.ds(pl.multiple_of(x * rows, rows), rows)]
+    g_mail = Mail(g_sends, g_recvs)
+    g_near = g_mail.copy(cot_ref.at[x], g_place, ((1 - y) * 2 + x, z, 1 - core))
+    g_far = g_mail.copy(cot_ref.at[1 - x], g_place, (core * 2 + 1 - x, z, y))
+    g_stay = pltpu.make_async_copy(cot_ref.at[x], g_place, local_sems.at[4])
+    g_far.start()
+
+    @pl.when(moved)
+    def _():
+        g_near.start()
+
+    @pl.when(jnp.logical_not(moved))
+    def _():
+        g_stay.start()
+
     sums = Mail(sum_send, sum_recv)
     grads = [
         (dgate_out, gate_land, gate_acc, gate_line), (dup_out, up_land, up_acc, up_line),
@@ -996,7 +1049,7 @@
         ]
         for ref, land, _, _ in grads
     ]
-    line = Line(sums, depth, [(acc, landing) for _, _, acc, landing in grads], depth - 2)
+    line = Line(sums, depth, [(acc, landing) for _, _, acc, landing in grads], range(1))
 
     def add_halves(item):
         ref, land, acc, _ = grads[item]
@@ -1017,7 +1070,15 @@
         spot = target.at[pl.ds(pl.multiple_of(core * size, size), size)]
         heads.append(mail.copy(source, spot, sibling))
         locals_.append(pltpu.make_async_copy(source, spot, local_sems.at[k]))
-    for copy in heads + locals_:
+    loads = [
+        pltpu.make_async_copy(source, target, local_sems.at[5 + k])
+        for k, (source, target) in enumerate(
+            ((x_any, x_ref), (own_any, w_own), (sib_any, w_sib), (g_any, g_rows))
+        )
+    ]
+    heads[0].start()
+    locals_[0].start()
+    for copy in loads[:3] + heads[1:] + locals_[1:] + loads[3:]:
         copy.start()
 
     def dispatch(block, k, kind):
@@ -1047,6 +1108,8 @@
     wide_rows[0:SMALL, :] = small_rows[...]
     heads[0].wait_recv()
     locals_[0].wait()
+    for copy in loads[:3]:
+        copy.wait()
     keep = (residual_ref, mixed_ref, pm_ref, place_ref)
     spread_refs = (
         att_own, att_sib, x_ref, ctl_ref, w_own, w_sib, small_rows, wide_rows
@@ -1063,7 +1126,7 @@
 
     for copy in heads[1:]:
         copy.wait_recv()
-    for copy in locals_[1:]:
+    for copy in locals_[1:] + loads[3:]:
         copy.wait()
 
     @pl.loop(0, blocks)
@@ -1104,28 +1167,31 @@
         copy.start()
     for item in range(3):
         add_halves(item)
-    for step in range(1, depth - 2):
-        for item in range(3):
-            line.send_edge(step, item)
+    g_far.wait()
+
+    @pl.when(moved)
+    def _():
+        g_near.wait()
+
+    @pl.when(jnp.logical_not(moved))
+    def _():
+        g_stay.wait()
 
     @pl.loop(0, blocks)
     def _(block):
-        for k, kind in every:
-            giveback(block, k, kind).wait_recv()
-        combine_block(
-            experts, routes, rows, block, (g_ref, ctl_ref, small_rows, wide_rows),
-            keep, back_ref, (out_ref, prev_ref, dres_ref, branch_ref), small_ref,
-        )
-
-        @pl.when(block == 0)
-        def _():
-            for step in range(depth - 3):
-                for item in range(3):
-                    line.take(step, item)
-                    line.send(step + 1, item)
+        refs = (g_ref, ctl_ref, small_rows, wide_rows)
+        outs = (out_ref, prev_ref, dres_ref, branch_ref)
+        for k in range(3):
+            giveback(block, k, 0).wait_recv()
+        combine_forward(
+            experts, routes, rows, block, refs, keep, back_ref, outs, small_ref
+        )
+        for k in range(3):
+            giveback(block, k, 1).wait_recv()
+        combine_backward(experts, rows, block, refs, keep, back_ref, outs, small_ref)
 
     for item in range(3):
-        line.take(depth - 3, item)
+        line.take(0, item)
     for copy in heads + halves[0] + halves[1] + halves[2]:
         copy.wait_send()
     line.close()
@@ -1136,11 +1202,11 @@
 
 
 def expert_layer(
-    experts, routes, rows, attended, x_all, cot_own, ctl, w_own, w_sib, small_all, w_gate,
+    experts, routes, rows, attended, x_own, cot, ctl, w_own, w_sib, small_all, w_gate,
     w_up, w_down, g_rows,
 ):
-    mine, width = cot_own.shape
-    blocks = mine // rows
+    blocks, rows, width = cot.shape
+    mine = blocks * rows
     peers = lax.axis_size("ep")
     span = attended.shape[1]
     hidden = w_gate.shape[1]
@@ -1149,10 +1215,10 @@
     grads = [(2 * w.shape[0], w.shape[1]) for w in (w_gate, w_up, w_down)]
     depth = lax.axis_size("dp")
     parts = [(dims[0] // (2 * depth), dims[1]) for dims in grads]
-    sums = 3 * depth + 6 * (depth - 2)
+    sums = 3 * depth + 6
     return pl.pallas_call(
         functools.partial(layer_kernel, experts, routes, rows, blocks),
-        in_specs=[vmem] * 11,
+        in_specs=[vmem] * 2 + [pl.BlockSpec(memory_space=pl.ANY)] * 9,
         out_specs=[vmem] * 8,
         out_shape=[
             shape((blocks, rows, width), BF16), shape((blocks, 8, rows), F32),
@@ -1161,7 +1227,7 @@
         + [shape((depth,) + part, BF16) for part in parts],
         scratch_shapes=[pltpu.VMEM(dims, BF16) for dims in grads]
         + [pltpu.VMEM((depth,) + part, BF16) for part in parts]
-        + [pltpu.VMEM((2, depth - 2) + part, BF16) for part in parts]
+        + [pltpu.VMEM((2, 1) + part, BF16) for part in parts]
         + [pltpu.VMEM((LANES, width), BF16)]
         + [pltpu.VMEM((mine, span), BF16)] * 2
         + [pltpu.VMEM(dims, BF16) for dims in grads]
@@ -1174,20 +1240,24 @@
         ]
         + [pltpu.VMEM((blocks, peers, KINDS, LANES, width), BF16)] * 2
         + [pltpu.VMEM((total, hidden), BF16)] * 3
-        + [pltpu.VMEM((total, width), BF16)]
+        + [pltpu.VMEM((total, width), BF16), pltpu.VMEM((mine, width), BF16)]
+        + [pltpu.VMEM((mine, width), BF16)]
+        + [pltpu.VMEM((span, width), BF16)] * 2
+        + [pltpu.VMEM((blocks, peers, LANES, width), BF16)]
         + [
             pltpu.SemaphoreType.DMA((4,)), pltpu.SemaphoreType.DMA((4,)),
-            pltpu.SemaphoreType.DMA((4,)),
+            pltpu.SemaphoreType.DMA((9,)),
         ]
         + [pltpu.SemaphoreType.DMA((blocks, 3, KINDS))] * 4
-        + [pltpu.SemaphoreType.DMA((sums,))] * 2,
+        + [pltpu.SemaphoreType.DMA((sums,))] * 2
+        + [pltpu.SemaphoreType.DMA((2,))] * 2,
         compiler_params=pltpu.CompilerParams(
             collective_id=2, has_side_effects=True, vmem_limit_bytes=62 * 1024 * 1024
         ),
         name="expert_layer",
     )(
-        attended.reshape(2, mine, span), x_all, cot_own, ctl, w_own, w_sib, small_all,
-        w_gate, w_up, w_down, g_rows,
+        ctl, small_all, attended.reshape(2, mine, span), cot, x_own, w_own, w_sib, g_rows, w_gate,
+        w_up, w_down,
     )
 
 
@@ -1195,18 +1265,19 @@
     def __init__(self, mail, depth, slots, steps):
         self.depth = depth
         self.slots = slots
+        self.first = steps[0]
         self.place = lax.axis_index("dp")
         y, x, z, core = position()
         self.copies = {}
         for way in range(2):
             step_to = 1 if way == 0 else -1
             device = (y * 2 + x, z + step_to, core)
-            for step in range(steps):
+            for step in steps:
                 for item, (acc, landing) in enumerate(slots):
                     shard = self.shard(way, step)
                     safe = jnp.clip(shard, 0, depth - 1)
                     self.copies[way, step, item] = mail.copy(
-                        acc.at[safe], landing.at[way, step], device
+                        acc.at[safe], landing.at[way, step - self.first], device
                     )
 
     def shard(self, way, step):
@@ -1231,7 +1302,7 @@
     def send(self, step, item):
         for way in range(2):
             wanted = self.sends(way, step)
-            if step > 0:
+            if step > self.first:
                 wanted = wanted & jnp.logical_not(self.edge(way))
 
             @pl.when(wanted)
@@ -1254,7 +1325,7 @@
             def _():
                 self.copies[way, step, item].wait_recv()
                 acc[shard] = (
-                    acc[shard].astype(F32) + landing[way, step].astype(F32)
+                    acc[shard].astype(F32) + landing[way, step - self.first].astype(F32)
                 ).astype(BF16)
 
     def finish(self, item, store):
@@ -1265,57 +1336,12 @@
             @pl.when(self.gets(way, self.depth - 2))
             def _():
                 self.copies[way, self.depth - 2, item].wait_recv()
-                store(landing[way, self.depth - 2].astype(F32), True)
+                store(landing[way, self.depth - 2 - self.first].astype(F32), True)
 
     def close(self):
         for (way, step, item), copy in self.copies.items():
 
             @pl.when(self.sends(way, step))
-            def _():
-                copy.wait_send()
-
-
-class Final:
-    def __init__(self, mail, depth, slots):
-        self.place = lax.axis_index("dp")
-        self.depth = depth
-        self.slots = slots
-        y, x, z, core = position()
-        self.copies = {}
-        for way in range(2):
-            target = z + (1 if way == 0 else -1)
-            safe = jnp.clip(target, 0, depth - 1)
-            for item, (acc, landing, _) in enumerate(slots):
-                self.copies[way, item] = mail.copy(
-                    acc.at[safe], landing.at[way], (y * 2 + x, target, core)
-                )
-
-    def sends(self, way):
-        return self.place < self.depth - 1 if way == 0 else self.place > 0
-
-    def gets(self, way):
-        return self.place > 0 if way == 0 else self.place < self.depth - 1
-
-    def start(self):
-        for (way, item), copy in self.copies.items():
-
-            @pl.when(self.sends(way))
-            def _():
-                copy.start()
-
-    def finish(self, item):
-        _, landing, result = self.slots[item]
-        for way in range(2):
-
-            @pl.when(self.gets(way))
-            def _():
-                self.copies[way, item].wait_recv()
-                result[0] = result[0] + landing[way].astype(F32)
-
-    def close(self):
-        for (way, item), copy in self.copies.items():
-
-            @pl.when(self.sends(way))
             def _():
                 copy.wait_send()
 
@@ -1399,15 +1425,24 @@
         start, width = key_span(block, rows, reach)
         here = pl.ds(block * rows, rows)
         there = pl.ds(start, width)
-        queries = qkv_ref[here, at_q]
+        queries = qkv_ref[here, at_q] * 0.125
         grads = datt_ref[here, at_q]
         keys = qkv_ref[there, at_k]
         values = qkv_ref[there, at_v]
         seg_k = segc_ref[there, 0:1]
         seg_q = segr_ref[0:1, here]
-        key_pos = start + lax.broadcasted_iota(jnp.int32, (width, rows), 0)
-        query_pos = block * rows + lax.broadcasted_iota(jnp.int32, (width, rows), 1)
-        allowed = (seg_q == seg_k) & (key_pos <= query_pos)
+        past = width - rows
+        order = lax.broadcasted_iota(jnp.int32, (rows, rows), 0) <= lax.broadcasted_iota(
+            jnp.int32, (rows, rows), 1
+        )
+
+        def masked(scores):
+            near = jnp.where((seg_q == seg_k[past:]) & order, scores[past:], NEG)
+            if past == 0:
+                return near
+            far = jnp.where(seg_q == seg_k[:past], scores[:past], NEG)
+            return jnp.concatenate([far, near], axis=0)
+
         lane = lax.broadcasted_iota(jnp.int32, (rows, LANES), 1)
         dq_parts = []
         for head in range(2):
@@ -1415,8 +1450,7 @@
             head_q = jnp.where(mine, queries, 0)
             head_g = jnp.where(mine, grads, 0)
             log_total = lse_ref[pair, head : head + 1, here]
-            scores = dot(keys, head_q, ((1,), (1,))) * 0.125
-            probs = jnp.exp(jnp.where(allowed, scores, NEG) - log_total)
+            probs = jnp.exp(masked(dot(keys, head_q, ((1,), (1,)))) - log_total)
             d_probs = dot(values, head_g, ((1,), (1,)))
             delta = jnp.sum(probs * d_probs, axis=0, keepdims=True)
             d_scores = (probs * (d_probs - delta)).astype(BF16)
@@ -1426,7 +1460,7 @@
             dq_parts.append(dot(turned, d_scores))
         dq = jnp.concatenate(dq_parts, axis=0).T * 0.125
         dqkv_ref[here, at_q] = dq.astype(BF16)
-    dqkv_ref[:, at_k] = (dk_sum[...] * 0.125).astype(BF16)
+    dqkv_ref[:, at_k] = dk_sum[...].astype(BF16)
     dqkv_ref[:, at_v] = dv_sum[...].astype(BF16)
 
 
@@ -1435,7 +1469,7 @@
         gate_any, up_any, down_any, branch_any, wout_any, att_any, qkv_any, segc_any, normed_any,
         wqkv_any, x_any, dres_any, out_ref, prev_ref, lse_ref, segr_ref, small_ref, small_rows,
         gate_out, up_out, down_out, qkv_out, wout_out, small_out, out_home, dtok_home, prev_home,
-        gate_land, up_land, down_land, gate_own, up_own, down_own, branch_ref, wout_ref, att_ref, qkv_ref, segc_ref, normed_ref, wqkv_ref, x_ref, dres_ref,
+        gate_line, up_line, down_line, gate_acc, up_acc, down_acc, branch_ref, wout_ref, att_ref, qkv_ref, segc_ref, normed_ref, wqkv_ref, x_ref, dres_ref,
         normed_turned, datt_ref, turned_ref, dqkv_ref, dk_sum, dv_sum, dn_send, dn_recv, dtok_ref,
         dense_ref, y1_land, x1_land, y1_acc, x1_acc, x2_land, y2_land, dense_acc, dense_line,
         tail_ref, ty1_land, tx1_land, ty1_acc, tx1_acc, tx2_land, ty2_land, tail_acc, tail_line,
@@ -1462,23 +1496,21 @@
     span = wout_ref.shape[0]
     pairs = span // LANES
     own_rows = pl.ds(pl.multiple_of(core * mine, mine), mine)
-    final = Final(
-        mail, depth,
-        [
-            (gate_any, gate_land, gate_out), (up_any, up_land, up_out),
-            (down_any, down_land, down_out),
-        ],
+    shares = [
+        (gate_acc, gate_line, gate_out), (up_acc, up_line, up_out), (down_acc, down_line, down_out)
+    ]
+    line = Line(
+        mail, depth, [(acc, landing) for acc, landing, _ in shares], range(1, depth - 1)
     )
     branch_copy = mail.copy(branch_any, branch_ref.at[own_rows], sibling)
     loads = [
         pltpu.make_async_copy(source, target, local_sems.at[k])
         for k, (source, target) in enumerate(
             [
-                (gate_any.at[z], gate_own), (up_any.at[z], up_own),
-                (down_any.at[z], down_own), (branch_any, branch_ref.at[own_rows]),
+                (gate_any, gate_acc), (up_any, up_acc), (down_any, down_acc), (branch_any, branch_ref.at[own_rows]),
                 (normed_any, normed_ref), (att_any, att_ref), (wout_any, wout_ref),
                 (segc_any, segc_ref), (qkv_any, qkv_ref), (wqkv_any, wqkv_ref),
-                (x_any.at[own_rows], x_ref), (dres_any, dres_ref),
+                (x_any, x_ref), (dres_any, dres_ref),
             ]
         )
     ]
@@ -1515,7 +1547,7 @@
     dense = Line(
         mail, depth,
         [(dense_acc.at[c], dense_line.at[c]) for c in range(pairs + 1)] + [(tail_acc, tail_line)],
-        depth - 1,
+        range(depth - 1),
     )
     chunks = pairs + 2
     size = tail_sum.shape[0]
@@ -1527,14 +1559,18 @@
     dn_copies = [mail.copy(dn_send.at[b], dn_recv.at[b], sibling) for b in range(2)]
 
     branch_copy.start()
-    final.start()
-    for copy in loads[3:] + loads[:3]:
+    for copy in loads:
         copy.start()
     fars[0].start()
     fars[1].start()
     go_near(0)
     go_near(1)
 
+    for item in range(3):
+        loads[item].wait()
+        line.send(1, item)
+    for item in range(3):
+        line.send_edge(2, item)
     loads[4].wait()
     normed_turned[...] = normed_ref[...].T
     for k in (3, 5, 6, 7):
@@ -1590,6 +1626,10 @@
                 if now == 0:
                     half_copy.wait_recv()
                     planes[0].start()
+                if now == 1:
+                    for item in range(3):
+                        line.take(1, item)
+                        line.send(2, item)
                 if now >= 1:
                     planes[now - 1].middle()
                 if now >= 2:
@@ -1648,12 +1688,12 @@
             launch(pairs + 1)
         else:
             go_near(2)
-    for item, (own, result) in enumerate(
-        ((gate_own, gate_out), (up_own, up_out), (down_own, down_out))
-    ):
-        loads[item].wait()
-        result[0] = own[...].astype(F32)
-        final.finish(item)
+    for item, (_, _, result) in enumerate(shares):
+
+        def store(value, add=False):
+            result[0] = result[0] + value if add else value
+
+        line.finish(item, store)
     for step in range(depth - 2):
         for c in range(chunks):
             dense.take(step, c)
@@ -1685,7 +1725,7 @@
         copy.wait_send()
     for plane in planes:
         plane.close()
-    final.close()
+    line.close()
     dense.close()
     for copy in fars:
         copy.wait()
@@ -1703,10 +1743,10 @@
 
 def back_all(
     grad_gate, grad_up, grad_down, d_branch, w_out, attended, qkv, seg_col, normed, qkv_weight,
-    x_all, d_residual, block_out, d_prev, lse, seg_row, small, small_all,
+    x_own, d_residual, block_out, d_prev, lse, seg_row, small, small_all,
 ):
     depth = lax.axis_size("dp")
-    length, width = x_all.shape
+    length, width = normed.shape
     mine = length // 2
     span = width // 2
     rows = block_out.shape[1]
@@ -1720,7 +1760,7 @@
     homes = [block_out.shape, block_out.shape, d_prev.shape]
     kinds = [block_out.dtype, BF16, d_prev.dtype]
     steps = 2 * (depth - 1)
-    copies = 6 + 2 + 6 + (groups + 1) * (4 + steps + 1) + 2
+    copies = 6 * (depth - 2) + 2 + 6 + (groups + 1) * (4 + steps + 1) + 2
 
     def plane_buffers(lead, columns):
         return [
@@ -1739,8 +1779,8 @@
         + [shape((size // 2, 6 * span), F32), shape((size // 2, width), F32)]
         + [shape((size // 2, LANES), F32)]
         + [shape(dims, kind) for dims, kind in zip(homes, kinds)],
-        scratch_shapes=[pltpu.VMEM((2,) + part, BF16) for part in parts]
-        + [pltpu.VMEM(part, BF16) for part in parts]
+        scratch_shapes=[pltpu.VMEM((2, depth - 2) + part, BF16) for part in parts]
+        + [pltpu.VMEM((depth,) + part, BF16) for part in parts]
         + [
             pltpu.VMEM((length, width), BF16), pltpu.VMEM((span, width), BF16),
             pltpu.VMEM((length, span), BF16), pltpu.VMEM((length, 3 * span), BF16),
@@ -1767,7 +1807,7 @@
         ),
         name="back_all",
     )(
-        grad_gate, grad_up, grad_down, d_branch, w_out, attended, qkv, seg_col, normed, qkv_weight, x_all, d_residual,
+        grad_gate, grad_up, grad_down, d_branch, w_out, attended, qkv, seg_col, normed, qkv_weight, x_own, d_residual,
         block_out, d_prev, lse, seg_row, small, small_all,
     )
 
@@ -1837,7 +1877,7 @@
     route_count = w_router.shape[1]
     experts = route_count - 4
     (
-        x_all, cot_own, ctl, normed, qkv, attended, lse, small_all, qkv_weight, out_sib,
+        x_own, ctl, normed, qkv, attended, lse, small_all, qkv_weight, out_sib,
         seg_col, seg_row, g_rows,
     ) = gather_all(
         experts, tokens, cotangent, w_qkv, w_out, prev_logits, routes, segments, w_router, const_proj,
@@ -1846,7 +1886,7 @@
     (
         block_out, d_prev, d_residual, d_branch, small, grad_gate, grad_up, grad_down,
     ) = expert_layer(
-        experts, route_count, rows, attended, x_all, cot_own, ctl, w_out, out_sib, small_all,
+        experts, route_count, rows, attended, x_own, cotangent, ctl, w_out, out_sib, small_all,
         w_gate[0], w_up[0], w_down[0], g_rows,
     )
 
@@ -1855,7 +1895,7 @@
         prev_home,
     ) = back_all(
         grad_gate, grad_up, grad_down, d_branch, w_out, attended, qkv, seg_col, normed,
-        qkv_weight, x_all, d_residual, block_out, d_prev, lse, seg_row, small, small_all,
+        qkv_weight, x_own, d_residual, block_out, d_prev, lse, seg_row, small, small_all,
     )
     (
         block_out, grad_tokens, grad_prev, gain_a, grad_qkv, grad_out, gain_m, grad_router,

time: 180 us -> 166 us (0.922)
  Pallas kernels: 179 us -> 165 us
    pallas_call x1, Pallas kernels: 45.4 us -> 34.3 us  [gather_all(): pl.pallas_call(functools.partial(gather_kernel, rows, length // 2, w_rout...]
where the time goes in v5:
time: 166 us
  Pallas kernels  165 us (99%)
    pallas_call x1, Pallas kernels, expert_layer(): pl.pallas_call(functools.partial(layer_kernel, experts, routes, rows, blo...  70.8 us
    pallas_call x1, Pallas kernels, back_all(): pl.pallas_call(functools.partial(back_kernel, depth, rows, length // 2),...  56.3 us
    pallas_call x1, Pallas kernels, gather_all(): pl.pallas_call(functools.partial(gather_kernel, rows, length // 2, w_rout...  34.3 us
    pallas_call x1, Pallas kernels, deliver(): pl.pallas_call(functools.partial(deliver_kernel, routes), in_specs=[vmem]...  3.84 us

profile of v5, /device:TPU:0, one launch (start us, length us, event | category | flops | bytes accessed | tf_op | source)
XLA Modules:
  0.0 166.0 jit_solution(14617239462697945514)
XLA Ops:
  0.6 34.3 %gather_all.1 = (bf16[512,768]{1,0:T(8,128)(2,1)}, f32[2,16,256]{2,1,0:T(8,128)}, bf16[1024,768]{1,0:T(8,128)(2,1)}, bf16[1024,1152]{1,0:T(8,128)(2,1)}, bf16[10...) custom-call(bf16[2,256,768]{2,1,0:T(8,128)(2,1)} %tok_ref.1, ...), custom_call_target="tpu_custom_call" | custom-call | tf_op jit(solution)/shard_map/gather_all/pallas_call | solution.py:777
  34.9 70.8 %expert_layer.1 = (bf16[2,256,768]{2,1,0:T(8,128)(2,1)}, f32[2,8,256]{2,1,0:T(8,128)}, f32[512,768]{1,0:T(8,128)}, bf16[512,768]{1,0:T(8,128)(2,1)}, f32[16,768]...) custom-call(f32[2,16,256]{2,1,0:T(8,128)} %get-tuple-element.55.ctl_ref, ...), custom_call_target="tpu_custom_call" | custom-call | tf_op jit(solution)/shard_map/expert_layer/pallas_call | solution.py:1219
  105.7 56.3 %back_all.1 = (f32[1,96,1024]{2,1,0:T(8,128)}, f32[1,96,1024]{2,1,0:T(8,128)}, f32[1,128,768]{2,1,0:T(8,128)}, f32[24,2304]{1,0:T(8,128)}, f32[24,768]{1,0:T(8,1...) custom-call(bf16[4,96,1024]{2,1,0:T(8,128)(2,1)} %get-tuple-element., ...), custom_call_target="tpu_custom_call" | custom-call | tf_op jit(solution)/shard_map/back_all/pallas_call | solution.py:1774
  162.0 3.8 %deliver.1 = (bf16[2,256,768]{2,1,0:T(8,128)(2,1)}, f32[2,256,768]{2,1,0:T(8,128)}, f32[6,2,256]{2,1,0:T(2,128)}, f32[24]{0:T(128)}, f32[24,2304]{1,0:T(8,128)},...) custom-call(bf16[2,256,768]{2,1,0:T(8,128)(2,1)} %get-tuple-element., ...), custom_call_target="tpu_custom_call" | custom-call | flops 1000000 | bytes 8000000 | tf_op jit(solution)/shard_map/deliver/pallas_call | solution.py:1842

commit v6 on v5

--- a/solution.py
+++ b/solution.py
@@ -997,11 +997,11 @@
     experts, routes, rows, blocks,
     ctl_ref, small_rows, att_ref, cot_ref, x_any, own_any, sib_any, g_any, gate_ref, up_ref,
     down_ref,
-    out_ref, prev_ref, dres_ref, branch_ref, small_ref, gate_acc, up_acc, down_acc,
+    out_end, prev_ref, dres_end, branch_end, small_ref, gate_acc, up_acc, down_acc,
     dgate_out, dup_out, ddown_out, gate_land, up_land, down_land, gate_line, up_line, down_line,
     wide_rows, att_own, att_sib, gate_w, up_w, down_w, residual_ref, mixed_ref, pm_ref, place_ref,
     send_ref, gate_send, gate_recv, recv_ref, result_ref, back_ref, hidden_ref, d_gate_ref,
-    d_up_ref, d_rows_ref, g_ref, x_ref, w_own, w_sib, g_rows,
+    d_up_ref, d_rows_ref, g_ref, x_ref, w_own, w_sib, g_rows, out_ref, dres_ref, branch_ref, end_sems,
     head_send, head_recv, local_sems, send_sems, recv_sems, back_send, back_recv, sum_send, sum_recv,
     g_sends, g_recvs,
 ):
@@ -1102,6 +1102,14 @@
             device_id_type=pl.DeviceIdType.MESH,
         )
 
+    def ends(block):
+        here = pl.ds(pl.multiple_of(block * rows, rows), rows)
+        return [
+            pltpu.make_async_copy(out_ref.at[block], out_end.at[block], end_sems.at[block, 0]),
+            pltpu.make_async_copy(dres_ref.at[here], dres_end.at[here], end_sems.at[block, 1]),
+            pltpu.make_async_copy(branch_ref.at[here], branch_end.at[here], end_sems.at[block, 2]),
+        ]
+
     every = [(k, kind) for kind in range(KINDS) for k in range(3)]
     small_ref[...] = jnp.zeros_like(small_ref)
     wide_rows[...] = jnp.zeros_like(wide_rows)
@@ -1189,9 +1197,14 @@
         for k in range(3):
             giveback(block, k, 1).wait_recv()
         combine_backward(experts, rows, block, refs, keep, back_ref, outs, small_ref)
+        for copy in ends(block):
+            copy.start()
 
     for item in range(3):
         line.take(0, item)
+    for block in range(blocks):
+        for copy in ends(block):
+            copy.wait()
     for copy in heads + halves[0] + halves[1] + halves[2]:
         copy.wait_send()
     line.close()
@@ -1211,6 +1224,7 @@
     span = attended.shape[1]
     hidden = w_gate.shape[1]
     vmem = pl.BlockSpec(memory_space=pltpu.VMEM)
+    anywhere = pl.BlockSpec(memory_space=pl.ANY)
     total = blocks * peers * LANES
     grads = [(2 * w.shape[0], w.shape[1]) for w in (w_gate, w_up, w_down)]
     depth = lax.axis_size("dp")
@@ -1218,8 +1232,8 @@
     sums = 3 * depth + 6
     return pl.pallas_call(
         functools.partial(layer_kernel, experts, routes, rows, blocks),
-        in_specs=[vmem] * 2 + [pl.BlockSpec(memory_space=pl.ANY)] * 9,
-        out_specs=[vmem] * 8,
+        in_specs=[vmem] * 2 + [anywhere] * 9,
+        out_specs=[anywhere, vmem, anywhere, anywhere] + [vmem] * 4,
         out_shape=[
             shape((blocks, rows, width), BF16), shape((blocks, 8, rows), F32),
             shape((mine, width), F32), shape((mine, width), BF16), shape((SMALL, width), F32),
@@ -1243,7 +1257,11 @@
         + [pltpu.VMEM((total, width), BF16), pltpu.VMEM((mine, width), BF16)]
         + [pltpu.VMEM((mine, width), BF16)]
         + [pltpu.VMEM((span, width), BF16)] * 2
-        + [pltpu.VMEM((blocks, peers, LANES, width), BF16)]
+        + [
+            pltpu.VMEM((blocks, peers, LANES, width), BF16),
+            pltpu.VMEM((blocks, rows, width), BF16), pltpu.VMEM((mine, width), F32),
+            pltpu.VMEM((mine, width), BF16), pltpu.SemaphoreType.DMA((blocks, 3)),
+        ]
         + [
             pltpu.SemaphoreType.DMA((4,)), pltpu.SemaphoreType.DMA((4,)),
             pltpu.SemaphoreType.DMA((9,)),

time: 166 us -> 166 us (level)
  no operation moved by 1% of the time
where the time goes in v6:
time: 166 us
  Pallas kernels  165 us (99%)
    pallas_call x1, Pallas kernels, expert_layer(): pl.pallas_call(functools.partial(layer_kernel, experts, routes, rows, blo...  70.8 us
    pallas_call x1, Pallas kernels, back_all(): pl.pallas_call(functools.partial(back_kernel, depth, rows, length // 2),...  56.4 us
    pallas_call x1, Pallas kernels, gather_all(): pl.pallas_call(functools.partial(gather_kernel, rows, length // 2, w_rout...  34.3 us
    pallas_call x1, Pallas kernels, deliver(): pl.pallas_call(functools.partial(deliver_kernel, routes), in_specs=[vmem]...  3.84 us

profile of v6, /device:TPU:0, one launch (start us, length us, event | category | flops | bytes accessed | tf_op | source)
XLA Modules:
  0.0 166.1 jit_solution(2429536047738972761)
XLA Ops:
  0.6 34.3 %gather_all.1 = (bf16[512,768]{1,0:T(8,128)(2,1)}, f32[2,16,256]{2,1,0:T(8,128)}, bf16[1024,768]{1,0:T(8,128)(2,1)}, bf16[1024,1152]{1,0:T(8,128)(2,1)}, bf16[10...) custom-call(bf16[2,256,768]{2,1,0:T(8,128)(2,1)} %tok_ref.1, ...), custom_call_target="tpu_custom_call" | custom-call | tf_op jit(solution)/shard_map/gather_all/pallas_call | solution.py:777
  34.9 70.8 %expert_layer.1 = (bf16[2,256,768]{2,1,0:T(8,128)(2,1)}, f32[2,8,256]{2,1,0:T(8,128)}, f32[512,768]{1,0:T(8,128)}, bf16[512,768]{1,0:T(8,128)(2,1)}, f32[16,768]...) custom-call(f32[2,16,256]{2,1,0:T(8,128)} %get-tuple-element.55.ctl_ref, ...), custom_call_target="tpu_custom_call" | custom-call | tf_op jit(solution)/shard_map/expert_layer/pallas_call | solution.py:1233
  105.7 56.4 %back_all.1 = (f32[1,96,1024]{2,1,0:T(8,128)}, f32[1,96,1024]{2,1,0:T(8,128)}, f32[1,128,768]{2,1,0:T(8,128)}, f32[24,2304]{1,0:T(8,128)}, f32[24,768]{1,0:T(8,1...) custom-call(bf16[4,96,1024]{2,1,0:T(8,128)(2,1)} %get-tuple-element., ...), custom_call_target="tpu_custom_call" | custom-call | tf_op jit(solution)/shard_map/back_all/pallas_call | solution.py:1792
  162.1 3.8 %deliver.1 = (bf16[2,256,768]{2,1,0:T(8,128)(2,1)}, f32[2,256,768]{2,1,0:T(8,128)}, f32[6,2,256]{2,1,0:T(2,128)}, f32[24]{0:T(128)}, f32[24,2304]{1,0:T(8,128)},...) custom-call(bf16[2,256,768]{2,1,0:T(8,128)(2,1)} %get-tuple-element., ...), custom_call_target="tpu_custom_call" | custom-call | flops 1000000 | bytes 8000000 | tf_op jit(solution)/shard_map/deliver/pallas_call | solution.py:1860
